TPU v7x, 32 devices: a whole 2x2x4 slice. The times are simulated.
32 devices in a mesh: dp: 4 (over y, x), item: 8 (over z, core).
Axes of the slice: x: 2, y: 2, z: 4, core: 2. Of those that a mesh axis runs over, the one named last changes fastest.
Arguments:
- queries: bfloat16 [32768, 256], P(('dp', 'item')), may hold values from -0.5 to 0.5
- item_table: float32 [32768, 256], P('item'), may hold values from -0.5 to 0.5
- adagrad_state: float32 [32768], P('item'), may hold values from 1 to 1000
- pos_owner: int32 [32768, 1], P(('dp', 'item')), may hold values from 0 to 7; in each aligned block of 1024 rows (0 to 1023, 1024 to 2047, ...) at most 384 rows name the same one
- pos_row: int32 [32768], P(('dp', 'item')), may hold values from 0 to 4095
- neg_rows: int32 [1536], P(('dp', 'item')), may hold values from 0 to 4095
Outputs:
- query_grad: bfloat16 [32768, 256], P(('dp', 'item'))
- example_loss: float32 [32768], P(('dp', 'item'))
- new_table: float32 [32768, 256], P('item')
- new_state: float32 [32768], P('item')
Inputs may be any that keep to these rules, and one draw needn't show every extreme that they name: `pos_owner`: within the rows of one device (aligned blocks of 1024 examples) no shard is named more than 384 times; some device's block names one shard exactly 384 times.
All inputs are finite; a program needn't handle non-finite values.
Results may differ from a plain program's by a relative error of at most 0.0049.
Values may be sent and summed in bfloat16 or wider, within the bound.
No kernel may reach another device: no remote copies, remote signals or barrier semaphores. Data moves between devices by JAX's collectives and lax.ppermute only.
A program may use at most 64 MiB of HBM per device.

v0:
```python
import math

import jax
import jax.numpy as jnp
from jax import lax
from jax.sharding import PartitionSpec as P

INV_TEMP = 20.0
LEARN_RATE = 0.05
EPSILON = 1e-06


def unit_rows(matrix):
    row_norm = jnp.sqrt(jnp.sum(matrix * matrix, axis=-1, keepdims=True) + EPSILON)
    return (matrix / row_norm, row_norm)


def on_device(queries, item_table, adagrad_state, pos_owner, pos_row, neg_rows):
    ex_count = queries.shape[0]
    rows_dev = item_table.shape[0]
    feat_width = item_table.shape[1]
    neg_dev = neg_rows.shape[0]
    item_count = lax.axis_size("item")
    dp_count = lax.axis_size("dp")
    capacity = 3 * ex_count // item_count
    item_index = lax.axis_index("item")
    query_hat, query_norm = unit_rows(queries.astype(jnp.float32))
    query_send = query_hat.astype(jnp.bfloat16)
    unit_table, table_norm = unit_rows(item_table)
    table_send = unit_table.astype(jnp.bfloat16)
    owners = pos_owner[:, 0]
    onehot = (owners[:, None] == jnp.arange(item_count, dtype=jnp.int32)[None, :]).astype(jnp.int32)
    earlier = jnp.cumsum(onehot, axis=0) - onehot
    slots = jnp.sum(earlier * onehot, axis=1)
    places = owners * capacity + slots
    requests = jnp.zeros((item_count * capacity,), jnp.int32).at[places].set(pos_row)
    requests = requests.reshape(item_count, capacity)
    asked_rows = lax.all_to_all(requests, "item", split_axis=0, concat_axis=0, tiled=True)
    found = table_send[asked_rows]
    returned = lax.all_to_all(found, "item", split_axis=0, concat_axis=0, tiled=True)
    pos_e = returned.reshape(item_count * capacity, feat_width)[places]
    pos_gid = owners * rows_dev + pos_row
    my_gid = item_index * rows_dev + neg_rows
    my_neg = table_send[neg_rows]
    block_rows, block_ids = (
        lax.all_gather(my_neg, "item", axis=0, tiled=True),
        lax.all_gather(my_gid, "item", axis=0, tiled=True),
    )
    all_rows, all_ids = (
        lax.all_gather(block_rows, "dp", axis=0, tiled=True),
        lax.all_gather(block_ids, "dp", axis=0, tiled=True),
    )
    negs = all_rows.shape[0]
    block_size = math.gcd(negs, 1024)
    block_count = negs // block_size
    row_blocks = all_rows.reshape(block_count, block_size, feat_width)
    id_blocks = all_ids.reshape(block_count, block_size)

    def block_scores(row_block, id_block):
        scores = (
            jnp.einsum("ed,nd->en", query_send, row_block, preferred_element_type=jnp.float32)
            * INV_TEMP
        )
        allowed = id_block[None, :] != pos_gid[:, None]
        return (scores, allowed)

    s_pos = INV_TEMP * jnp.sum(query_send.astype(jnp.float32) * pos_e.astype(jnp.float32), axis=1)

    def add_exp(carry, pieces):
        scores, allowed = block_scores(pieces[0], pieces[1])
        return (carry + jnp.sum(jnp.where(allowed, jnp.exp(scores), 0.0), axis=1), None)

    neg_totals, _ = lax.scan(add_exp, jnp.zeros((ex_count,), jnp.float32), (row_blocks, id_blocks))
    lse = jnp.log(jnp.exp(s_pos) + neg_totals)
    example_loss = lse - s_pos

    def both_products(carry, pieces):
        scores, allowed = block_scores(pieces[0], pieces[1])
        probs = jnp.where(allowed, jnp.exp(scores - lse[:, None]), 0.0).astype(jnp.bfloat16)
        carry = carry + jnp.dot(probs, pieces[0], preferred_element_type=jnp.float32)
        partial_rows = INV_TEMP * jnp.einsum(
            "en,ed->nd", probs, query_send, preferred_element_type=jnp.float32
        )
        return (carry, partial_rows)

    neg_part, partial_blocks = lax.scan(
        both_products, jnp.zeros((ex_count, feat_width), jnp.float32), (row_blocks, id_blocks)
    )
    neg_partials = partial_blocks.reshape(negs, feat_width)
    p_pos = jnp.exp(s_pos - lse)
    g_query = INV_TEMP * ((p_pos - 1.0)[:, None] * pos_e.astype(jnp.float32) + neg_part)
    query_grad = (
        (g_query - query_hat * jnp.sum(query_hat * g_query, axis=1, keepdims=True)) / query_norm
    ).astype(jnp.bfloat16)
    g_pos = INV_TEMP * (p_pos - 1.0)[:, None] * query_hat
    outbox = jnp.zeros((item_count * capacity, feat_width), jnp.float32).at[places].set(g_pos)
    outbox = outbox.reshape(item_count, capacity, feat_width)
    inbox = lax.all_to_all(
        outbox.astype(jnp.bfloat16), "item", split_axis=0, concat_axis=0, tiled=True
    ).astype(outbox.dtype)
    dense = jnp.zeros((rows_dev, feat_width), jnp.float32)
    dense = dense.at[asked_rows.reshape(-1)].add(inbox.reshape(-1, feat_width))
    item_partials = (
        neg_partials.reshape(dp_count, item_count, neg_dev, feat_width)
        .transpose(1, 0, 2, 3)
        .reshape(negs, feat_width)
    )
    item_ids = all_ids.reshape(dp_count, item_count, neg_dev).transpose(1, 0, 2).reshape(negs)
    span_rows = dp_count * neg_dev
    neg_grad = lax.psum_scatter(
        item_partials.astype(jnp.bfloat16), "item", scatter_dimension=0, tiled=True
    ).astype(jnp.float32)
    local_rows = (
        lax.dynamic_slice_in_dim(item_ids, item_index * span_rows, span_rows, 0)
        - item_index * rows_dev
    )
    dense = dense.at[local_rows].add(neg_grad)
    g_unit = lax.psum(dense.astype(jnp.bfloat16), "dp").astype(jnp.float32)
    g_row = (g_unit - unit_table * jnp.sum(unit_table * g_unit, axis=1, keepdims=True)) / table_norm
    new_state = adagrad_state + jnp.mean(g_row * g_row, axis=1)
    new_table = item_table - LEARN_RATE * g_row / jnp.sqrt(new_state)[:, None]
    return (query_grad, example_loss, new_table, new_state)


def solution(mesh):
    placed = (
        P(("dp", "item"), None),
        P("item", None),
        P("item"),
        P(("dp", "item"), None),
        P(("dp", "item")),
        P(("dp", "item")),
    )
    return jax.shard_map(
        on_device,
        mesh=mesh,
        in_specs=placed,
        out_specs=(P(("dp", "item"), None), P(("dp", "item")), P("item", None), P("item")),
        check_vma=False,
    )
```

profile of v0, /device:TPU:0, one launch (start us, length us, event | category | flops | bytes accessed | tf_op | source)
XLA Modules:
  0.0 306.7 jit_solution(16396751657277209719)
XLA Ops:
  7.2 0.7 fusion.31
  7.9 2.3 reduce-window.6
  10.6 0.7 fusion.30
  11.3 0.7 compare_select_fusion.2
  12.1 5.0 %scatter_custom_fusion = s32[3072]{0:T(1024)} fusion(s32[1024]{0:T(1024)S(1)} %bitcast.110, s32[1024]{0:T(1024)} %param.14, s32[]{:T(128)} %constant.35.clone.1), kind=kCustom, calls=%fused_computation.69 | custom fusion | bytes 12800 | tf_op jit(solution)/shard_map/scatter | solution.py:36
  17.1 6.4 %all-to-all-start = ((s32[8,1,384]{2,1,0:T(1,128)}), s32[8,1,384]{2,1,0:T(1,128)S(1)}, u32[]{:S(2)}, u32[]{:S(2)}) async-start(s32[8,1,384]{2,1,0:T(1,128)} %bitcast.5), calls=%async_computation | async-start | bytes 24576 | tf_op jit(solution)/shard_map/all_to_all | solution.py:38
  23.5 3.0 multiply_reduce_fusion.1
  26.4 0.5 copy-done
  26.9 0.7 fusion.35
  27.6 1.5 all-to-all-done
  29.1 13.0 %gather_fusion = bf16[3072,256]{1,0:T(8,128)(2,1)} fusion(bf16[4096,256]{1,0:T(8,128)(2,1)S(1)} %fusion.35, s32[3072]{0:T(1024)S(1)} %broadcast_clamp_fusion), kind=kCustom, calls=%fused_computation | custom fusion | bytes 3158016 | tf_op jit(solution)/shard_map/gather | solution.py:39
  42.2 4.4 %all-to-all-start.1 = ((bf16[8,384,256]{2,1,0:T(8,128)(2,1)}), bf16[8,384,256]{2,1,0:T(8,128)(2,1)}, u32[]{:S(2)}, u32[]{:S(2)}) async-start(bf16[8,384,256]{2,1,0:T(8,128)(2,1)} %bitcast.96), calls=%async_computation.1 | async-start | bytes 3145728 | tf_op jit(solution)/shard_map/all_to_all | solution.py:40
  46.7 0.6 dynamic-slice
  48.0 36.5 %all-reduce = s32[384]{0:T(512)S(1)} all-reduce(s32[384]{0:T(512)S(1)} %get-tuple-element.167), channel_id=1, replica_groups=mesh['dp'=4,'item'=8] {'item'}, use_global_device_ids=true, to_apply=%add | all-reduce | flops 384 | bytes 3072
  84.6 8.1 %all-gather.2 = s32[4,1,384]{2,1,0:T(1,128)S(1)} all-gather(s32[1,1,384]{2,1,0:T(1,128)S(1)} %reshape.211), channel_id=1, replica_groups=mesh['dp'=4,'item'=8] {'dp'}, dimensions={0}, use_global_device_ids=true | all-gather | bytes 7680 | tf_op jit(solution)/shard_map/all_gather | solution.py:51
  92.7 0.7 gather_fusion.2
  93.4 14.1 %all-gather = bf16[384,256]{1,0:T(8,128)(2,1)S(1)} all-gather(bf16[48,256]{1,0:T(8,128)(2,1)S(1)} %gather_fusion.2), channel_id=2, replica_groups=mesh['dp'=4,'item'=8] {'item'}, dimensions={0}, use_global_device_ids=true | all-gather | bytes 221184 | tf_op jit(solution)/shard_map/all_gather | solution.py:46
  107.5 1.3 fusion.20
  108.8 12.4 %all-gather.1 = bf16[1536,256]{1,0:T(8,128)(2,1)S(1)} all-gather(bf16[384,256]{1,0:T(8,128)(2,1)S(1)} %all-gather), channel_id=3, replica_groups=mesh['dp'=4,'item'=8] {'dp'}, dimensions={0}, use_global_device_ids=true | all-gather | bytes 983040 | tf_op jit(solution)/shard_map/all_gather | solution.py:50
  121.2 5.1 %gather_fusion.1 = bf16[1024,256]{1,0:T(8,128)(2,1)S(1)} fusion(bf16[3072,256]{1,0:T(8,128)(2,1)} %bitcast.9, s32[1024]{0:T(1024)S(1)} %broadcast_clamp_fusion.1), kind=kCustom, calls=%fused_computation.1 | custom fusion | bytes 1052672 | tf_op jit(solution)/shard_map/gather | solution.py:41
  126.8 2.0 while.24
  126.8 0.6 fusion.56
  127.5 0.6 fusion.56
  128.2 0.6 fusion.56
  128.8 0.6 broadcast_multiply_fusion
  129.4 7.1 %scatter_custom_fusion.1 = f32[3072,256]{1,0:T(8,128)} fusion(s32[1024]{0:T(1024)S(1)} %bitcast.112, f32[]{:T(128)} %constant.11.clone.1, f32[1024]{0:T(1024)S(1)} %get-tuple-element.160, bf16[1024,256]{1,0:T(8,128)(2,1)S(1)} %copy-done.3, f32[1024]{0:T(1024)S(1)} %add_sqrt_fusion.1), kind=kCustom, calls=%fused_computation.38 | custom fusion | flops 786432 | bytes 3678212 | tf_op jit(solution)/shard_map/scatter | solution.py:96
  136.5 3.2 %convert_element_type.65 = bf16[3072,256]{1,0:T(8,128)(2,1)} convert(f32[3072,256]{1,0:T(8,128)} %scatter_custom_fusion.1) | non-fusion elementwise | flops 786432 | bytes 4718592 | tf_op jit(solution)/shard_map/convert_element_type | solution.py:99
  139.7 4.3 %all-to-all-start.2 = ((bf16[8,384,256]{2,1,0:T(8,128)(2,1)}), bf16[8,384,256]{2,1,0:T(8,128)(2,1)}, u32[]{:S(2)}, u32[]{:S(2)}) async-start(bf16[8,384,256]{2,1,0:T(8,128)(2,1)} %bitcast.97), calls=%async_computation.2 | async-start | bytes 3145728 | tf_op jit(solution)/shard_map/all_to_all | solution.py:98
  144.1 7.4 %while.25 = (s32[]{:T(128)}, f32[1024,256]{1,0:T(8,128)S(1)}, bf16[3,512,256]{2,1,0:T(8,128)(2,1)}, s32[3,512]{1,0:T(4,128)S(1)}, s32[1024]{0:T(1024)S(1)}, /*in...) while((s32[]{:T(128)}, f32[1024,256]{1,0:T(8,128)S(1)}, ...), condition=%wide.region_11.12_spmd.clone, body=%wide.region_10.11_spmd.clone.sunk | while | flops 808583168 | bytes 13646015 | solution.py:86
  144.1 0.6 fusion.63
  145.7 0.9 convolution_add_fusion.2
  146.6 0.7 fusion.63
  148.1 0.9 convolution_add_fusion.2
  149.1 0.6 fusion.63
  150.6 0.8 convolution_add_fusion.2
  151.5 2.1 copy.15
  154.1 34.6 %all-to-all-done.2 = bf16[8,384,256]{2,1,0:T(8,128)(2,1)} async-done(((bf16[8,384,256]{2,1,0:T(8,128)(2,1)}), bf16[8,384,256]{2,1,0:T(8,128)(2,1)}, u32[]{:S(2)}, u32[]{:S(2)}) %all-to-all-start.2) | async-done | bytes 1572896 | tf_op jit(solution)/shard_map/all_to_all | solution.py:98
  188.7 23.2 %scatter_custom_fusion.2 = f32[4096,256]{1,0:T(8,128)} fusion(s32[3072]{0:T(1024)S(1)} %bitcast.114, bf16[3072,256]{1,0:T(8,128)(2,1)} %bitcast.27, f32[]{:T(128)} %constant.11.clone.1), kind=kCustom, calls=%fused_computation.34 | custom fusion | flops 1572864 | bytes 5767172 | tf_op jit(solution)/shard_map/scatter-add | solution.py:102
  211.8 6.0 %scatter_custom_fusion.3 = f32[4096,256]{1,0:T(8,128)} fusion(f32[4096,256]{1,0:T(8,128)} %scatter_custom_fusion.2, s32[192]{0:T(256)S(1)} %compare_select_fusion.3, bf16[192,256]{1,0:T(8,128)(2,1)} %reduce-scatter.2.cloned.1.call-done), kind=kCustom, calls=%fused_computation.52 | custom fusion | flops 98304 | bytes 4292608 | tf_op jit(solution)/shard_map/scatter-add | solution.py:117
  217.9 3.7 %convert_element_type.72 = bf16[4096,256]{1,0:T(8,128)(2,1)} convert(f32[4096,256]{1,0:T(8,128)} %scatter_custom_fusion.3) | non-fusion elementwise | flops 1048576 | bytes 6291456 | tf_op jit(solution)/shard_map/convert_element_type | solution.py:118
  221.6 0.5 multiply_reduce_fusion.2
  222.1 1.3 divide_convert_fusion
  223.4 64.6 %all-reduce.3.cloned.1.call-done = bf16[4096,256]{1,0:T(8,128)(2,1)} async-done(((bf16[4096,256]{1,0:T(8,128)(2,1)}), bf16[4096,256]{1,0:T(8,128)(2,1)}) %all-reduce.3.cloned.1.call-update) | async-done | bytes 2097168 | tf_op jit(solution)/shard_map/psum | solution.py:118
  288.0 3.9 %fusion.13 = f32[4096]{0:T(1024)S(1)} fusion(bf16[4096,256]{1,0:T(8,128)(2,1)} %all-reduce.3.cloned.1.call-done, f32[4096,256]{1,0:T(8,128)} %param.11, f32[4096]{0:T(1024)S(1)} %add_sqrt_fusion), kind=kLoop, calls=%fused_computation.29 | loop fusion | flops 4190208 | bytes 6324224 | tf_op jit(solution)/shard_map/reduce_sum | solution.py:119
  292.0 0.7 copy-done.2
  292.7 2.0 multiply_reduce_fusion
  294.7 0.6 fusion.36
  295.3 4.5 %divide_subtract_fusion = f32[4096,256]{1,0:T(8,128)} fusion(f32[4096,256]{1,0:T(8,128)S(1)} %copy-done.1, f32[4096]{0:T(1024)S(1)} %get-tuple-element.158, f32[4096]{0:T(1024)S(1)} %add_sqrt_fusion, f32[4096]{0:T(1024)S(1)} %fusion.13, bf16[4096,256]{1,0:T(8,128)(2,1)S(1)} %copy-done.2), kind=kLoop, calls=%fused_computation.31 | loop fusion | flops 8388608 | bytes 10534912 | tf_op jit(solution)/shard_map/sub | solution.py:121
  (70 shorter events, 4.7 us)
Async XLA Ops:
  17.1 12.0 %all-to-all-start = ((s32[8,1,384]{2,1,0:T(1,128)}), s32[8,1,384]{2,1,0:T(1,128)S(1)}, u32[]{:S(2)}, u32[]{:S(2)}) async-start(s32[8,1,384]{2,1,0:T(1,128)} %bitcast.5), calls=%async_computation | async-start | bytes 24576 | tf_op jit(solution)/shard_map/all_to_all | solution.py:38
  23.5 3.4 %copy-start = (f32[4096,256]{1,0:T(8,128)S(1)}, f32[4096,256]{1,0:T(8,128)}, u32[]{:S(2)}) copy-start(f32[4096,256]{1,0:T(8,128)} %param.11) | copy-start | bytes 12582916
  42.2 4.5 %copy-start.10 = (u32[32]{0:T(128)S(1)}, u32[32]{0:T(128)}, u32[]{:S(2)}) copy-start(u32[32]{0:T(128)} %constant.31) | copy-start | bytes 388
  42.2 5.8 %copy-start.9 = (s32[48]{0:T(128)S(1)}, s32[48]{0:T(128)}, u32[]{:S(2)}) copy-start(s32[48]{0:T(128)} %param.15) | copy-start | bytes 580
  42.2 79.0 %copy-start.6 = (s32[1024,1]{0,1:T(1,128)S(1)}, s32[1024,1]{0,1:T(1,128)}, u32[]{:S(2)}) copy-start(s32[1024,1]{0,1:T(1,128)} %param.13) | copy-start | bytes 12292
  42.2 79.0 %copy-start.8 = (s32[1024]{0:T(1024)S(1)}, s32[1024]{0:T(1024)}, u32[]{:S(2)}) copy-start(s32[1024]{0:T(1024)} %param.14) | copy-start | bytes 12292
  42.2 79.1 %all-to-all-start.1 = ((bf16[8,384,256]{2,1,0:T(8,128)(2,1)}), bf16[8,384,256]{2,1,0:T(8,128)(2,1)}, u32[]{:S(2)}, u32[]{:S(2)}) async-start(bf16[8,384,256]{2,1,0:T(8,128)(2,1)} %bitcast.96), calls=%async_computation.1 | async-start | bytes 3145728 | tf_op jit(solution)/shard_map/all_to_all | solution.py:40
  107.5 18.9 %copy-start.3 = (bf16[1024,256]{1,0:T(8,128)(2,1)S(1)}, bf16[1024,256]{1,0:T(8,128)(2,1)}, u32[]{:S(2)}) copy-start(bf16[1024,256]{1,0:T(8,128)(2,1)} %param.10) | copy-start | bytes 1572868
  139.7 48.9 %all-to-all-start.2 = ((bf16[8,384,256]{2,1,0:T(8,128)(2,1)}), bf16[8,384,256]{2,1,0:T(8,128)(2,1)}, u32[]{:S(2)}, u32[]{:S(2)}) async-start(bf16[8,384,256]{2,1,0:T(8,128)(2,1)} %bitcast.97), calls=%async_computation.2 | async-start | bytes 3145728 | tf_op jit(solution)/shard_map/all_to_all | solution.py:98
  144.0 67.8 %reduce-scatter.2.cloned.1.call-start = ((), (), s32[]{:S(2)}) async-start(), calls=%async_computation.4 | async-start | bytes 884736 | tf_op jit(solution)/shard_map/reduce_scatter | solution.py:110
  144.1 1.1 copy-start.4
  145.7 0.9 copy-start.5
  146.6 1.1 copy-start.4
  148.1 0.9 copy-start.5
  149.0 1.1 copy-start.4
  150.6 0.9 copy-start.5
  153.6 134.4 %all-reduce.3.cloned.1.call-start = ((), (), s32[]{:S(2)}) async-start(), calls=%async_computation.5 | async-start | bytes 4194304 | tf_op jit(solution)/shard_map/psum | solution.py:118
  288.0 4.1 %copy-start.1 = (f32[4096,256]{1,0:T(8,128)S(1)}, f32[4096,256]{1,0:T(8,128)}, u32[]{:S(2)}) copy-start(f32[4096,256]{1,0:T(8,128)} %param.11) | copy-start | bytes 12582916
  288.0 4.7 %copy-start.2 = (bf16[4096,256]{1,0:T(8,128)(2,1)S(1)}, bf16[4096,256]{1,0:T(8,128)(2,1)}, u32[]{:S(2)}) copy-start(bf16[4096,256]{1,0:T(8,128)(2,1)} %all-reduce.3.cloned.1.call-done) | copy-start | bytes 6291460
  292.7 2.0 copy-start.7
Sparse Core Ops, SparseCore 0:
  153.7 36.1 reduce-scatter.1
  221.7 66.2 all-reduce.2
where the time goes:
time: 308 us; the launch traced here: 307 us
  waiting for transfers between devices  101 us (33%)
  blocking collectives  71.1 us (23%)
  other arithmetic  66.9 us (22%)
  local copies, waits for them, and re-layouts  29.8 us (10%)
  starting transfers between devices  15.3 us (5%)
  between operations  15 us (5%)
  matrix products  7.68 us (2%)
    psum x1, waiting for transfers between devices, on_device(): g_unit = lax.psum(dense.astype(jnp.bfloat16), 'dp').astype(jnp.float32)  64.6 us
    unnamed x1, blocking collectives  36.5 us
    all_to_all x1, waiting for transfers between devices, on_device(): lax.all_to_all(outbox.astype(jnp.bfloat16), 'item', split_axis=0, concat_...  34.6 us
    scatter-add x1, other arithmetic, on_device(): dense = dense.at[asked_rows.reshape(-1)].add(inbox.reshape(-1, feat_width))  23.2 us
    all_gather x1, blocking collectives, on_device(): lax.all_gather(my_neg, 'item', axis=0, tiled=True)  14.1 us
    gather x1, local copies, waits for them, and re-layouts, on_device(): found = table_send[asked_rows]  13 us
    all_gather x1, blocking collectives, on_device(): lax.all_gather(block_rows, 'dp', axis=0, tiled=True)  12.4 us
    all_gather x1, blocking collectives, on_device(): lax.all_gather(block_ids, 'dp', axis=0, tiled=True)  8.08 us
  transfers between devices with their start and end apart: 5, of which 3 were waited for; matrix products, arithmetic and copies ran while one was open for 13% of the time, Pallas kernels for 0%

commit v1 on v0

v1 whole, which is shorter than its diff:
```python
import math

import jax
import jax.numpy as jnp
from jax import lax
from jax.experimental import pallas as pl
from jax.experimental.pallas import tpu as pltpu
from jax.sharding import PartitionSpec as P

INV_TEMP = 20.0
LEARN_RATE = 0.05
EPSILON = 1e-06
F32 = jnp.float32
BF16 = jnp.bfloat16
NT = (((1,), (1,)), ((), ()))


def unit_rows(matrix):
    row_norm = jnp.sqrt(jnp.sum(matrix * matrix, axis=-1, keepdims=True) + EPSILON)
    return (matrix / row_norm, row_norm)


def iota(shape, axis):
    return lax.broadcasted_iota(jnp.int32, shape, axis).astype(F32)


def to_sub(row):
    return jnp.transpose(jnp.broadcast_to(row, (128, row.shape[1])))[:, :1]


def to_lane(col):
    return jnp.transpose(jnp.broadcast_to(col, (col.shape[0], 128)))[:1, :]


def one_hot(test):
    return jnp.where(test, 1.0, 0.0).astype(BF16)


def earlier_count(mask):
    total, step = mask, 1
    lane = lax.broadcasted_iota(jnp.int32, mask.shape, 1)
    while step < mask.shape[1]:
        total = total + jnp.where(lane >= step, pltpu.roll(total, step, axis=1), 0.0)
        step *= 2
    return total - mask


def rows_at(start, size):
    return pl.ds(pl.multiple_of(start * size, size), size)


def route_kernel(me_ref, gid_ref, own_ref, table_ref, found_ref, rank_ref, rid_ref, place_ref, send_ref):
    blocks, examples = gid_ref.shape
    table_rows = table_ref.shape[0]
    slots = rid_ref.shape[1]
    chunk = math.gcd(table_rows, 512)
    base = me_ref[0] * table_rows

    def normalize(step, carry):
        part = table_ref[rows_at(step, chunk), :]
        send_ref[rows_at(step, chunk), :] = unit_rows(part)[0].astype(BF16)
        return carry

    lax.fori_loop(0, table_rows // chunk, normalize, 0)
    local = gid_ref[...] - base
    mine = jnp.logical_and(local >= 0, local < table_rows)
    rank = earlier_count(jnp.where(mine, 1.0, 0.0))
    rank_ref[...] = jnp.where(mine, rank, -1.0)
    local = local.astype(F32)

    owner = lax.broadcasted_iota(jnp.int32, (blocks, examples), 0)
    own = own_ref[...]
    named = jnp.logical_and(own >= owner * table_rows, own < (owner + 1) * table_rows)
    count = earlier_count(jnp.where(named, 1.0, 0.0))
    spot = jnp.where(named, count + owner.astype(F32) * slots, 0.0)
    place_ref[...] = jnp.sum(spot, axis=0, keepdims=True)

    for block in range(blocks):
        chosen = iota((slots, examples), 0) == rank_ref[block : block + 1, :]
        wanted = jnp.sum(
            jnp.where(chosen, local[block : block + 1, :], 0.0), axis=1, keepdims=True
        )
        rid_ref[block : block + 1, :] = to_lane(wanted)

    def find(block, carry):
        wanted = to_sub(rid_ref[pl.ds(block, 1), :])

        def gather(step, total):
            pick = one_hot(wanted - (step * chunk).astype(F32) == iota((slots, chunk), 1))
            return total + jnp.dot(
                pick, send_ref[rows_at(step, chunk), :], preferred_element_type=F32
            )

        total = lax.fori_loop(
            0, table_rows // chunk, gather, jnp.zeros((slots, table_ref.shape[1]), F32)
        )
        found_ref[rows_at(block, slots), :] = total.astype(BF16)
        return carry

    lax.fori_loop(0, blocks, find, 0)


def owner_kernel(count, first, me_ref, *refs):
    queries, refs = refs[:count], refs[count:]
    rank_ref, rid_ref, found_ref, negs_ref, nid_ref, refs = *refs[:5], refs[5:]
    prior_ref = None
    if not first:
        prior_ref, refs = refs[0], refs[1:]
    pull_ref, outrid_ref, neg_ref, held, nsub, exps, copy_sem = refs
    slots = rid_ref.shape[1]
    examples = held.shape[1]
    negs = negs_ref.shape[0]
    chunk = math.gcd(negs, 256)
    copies = [
        pltpu.make_async_copy(query, held.at[spot], copy_sem.at[spot])
        for spot, query in enumerate(queries)
    ]
    for copy in copies:
        copy.start()
    for step in range(negs // chunk):
        part = nid_ref[:, step * chunk : (step + 1) * chunk]
        nsub[step * chunk : (step + 1) * chunk, :] = jnp.broadcast_to(to_sub(part), (chunk, 128))
    if first:
        neg_ref[...] = jnp.zeros_like(neg_ref)
    else:
        neg_ref[...] = prior_ref[...]
    for copy in copies:
        copy.wait()

    def block_step(spot, carry):
        source = me_ref[1 + spot]
        rank = rank_ref[pl.ds(source, 1), :]
        rid = rid_ref[pl.ds(source, 1), :]
        outrid_ref[pl.ds(spot, 1), :] = rid
        pick = one_hot(iota((slots, examples), 0) == rank)
        query_hat, _ = unit_rows(jnp.dot(pick, held[spot], preferred_element_type=F32))
        query_send = query_hat.astype(BF16)
        pos_e = found_ref[rows_at(source, slots), :].astype(F32)
        s_pos = INV_TEMP * jnp.sum(query_send.astype(F32) * pos_e, axis=1, keepdims=True)
        pos_exp = to_lane(jnp.exp(s_pos))

        def add_exp(step, total):
            scores = INV_TEMP * lax.dot_general(
                negs_ref[rows_at(step, chunk), :], query_send, NT, preferred_element_type=F32
            )
            keep = nsub[rows_at(step, chunk), :][:, :1] != rid
            part = jnp.where(keep, jnp.exp(scores), 0.0)
            exps[rows_at(step, chunk), :] = part
            return total + jnp.sum(part, axis=0, keepdims=True)

        total = lax.fori_loop(0, negs // chunk, add_exp, pos_exp)
        scale = 1.0 / total

        def add_grad(step, inner):
            probs = (exps[rows_at(step, chunk), :] * scale).astype(BF16)
            neg_ref[rows_at(step, chunk), :] += jnp.dot(
                probs, query_send, preferred_element_type=F32
            )
            return inner

        lax.fori_loop(0, negs // chunk, add_grad, 0)
        p_pos = to_sub(pos_exp * scale)
        pull_ref[rows_at(spot, slots), :] = (INV_TEMP * (p_pos - 1.0) * query_hat).astype(BF16)
        return carry

    lax.fori_loop(0, count, block_step, 0)


def scatter_kernel(pieces, *refs):
    pulls, rids, dense_ref = refs[:pieces], refs[pieces : 2 * pieces], refs[2 * pieces]
    rows = dense_ref.shape[0]
    offset = (pl.program_id(0) * rows).astype(F32)
    total = jnp.zeros(dense_ref.shape, F32)
    for pull_ref, rid_ref in zip(pulls, rids):
        count, slots = rid_ref.shape
        ids = jnp.concatenate([rid_ref[spot : spot + 1, :] for spot in range(count)], axis=1)
        put = one_hot(iota((rows, count * slots), 0) == ids - offset)
        total = total + jnp.dot(put, pull_ref[...], preferred_element_type=F32)
    dense_ref[...] = total.astype(BF16)


def home_kernel(query_ref, place_ref, gid_ref, back_ref, negs_ref, nid_ref, grad_ref, loss_ref):
    examples = query_ref.shape[0]
    spots = back_ref.shape[0]
    pick = one_hot(iota((examples, spots), 1) == to_sub(place_ref[...]))
    pos_e = jnp.dot(pick, back_ref[...], preferred_element_type=F32)
    query_hat, query_norm = unit_rows(query_ref[...].astype(F32))
    query_send = query_hat.astype(BF16)
    s_pos = INV_TEMP * jnp.sum(query_send.astype(F32) * pos_e, axis=1, keepdims=True)
    pos_exp = jnp.exp(s_pos)
    scores = INV_TEMP * lax.dot_general(
        query_send, negs_ref[...], NT, preferred_element_type=F32
    )
    keep = nid_ref[...] != to_sub(gid_ref[...])
    part = jnp.where(keep, jnp.exp(scores), 0.0)
    total = pos_exp + jnp.sum(part, axis=1, keepdims=True)
    scale = 1.0 / total
    loss_ref[...] = to_lane(jnp.log(total) - s_pos)
    probs = (part * scale).astype(BF16)
    g_query = INV_TEMP * (
        (pos_exp * scale - 1.0) * pos_e
        + jnp.dot(probs, negs_ref[...], preferred_element_type=F32)
    )
    along = jnp.sum(query_hat * g_query, axis=1, keepdims=True)
    grad_ref[...] = ((g_query - query_hat * along) / query_norm).astype(BF16)


def update_kernel(table_ref, state_ref, pull_ref, neg_ref, row_ref, new_ref, new_state_ref):
    rows = table_ref.shape[0]
    offset = (pl.program_id(0) * rows).astype(F32)
    put = one_hot(iota((rows, row_ref.shape[1]), 0) == row_ref[...] - offset)
    g_unit = pull_ref[...].astype(F32) + jnp.dot(put, neg_ref[...], preferred_element_type=F32)
    table = table_ref[...]
    unit, norm = unit_rows(table)
    g_row = (g_unit - unit * jnp.sum(unit * g_unit, axis=1, keepdims=True)) / norm
    state = to_sub(state_ref[...]) + jnp.mean(g_row * g_row, axis=1, keepdims=True)
    new_state_ref[...] = to_lane(state)
    new_ref[...] = table - LEARN_RATE * g_row / jnp.sqrt(state)


def whole(ndim=2):
    return pl.BlockSpec(memory_space=pltpu.VMEM)


def flip(name, count, bit):
    return [(index, index ^ (1 << bit)) for index in range(count)]


def halve(value, name, count, bit):
    half = value.shape[0] // 2
    mine = (lax.axis_index(name) >> bit) & 1
    give = lax.dynamic_slice_in_dim(value, (1 - mine) * half, half, 0)
    keep = lax.dynamic_slice_in_dim(value, mine * half, half, 0)
    got = lax.ppermute(give, name, flip(name, count, bit))
    return (keep.astype(F32) + got.astype(F32)).astype(BF16)


def double(value, name, count, bit):
    mine = (lax.axis_index(name) >> bit) & 1
    got = lax.ppermute(value, name, flip(name, count, bit))
    low = jnp.concatenate([value, got], axis=0)
    high = jnp.concatenate([got, value], axis=0)
    return jnp.where(mine == 0, low, high)


def to_all(value, name, count):
    copies = jnp.broadcast_to(value[None], (count, *value.shape))
    return lax.all_to_all(copies, name, split_axis=0, concat_axis=0, tiled=True)


def on_device(queries, item_table, adagrad_state, pos_owner, pos_row, neg_rows):
    examples, width = queries.shape
    table_rows = item_table.shape[0]
    neg_dev = neg_rows.shape[0]
    items = lax.axis_size("item")
    groups = lax.axis_size("dp")
    bits = groups.bit_length() - 1
    assert groups == 1 << bits and items % 2 == 0
    capacity = 3 * examples // items
    slots = -(-capacity // 128) * 128
    negs = groups * items * neg_dev
    item = lax.axis_index("item")

    own_gid = pos_owner[:, 0] * table_rows + pos_row
    my_ids = item * table_rows + neg_rows
    id_pad = -(-neg_dev // 128) * 128
    ints = jnp.concatenate([own_gid, jnp.pad(my_ids, (0, id_pad - neg_dev))])
    all_ints = to_all(ints, "item", items)
    gids = all_ints[:, :examples]
    column_ids = all_ints[:, examples : examples + neg_dev].reshape(items * neg_dev)
    my_negs = unit_rows(item_table[neg_rows])[0].astype(BF16)
    column_negs = to_all(my_negs, "item", items).reshape(items * neg_dev, width)
    all_ids = to_all(column_ids, "dp", groups).reshape(negs)
    all_negs = to_all(column_negs, "dp", groups).reshape(negs, width)

    ring = [(index, (index + 2) % items) for index in range(items)]
    pair = flip("item", items, 0)
    steps, block = [], queries
    for step in range(items // 2):
        if step:
            block = lax.ppermute(block, "item", ring)
        other = lax.ppermute(block, "item", pair)
        steps.append((block, other, (item - 2 * step) % items, ((item ^ 1) - 2 * step) % items))

    found, rank, rid, place = pl.pallas_call(
        route_kernel,
        out_shape=(
            jax.ShapeDtypeStruct((items * slots, width), BF16),
            jax.ShapeDtypeStruct((items, examples), F32),
            jax.ShapeDtypeStruct((items, slots), F32),
            jax.ShapeDtypeStruct((1, examples), F32),
        ),
        in_specs=[pl.BlockSpec(memory_space=pltpu.SMEM), whole(), whole(), whole()],
        out_specs=(whole(), whole(), whole(), whole()),
        scratch_shapes=[pltpu.VMEM((table_rows, width), BF16)],
        name="route",
    )(item[None], gids, own_gid[None, :], item_table)
    back = lax.all_to_all(
        found.reshape(items, slots, width), "item", split_axis=0, concat_axis=0, tiled=True
    ).reshape(items * slots, width)

    local_ids = (all_ids - item * table_rows).astype(F32)[None, :]
    blocks = [block for step in steps for block in step[:2]]
    sources = [source for step in steps for source in step[2:]]
    count = len(blocks)
    pull, out_rid, neg_part = pl.pallas_call(
        lambda *refs: owner_kernel(count, True, *refs),
        out_shape=(
            jax.ShapeDtypeStruct((count * slots, width), BF16),
            jax.ShapeDtypeStruct((count, slots), F32),
            jax.ShapeDtypeStruct((negs, width), F32),
        ),
        in_specs=[pl.BlockSpec(memory_space=pltpu.SMEM)]
        + [pl.BlockSpec(memory_space=pl.ANY)] * count
        + [whole()] * 5,
        out_specs=(whole(), whole(), whole()),
        scratch_shapes=[
            pltpu.VMEM((count, examples, width), BF16),
            pltpu.VMEM((negs, 128), F32),
            pltpu.VMEM((negs, slots), F32),
            pltpu.SemaphoreType.DMA((count,)),
        ],
        name="owner",
    )(jnp.stack([item] + sources), *blocks, rank, rid, found, all_negs, local_ids)

    parts = (INV_TEMP * neg_part).astype(BF16).reshape(groups, items, neg_dev, width)
    parts = parts.transpose(1, 0, 2, 3).reshape(items, groups * neg_dev, width)
    parts = lax.all_to_all(parts, "item", split_axis=0, concat_axis=0, tiled=True)
    neg_sum = jnp.sum(parts.astype(F32), axis=0).astype(BF16)
    for bit in range(bits):
        got = lax.ppermute(neg_sum, "dp", flip("dp", groups, bit))
        neg_sum = (neg_sum.astype(F32) + got.astype(F32)).astype(BF16)
    neg_spots = lax.dynamic_slice_in_dim(
        local_ids.reshape(groups, items, neg_dev), item, 1, 1
    ).reshape(1, groups * neg_dev)

    chunk = math.gcd(table_rows, 512)
    dense = pl.pallas_call(
        lambda *refs: scatter_kernel(1, *refs),
        out_shape=jax.ShapeDtypeStruct((table_rows, width), BF16),
        grid=(table_rows // chunk,),
        in_specs=[whole()] * 2,
        out_specs=pl.BlockSpec((chunk, width), lambda step: (step, 0)),
        name="scatter",
    )(pull, out_rid)
    half = table_rows // 2
    summed = []
    for side in range(2):
        order = list(range(bits)) if side == 0 else list(range(bits))[::-1]
        value = dense[side * half : (side + 1) * half]
        for bit in order:
            value = halve(value, "dp", groups, bit)
        for bit in order[::-1]:
            value = double(value, "dp", groups, bit)
        summed.append(value)
    g_unit = jnp.concatenate(summed, axis=0)

    new_table, new_state = pl.pallas_call(
        update_kernel,
        out_shape=(
            jax.ShapeDtypeStruct((table_rows, width), F32),
            jax.ShapeDtypeStruct((1, table_rows), F32),
        ),
        grid=(table_rows // chunk,),
        in_specs=[
            pl.BlockSpec((chunk, width), lambda step: (step, 0)),
            pl.BlockSpec((1, chunk), lambda step: (0, step)),
            pl.BlockSpec((chunk, width), lambda step: (step, 0)),
            whole(),
            whole(),
        ],
        out_specs=(
            pl.BlockSpec((chunk, width), lambda step: (step, 0)),
            pl.BlockSpec((1, chunk), lambda step: (0, step)),
        ),
        name="update",
    )(item_table, adagrad_state[None, :], g_unit, neg_sum, neg_spots)

    part = math.gcd(examples, 256)
    query_grad, example_loss = pl.pallas_call(
        home_kernel,
        out_shape=(
            jax.ShapeDtypeStruct((examples, width), BF16),
            jax.ShapeDtypeStruct((1, examples), F32),
        ),
        grid=(examples // part,),
        in_specs=[
            pl.BlockSpec((part, width), lambda step: (step, 0)),
            pl.BlockSpec((1, part), lambda step: (0, step)),
            pl.BlockSpec((1, part), lambda step: (0, step)),
            whole(),
            whole(),
            whole(),
        ],
        out_specs=(
            pl.BlockSpec((part, width), lambda step: (step, 0)),
            pl.BlockSpec((1, part), lambda step: (0, step)),
        ),
        name="home",
    )(queries, place, own_gid.astype(F32)[None, :], back, all_negs, all_ids.astype(F32)[None, :])
    return (query_grad, example_loss.reshape(examples), new_table, new_state.reshape(table_rows))


def solution(mesh):
    placed = (
        P(("dp", "item"), None),
        P("item", None),
        P("item"),
        P(("dp", "item"), None),
        P(("dp", "item")),
        P(("dp", "item")),
    )
    return jax.shard_map(
        on_device,
        mesh=mesh,
        in_specs=placed,
        out_specs=(P(("dp", "item"), None), P(("dp", "item")), P("item", None), P("item")),
        check_vma=False,
    )
```

time: 308 us -> 231 us (0.75)
  Pallas kernels: 0 us -> 96.8 us
  blocking collectives: 71.1 us -> 14.8 us
  other arithmetic: 66.9 us -> 11.2 us
  waiting for transfers between devices: 101 us -> 54 us
  starting transfers between devices: 15.3 us -> 39.2 us
  local copies, waits for them, and re-layouts: 29.8 us -> 12.8 us
  between operations: 15 us -> 0.87 us
  matrix products: 7.68 us -> 0 us
    pallas_call x0 -> x5, Pallas kernels: none -> 96.8 us  [the longest x1 36.7 us: on_device(): pl.pallas_call(lambda *refs: owner_kernel(count, True, *refs), out_shape=...]
    psum x1 -> x0, waiting for transfers between devices: 64.6 us -> none  [on_device(): g_unit = lax.psum(dense.astype(jnp.bfloat16), 'dp').astype(jnp.float32)]
    unnamed x1 -> x0, blocking collectives: 36.5 us -> none
    all_gather x3 -> x0, blocking collectives: 34.6 us -> none  [the longest x1 14.1 us: on_device(): lax.all_gather(my_neg, 'item', axis=0, tiled=True)]
    ppermute x0 -> x17, waiting for transfers between devices: none -> 32.1 us  [the longest x4 14.8 us: halve(): got = lax.ppermute(give, name, flip(name, count, bit))]
    scatter-add x2 -> x0, other arithmetic: 29.2 us -> none  [the longest x1 23.2 us: on_device(): dense = dense.at[asked_rows.reshape(-1)].add(inbox.reshape(-1, feat_width))]
    ppermute x0 -> x17, starting transfers between devices: none -> 18.8 us  [the longest x4 6.82 us: halve(): got = lax.ppermute(give, name, flip(name, count, bit))]
    gather x3 -> x1, local copies, waits for them, and re-layouts: 18.8 us -> 2.82 us  [on_device(): my_negs = unit_rows(item_table[neg_rows])[0].astype(BF16)]
  transfers between devices with their start and end apart: 5 -> 22, of which waited for: 3 -> 8; matrix products, arithmetic and copies ran while one was open for 13% -> 8% of each run, Pallas kernels for 0% -> 21%
where the time goes in v1:
time: 231 us; the launch traced here: 230 us
  Pallas kernels  96.8 us (42%)
  waiting for transfers between devices  54 us (23%)
  starting transfers between devices  39.2 us (17%)
  blocking collectives  14.8 us (6%)
  local copies, waits for them, and re-layouts  12.8 us (6%)
  other arithmetic  11.2 us (5%)
    pallas_call x1, Pallas kernels, on_device(): pl.pallas_call(lambda *refs: owner_kernel(count, True, *refs), out_shape=...  36.7 us
    pallas_call x1, Pallas kernels, on_device(): pl.pallas_call(route_kernel, out_shape=(jax.ShapeDtypeStruct((items * slo...  28.8 us
    all_to_all x1, blocking collectives, to_all(): return lax.all_to_all(copies, name, split_axis=0, concat_axis=0, tiled=True)  14.8 us
    ppermute x4, waiting for transfers between devices, halve(): got = lax.ppermute(give, name, flip(name, count, bit))  14.8 us
    all_to_all x3, starting transfers between devices, to_all(): return lax.all_to_all(copies, name, split_axis=0, concat_axis=0, tiled=True)  12.4 us
    ppermute x3, waiting for transfers between devices, on_device(): block = lax.ppermute(block, 'item', ring)  11.5 us
    all_to_all x3, waiting for transfers between devices, to_all(): return lax.all_to_all(copies, name, split_axis=0, concat_axis=0, tiled=True)  11.1 us
    pallas_call x1, Pallas kernels, on_device(): pl.pallas_call(update_kernel, out_shape=(jax.ShapeDtypeStruct((table_rows...  10.9 us
  transfers between devices with their start and end apart: 22, of which 8 were waited for; matrix products, arithmetic and copies ran while one was open for 8% of the time, Pallas kernels for 21%

profile of v1, /device:TPU:0, one launch (start us, length us, event | category | flops | bytes accessed | tf_op | source)
XLA Modules:
  0.0 229.7 jit_solution(8903011570987362214)
XLA Ops:
  0.6 3.1 %collective-permute-start.1 = (bf16[1024,256]{1,0:T(8,128)(2,1)}, bf16[1024,256]{1,0:T(8,128)(2,1)S(1)}, u32[]{:S(2)}, u32[]{:S(2)}) collective-permute-start(bf16[1024,256]{1,0:T(8,128)(2,1)} %refs_1_.1), channel_id=1, source_target_pairs={{0,2},{1,3},{2,4},{3,5},{4,6},{5,7},{6,0},{7,1},{8,10},{9,11},{10,... | collective-permute-start | bytes 1572872 | tf_op jit(solution)/shard_map/ppermute | solution.py:281
  3.7 0.7 compare_select_fusion
  4.4 0.7 broadcast_multiply_fusion
  5.1 1.3 fusion.2
  6.4 11.5 %collective-permute-done.1.refs_3_ = bf16[1024,256]{1,0:T(8,128)(2,1)S(1)} collective-permute-done((bf16[1024,256]{1,0:T(8,128)(2,1)}, bf16[1024,256]{1,0:T(8,128)(2,1)S(1)}, u32[]{:S(2)}, u32[]{:S(2)}) %collective-permute-start.1) | collective-permute-done | bytes 524320 | tf_op jit(solution)/shard_map/ppermute | solution.py:281
  17.9 0.7 broadcast_in_dim.45
  18.6 5.0 %all-to-all-start = ((s32[8,1,1152]{2,1,0:T(1,128)}), s32[8,1,1152]{2,1,0:T(1,128)S(1)}, u32[]{:S(2)}, u32[]{:S(2)}) async-start(s32[8,1,1152]{2,1,0:T(1,128)} %broadcast_in_dim.45), calls=%async_computation | async-start | bytes 73728 | tf_op jit(solution)/shard_map/all_to_all | solution.py:248
  23.7 2.8 %gather_fusion = f32[48,256]{1,0:T(8,128)S(1)} fusion(f32[4096,256]{1,0:T(8,128)} %table_ref.3, s32[1024]{0:T(1024)S(1)} %pad_clamp_fusion), kind=kCustom, calls=%fused_computation | custom fusion | bytes 98496 | tf_op jit(solution)/shard_map/gather | solution.py:271
  26.6 7.0 %all-to-all-done = s32[8,1,1152]{2,1,0:T(1,128)S(1)} async-done(((s32[8,1,1152]{2,1,0:T(1,128)}), s32[8,1,1152]{2,1,0:T(1,128)S(1)}, u32[]{:S(2)}, u32[]{:S(2)}) %all-to-all-start) | async-done | bytes 36896 | tf_op jit(solution)/shard_map/all_to_all | solution.py:248
  34.3 3.5 %all-to-all-start.4 = ((s32[4,1,384]{2,1,0:T(1,128)}), s32[4,1,384]{2,1,0:T(1,128)S(1)}, u32[]{:S(2)}, u32[]{:S(2)}) async-start(s32[4,1,384]{2,1,0:T(1,128)} %broadcast_in_dim.53), calls=%async_computation.4 | async-start | bytes 12288 | tf_op jit(solution)/shard_map/all_to_all | solution.py:248
  38.4 4.1 %all-to-all-done.4 = s32[4,1,384]{2,1,0:T(1,128)S(1)} async-done(((s32[4,1,384]{2,1,0:T(1,128)}), s32[4,1,384]{2,1,0:T(1,128)S(1)}, u32[]{:S(2)}, u32[]{:S(2)}) %all-to-all-start.4) | async-done | bytes 6176 | tf_op jit(solution)/shard_map/all_to_all | solution.py:248
  42.5 14.8 %all_to_all.35 = bf16[8,48,256]{2,1,0:T(8,128)(2,1)S(1)} all-to-all(bf16[8,48,256]{2,1,0:T(8,128)(2,1)S(1)} %broadcast_in_dim.49), channel_id=1, replica_groups=mesh['dp'=4,'item'=8] {'item'}, dimensions={0} | all-to-all | bytes 393216 | tf_op jit(solution)/shard_map/all_to_all | solution.py:248
  57.3 0.9 broadcast_in_dim.51
  58.3 3.8 %all-to-all-start.3 = ((bf16[4,384,256]{2,1,0:T(8,128)(2,1)}), bf16[4,384,256]{2,1,0:T(8,128)(2,1)S(1)}, u32[]{:S(2)}, u32[]{:S(2)}) async-start(bf16[4,384,256]{2,1,0:T(8,128)(2,1)} %broadcast_in_dim.51), calls=%async_computation.3 | async-start | bytes 1572864 | tf_op jit(solution)/shard_map/all_to_all | solution.py:248
  63.1 0.6 stack.36.refs_0_
  64.4 28.8 %route.1 = (bf16[3072,256]{1,0:T(8,128)(2,1)}, f32[8,1024]{1,0:T(8,128)}, f32[8,384]{1,0:T(8,128)}, f32[1,1024]{1,0:T(1,128)}) custom-call(s32[1]{0:T(128)} %bitcast.me_ref, s32[8,1024]{1,0:T(8,128)} %slice.18.gid_ref, s32[1,1024]{1,0:T(1,128)} %bitcast.35, f32[4096,256]{1,0:T(8,128)} %table_ref.3), custom_call_target="tpu_custom_call" | custom-call | tf_op jit(solution)/shard_map/route/pallas_call | solution.py:285
  93.8 0.7 copy-done.9
  94.8 36.7 %owner.1 = (bf16[3072,256]{1,0:T(8,128)(2,1)}, f32[8,384]{1,0:T(8,128)}, f32[1536,256]{1,0:T(8,128)}) custom-call(s32[9]{0:T(128)} %stack.36.refs_0_, bf16[1024,256]{1,0:T(8,128)(2,1)} %refs_1_.1, bf16[1024,256]{1,0:T(8,128)(2,1)} %copy-done.9, bf16[1024,256]{1,0:T(8,128)(2,1)} %copy-done.6, bf16[1024,256]{1,0:T(8,128)(2,1)} %collective-permute-done.2.refs_4_, ...), custom_call_target="tpu_custom_call" | custom-call | tf_op jit(solution)/shard_map/owner/pallas_call | solution.py:306
  131.5 1.5 multiply_convert_fusion
  133.1 1.0 copy.11
  134.1 3.5 %all-to-all-start.5 = ((bf16[8,192,256]{2,1,0:T(8,128)(2,1)}), bf16[8,192,256]{2,1,0:T(8,128)(2,1)S(1)}, u32[]{:S(2)}, u32[]{:S(2)}) async-start(bf16[8,192,256]{2,1,0:T(8,128)(2,1)} %bitcast.22), calls=%async_computation.5 | async-start | bytes 1572864 | tf_op jit(solution)/shard_map/all_to_all | solution.py:328
  137.6 10.1 %scatter.1 = bf16[4096,256]{1,0:T(8,128)(2,1)} custom-call(bf16[3072,256]{1,0:T(8,128)(2,1)} %get-tuple-element.21.refs_0_, f32[8,384]{1,0:T(8,128)} %get-tuple-element.22.refs_1_), custom_call_target="tpu_custom_call" | custom-call | tf_op jit(solution)/shard_map/scatter/pallas_call | solution.py:338
  147.7 10.8 %all-to-all-done.5 = bf16[8,192,256]{2,1,0:T(8,128)(2,1)S(1)} async-done(((bf16[8,192,256]{2,1,0:T(8,128)(2,1)}), bf16[8,192,256]{2,1,0:T(8,128)(2,1)S(1)}, u32[]{:S(2)}, u32[]{:S(2)}) %all-to-all-start.5) | async-done | bytes 786464 | tf_op jit(solution)/shard_map/all_to_all | solution.py:328
  158.5 0.9 copy-done.3
  159.4 4.5 %all-to-all-start.1 = ((bf16[8,384,256]{2,1,0:T(8,128)(2,1)}), bf16[8,384,256]{2,1,0:T(8,128)(2,1)}, u32[]{:S(2)}, u32[]{:S(2)}) async-start(bf16[8,384,256]{2,1,0:T(8,128)(2,1)} %bitcast.30), calls=%async_computation.1 | async-start | bytes 3145728 | tf_op jit(solution)/shard_map/all_to_all | solution.py:298
  164.0 1.0 copy-done.2
  165.0 2.1 collective-permute-start.11
  167.1 0.8 constant_dynamic-slice_fusion.4
  168.0 1.5 collective-permute-start.7
  169.4 10.0 %collective-permute-done.11 = bf16[1024,256]{1,0:T(8,128)(2,1)S(1)} collective-permute-done((bf16[1024,256]{1,0:T(8,128)(2,1)S(1)}, bf16[1024,256]{1,0:T(8,128)(2,1)S(1)}, u32[]{:S(2)}, u32[]{:S(2)}) %collective-permute-start.11) | collective-permute-done | bytes 524320 | tf_op jit(solution)/shard_map/ppermute | solution.py:234
  179.4 1.2 add_convert_fusion
  180.6 0.7 constant_dynamic-slice_fusion.1
  181.3 1.7 collective-permute-start.12
  183.2 1.5 collective-permute-start.8
  184.8 4.8 %collective-permute-done.12 = bf16[512,256]{1,0:T(8,128)(2,1)} collective-permute-done((bf16[512,256]{1,0:T(8,128)(2,1)}, bf16[512,256]{1,0:T(8,128)(2,1)}, u32[]{:S(2)}, u32[]{:S(2)}) %collective-permute-start.12) | collective-permute-done | bytes 262176 | tf_op jit(solution)/shard_map/ppermute | solution.py:234
  189.6 1.0 add_convert_fusion.2
  190.6 1.5 collective-permute-start.13
  192.2 1.5 collective-permute-start.9
  193.7 4.0 %collective-permute-done.13 = bf16[512,256]{1,0:T(8,128)(2,1)S(1)} collective-permute-done((bf16[512,256]{1,0:T(8,128)(2,1)S(1)}, bf16[512,256]{1,0:T(8,128)(2,1)S(1)}, u32[]{:S(2)}, u32[]{:S(2)}) %collective-permute-start.13) | collective-permute-done | bytes 262176 | tf_op jit(solution)/shard_map/ppermute | solution.py:240
  197.9 1.2 collective-permute-start.14
  199.3 1.5 collective-permute-start.15
  201.8 0.6 reshape.112.row_ref
  203.0 10.4 %home.1 = (bf16[1024,256]{1,0:T(8,128)(2,1)}, f32[1,1024]{1,0:T(1,128)}) custom-call(bf16[1024,256]{1,0:T(8,128)(2,1)} %refs_1_.1, f32[1,1024]{1,0:T(1,128)} %get-tuple-element.15.place_ref, f32[1,1024]{1,0:T(1,128)} %bitcast.39, bf16[3072,256]{1,0:T(8,128)(2,1)} %bitcast.5.back_ref, bf16[1536,256]{1,0:T(8,128)(2,1)} %bitcast.29, f32[1,1536]{1,0:T(1,128)} %bitcast.36), custom_call_target="tpu_custom_call" | custom-call | tf_op jit(solution)/shard_map/home/pallas_call | solution.py:380
  213.4 0.9 collective-permute-start.16
  214.9 1.5 pad_maximum_fusion.pull_ref
  216.3 1.8 collective-permute-done.16
  218.1 0.7 add_convert_fusion.4.neg_ref
  218.8 10.9 %update.1 = (f32[4096,256]{1,0:T(8,128)}, f32[1,4096]{1,0:T(1,128)}) custom-call(f32[4096,256]{1,0:T(8,128)} %table_ref.3, f32[1,4096]{1,0:T(1,128)} %bitcast.38, bf16[4096,256]{1,0:T(8,128)(2,1)} %pad_maximum_fusion.pull_ref, bf16[192,256]{1,0:T(8,128)(2,1)} %add_convert_fusion.4.neg_ref, f32[1,192]{1,0:T(1,128)} %reshape.112.row_ref), custom_call_target="tpu_custom_call" | custom-call | tf_op jit(solution)/shard_map/update/pallas_call | solution.py:358
  (66 shorter events, 6.8 us)
Async XLA Ops:
  0.6 61.5 %copy-start.5 = (bf16[1024,256]{1,0:T(8,128)(2,1)S(1)}, bf16[1024,256]{1,0:T(8,128)(2,1)}, u32[]{:S(2)}) copy-start(bf16[1024,256]{1,0:T(8,128)(2,1)} %refs_1_.1) | copy-start | bytes 1572868
  0.6 17.3 %collective-permute-start.1 = (bf16[1024,256]{1,0:T(8,128)(2,1)}, bf16[1024,256]{1,0:T(8,128)(2,1)S(1)}, u32[]{:S(2)}, u32[]{:S(2)}) collective-permute-start(bf16[1024,256]{1,0:T(8,128)(2,1)} %refs_1_.1), channel_id=1, source_target_pairs={{0,2},{1,3},{2,4},{3,5},{4,6},{5,7},{6,0},{7,1},{8,10},{9,11},{10,... | collective-permute-start | bytes 1572872 | tf_op jit(solution)/shard_map/ppermute | solution.py:281
  6.4 56.7 %copy-start.10 = (s32[1024]{0:T(1024)}, s32[1024]{0:T(1024)S(1)}, u32[]{:S(2)}) copy-start(s32[1024]{0:T(1024)S(1)} %get-tuple-element.29) | copy-start | bytes 12292
  17.9 45.2 %copy-start.6 = (bf16[1024,256]{1,0:T(8,128)(2,1)}, bf16[1024,256]{1,0:T(8,128)(2,1)S(1)}, u32[]{:S(2)}) copy-start(bf16[1024,256]{1,0:T(8,128)(2,1)S(1)} %collective-permute-done.1.refs_3_) | copy-start | bytes 1572868
  17.9 19.9 %collective-permute-start.3 = (bf16[1024,256]{1,0:T(8,128)(2,1)S(1)}, bf16[1024,256]{1,0:T(8,128)(2,1)S(1)}, u32[]{:S(2)}, u32[]{:S(2)}) collective-permute-start(bf16[1024,256]{1,0:T(8,128)(2,1)S(1)} %collective-permute-done.1.refs_3_), channel_id=1, source_target_pairs={{0,2},{1,3},{2,4},{3,5},{4,6},{5,7},{6,0},{7,1},{8,10},{9,11},{10,... | collective-permute-start | bytes 1572872 | tf_op jit(solution)/shard_map/ppermute | solution.py:281
  18.6 15.0 %all-to-all-start = ((s32[8,1,1152]{2,1,0:T(1,128)}), s32[8,1,1152]{2,1,0:T(1,128)S(1)}, u32[]{:S(2)}, u32[]{:S(2)}) async-start(s32[8,1,1152]{2,1,0:T(1,128)} %broadcast_in_dim.45), calls=%async_computation | async-start | bytes 73728 | tf_op jit(solution)/shard_map/all_to_all | solution.py:248
  34.3 8.2 %all-to-all-start.4 = ((s32[4,1,384]{2,1,0:T(1,128)}), s32[4,1,384]{2,1,0:T(1,128)S(1)}, u32[]{:S(2)}, u32[]{:S(2)}) async-start(s32[4,1,384]{2,1,0:T(1,128)} %broadcast_in_dim.53), calls=%async_computation.4 | async-start | bytes 12288 | tf_op jit(solution)/shard_map/all_to_all | solution.py:248
  37.8 55.4 %copy-start.7 = (bf16[1024,256]{1,0:T(8,128)(2,1)}, bf16[1024,256]{1,0:T(8,128)(2,1)S(1)}, u32[]{:S(2)}) copy-start(bf16[1024,256]{1,0:T(8,128)(2,1)S(1)} %collective-permute-done.3.refs_5_) | copy-start | bytes 1572868
  37.8 24.9 %collective-permute-start.5 = (bf16[1024,256]{1,0:T(8,128)(2,1)S(1)}, bf16[1024,256]{1,0:T(8,128)(2,1)S(1)}, u32[]{:S(2)}, u32[]{:S(2)}) collective-permute-start(bf16[1024,256]{1,0:T(8,128)(2,1)S(1)} %collective-permute-done.3.refs_5_), channel_id=1, source_target_pairs={{0,2},{1,3},{2,4},{3,5},{4,6},{5,7},{6,0},{7,1},{8,10},{9,11},{10,... | collective-permute-start | bytes 1572872 | tf_op jit(solution)/shard_map/ppermute | solution.py:281
  58.3 35.5 %all-to-all-start.3 = ((bf16[4,384,256]{2,1,0:T(8,128)(2,1)}), bf16[4,384,256]{2,1,0:T(8,128)(2,1)S(1)}, u32[]{:S(2)}, u32[]{:S(2)}) async-start(bf16[4,384,256]{2,1,0:T(8,128)(2,1)} %broadcast_in_dim.51), calls=%async_computation.3 | async-start | bytes 1572864 | tf_op jit(solution)/shard_map/all_to_all | solution.py:248
  62.1 31.7 %collective-permute-start = (bf16[1024,256]{1,0:T(8,128)(2,1)S(1)}, bf16[1024,256]{1,0:T(8,128)(2,1)S(1)}, u32[]{:S(2)}, u32[]{:S(2)}) collective-permute-start(bf16[1024,256]{1,0:T(8,128)(2,1)S(1)} %copy-done.5), channel_id=1, source_target_pairs={{0,1},{1,0},{2,3},{3,2},{4,5},{5,4},{6,7},{7,6},{8,9},{9,8},{10,11... | collective-permute-start | bytes 1572872 | tf_op jit(solution)/shard_map/ppermute | solution.py:282
  62.1 31.7 %collective-permute-start.2 = (bf16[1024,256]{1,0:T(8,128)(2,1)S(1)}, bf16[1024,256]{1,0:T(8,128)(2,1)}, u32[]{:S(2)}, u32[]{:S(2)}) collective-permute-start(bf16[1024,256]{1,0:T(8,128)(2,1)S(1)} %collective-permute-done.1.refs_3_), channel_id=1, source_target_pairs={{0,1},{1,0},{2,3},{3,2},{4,5},{5,4},{6,7},{7,6},{8,9},{9,8},{10,11... | collective-permute-start | bytes 1572872 | tf_op jit(solution)/shard_map/ppermute | solution.py:282
  62.6 31.2 %collective-permute-start.4 = (bf16[1024,256]{1,0:T(8,128)(2,1)S(1)}, bf16[1024,256]{1,0:T(8,128)(2,1)}, u32[]{:S(2)}, u32[]{:S(2)}) collective-permute-start(bf16[1024,256]{1,0:T(8,128)(2,1)S(1)} %collective-permute-done.3.refs_5_), channel_id=1, source_target_pairs={{0,1},{1,0},{2,3},{3,2},{4,5},{5,4},{6,7},{7,6},{8,9},{9,8},{10,11... | collective-permute-start | bytes 1572872 | tf_op jit(solution)/shard_map/ppermute | solution.py:282
  62.7 30.5 %copy-start.8 = (bf16[1024,256]{1,0:T(8,128)(2,1)}, bf16[1024,256]{1,0:T(8,128)(2,1)S(1)}, u32[]{:S(2)}) copy-start(bf16[1024,256]{1,0:T(8,128)(2,1)S(1)} %collective-permute-done.5.refs_7_) | copy-start | bytes 1572868
  62.7 31.2 %collective-permute-start.6 = (bf16[1024,256]{1,0:T(8,128)(2,1)S(1)}, bf16[1024,256]{1,0:T(8,128)(2,1)}, u32[]{:S(2)}, u32[]{:S(2)}) collective-permute-start(bf16[1024,256]{1,0:T(8,128)(2,1)S(1)} %collective-permute-done.5.refs_7_), channel_id=1, source_target_pairs={{0,1},{1,0},{2,3},{3,2},{4,5},{5,4},{6,7},{7,6},{8,9},{9,8},{10,11... | collective-permute-start | bytes 1572872 | tf_op jit(solution)/shard_map/ppermute | solution.py:282
  93.8 0.8 copy-start.9
  93.8 1.0 copy-start.1
  134.1 24.4 %all-to-all-start.5 = ((bf16[8,192,256]{2,1,0:T(8,128)(2,1)}), bf16[8,192,256]{2,1,0:T(8,128)(2,1)S(1)}, u32[]{:S(2)}, u32[]{:S(2)}) async-start(bf16[8,192,256]{2,1,0:T(8,128)(2,1)} %bitcast.22), calls=%async_computation.5 | async-start | bytes 1572864 | tf_op jit(solution)/shard_map/all_to_all | solution.py:328
  147.7 16.2 %copy-start = (bf16[4096,256]{1,0:T(8,128)(2,1)S(1)}, bf16[4096,256]{1,0:T(8,128)(2,1)}, u32[]{:S(2)}) copy-start(bf16[4096,256]{1,0:T(8,128)(2,1)} %scatter.1) | copy-start | bytes 6291460
  158.5 0.9 copy-start.3
  159.4 43.6 %all-to-all-start.1 = ((bf16[8,384,256]{2,1,0:T(8,128)(2,1)}), bf16[8,384,256]{2,1,0:T(8,128)(2,1)}, u32[]{:S(2)}, u32[]{:S(2)}) async-start(bf16[8,384,256]{2,1,0:T(8,128)(2,1)} %bitcast.30), calls=%async_computation.1 | async-start | bytes 3145728 | tf_op jit(solution)/shard_map/all_to_all | solution.py:298
  164.0 1.0 copy-start.2
  165.0 14.4 %collective-permute-start.11 = (bf16[1024,256]{1,0:T(8,128)(2,1)S(1)}, bf16[1024,256]{1,0:T(8,128)(2,1)S(1)}, u32[]{:S(2)}, u32[]{:S(2)}) collective-permute-start(bf16[1024,256]{1,0:T(8,128)(2,1)S(1)} %constant_dynamic-slice_fusion.2), channel_id=1, source_target_pairs={{0,16},{8,24},{16,0},{24,8},{1,17},{9,25},{17,1},{25,9},{2,18},{10... | collective-permute-start | bytes 1572872 | tf_op jit(solution)/shard_map/ppermute | solution.py:234
  168.0 15.1 %collective-permute-start.7 = (bf16[1024,256]{1,0:T(8,128)(2,1)}, bf16[1024,256]{1,0:T(8,128)(2,1)S(1)}, u32[]{:S(2)}, u32[]{:S(2)}) collective-permute-start(bf16[1024,256]{1,0:T(8,128)(2,1)} %constant_dynamic-slice_fusion.4), channel_id=1, source_target_pairs={{0,8},{8,0},{16,24},{24,16},{1,9},{9,1},{17,25},{25,17},{2,10},{10... | collective-permute-start | bytes 1572872 | tf_op jit(solution)/shard_map/ppermute | solution.py:234
  181.3 17.9 %copy-start.4 = (bf16[8,192,256]{2,1,0:T(8,128)(2,1)S(1)}, bf16[8,192,256]{2,1,0:T(8,128)(2,1)}, u32[]{:S(2)}) copy-start(bf16[8,192,256]{2,1,0:T(8,128)(2,1)} %copy-done.3) | copy-start | bytes 2359300
  181.3 8.2 %collective-permute-start.12 = (bf16[512,256]{1,0:T(8,128)(2,1)}, bf16[512,256]{1,0:T(8,128)(2,1)}, u32[]{:S(2)}, u32[]{:S(2)}) collective-permute-start(bf16[512,256]{1,0:T(8,128)(2,1)} %constant_dynamic-slice_fusion.1), channel_id=1, source_target_pairs={{0,8},{8,0},{16,24},{24,16},{1,9},{9,1},{17,25},{25,17},{2,10},{10... | collective-permute-start | bytes 786440 | tf_op jit(solution)/shard_map/ppermute | solution.py:234
  183.2 8.9 %collective-permute-start.8 = (bf16[512,256]{1,0:T(8,128)(2,1)S(1)}, bf16[512,256]{1,0:T(8,128)(2,1)S(1)}, u32[]{:S(2)}, u32[]{:S(2)}) collective-permute-start(bf16[512,256]{1,0:T(8,128)(2,1)S(1)} %constant_dynamic-slice_fusion.3), channel_id=1, source_target_pairs={{0,16},{8,24},{16,0},{24,8},{1,17},{9,25},{17,1},{25,9},{2,18},{10... | collective-permute-start | bytes 786440 | tf_op jit(solution)/shard_map/ppermute | solution.py:234
  190.6 7.1 %collective-permute-start.13 = (bf16[512,256]{1,0:T(8,128)(2,1)S(1)}, bf16[512,256]{1,0:T(8,128)(2,1)S(1)}, u32[]{:S(2)}, u32[]{:S(2)}) collective-permute-start(bf16[512,256]{1,0:T(8,128)(2,1)S(1)} %add_convert_fusion.2), channel_id=1, source_target_pairs={{0,8},{8,0},{16,24},{24,16},{1,9},{9,1},{17,25},{25,17},{2,10},{10... | collective-permute-start | bytes 786440 | tf_op jit(solution)/shard_map/ppermute | solution.py:240
  192.2 8.7 %collective-permute-start.9 = (bf16[512,256]{1,0:T(8,128)(2,1)S(1)}, bf16[512,256]{1,0:T(8,128)(2,1)S(1)}, u32[]{:S(2)}, u32[]{:S(2)}) collective-permute-start(bf16[512,256]{1,0:T(8,128)(2,1)S(1)} %add_convert_fusion.3), channel_id=1, source_target_pairs={{0,16},{8,24},{16,0},{24,8},{1,17},{9,25},{17,1},{25,9},{2,18},{10... | collective-permute-start | bytes 786440 | tf_op jit(solution)/shard_map/ppermute | solution.py:240
  197.9 16.4 %collective-permute-start.14 = (bf16[1024,256]{1,0:T(8,128)(2,1)S(1)}, bf16[1024,256]{1,0:T(8,128)(2,1)S(1)}, u32[]{:S(2)}, u32[]{:S(2)}) collective-permute-start(bf16[1024,256]{1,0:T(8,128)(2,1)S(1)} %maximum_select_fusion.3), channel_id=1, source_target_pairs={{0,16},{8,24},{16,0},{24,8},{1,17},{9,25},{17,1},{25,9},{2,18},{10... | collective-permute-start | bytes 1572872 | tf_op jit(solution)/shard_map/ppermute | solution.py:240
  199.3 14.1 %collective-permute-start.15 = (bf16[192,256]{1,0:T(8,128)(2,1)S(1)}, bf16[192,256]{1,0:T(8,128)(2,1)S(1)}, u32[]{:S(2)}, u32[]{:S(2)}) collective-permute-start(bf16[192,256]{1,0:T(8,128)(2,1)S(1)} %reduce_sum.22), channel_id=1, source_target_pairs={{0,8},{8,0},{16,24},{24,16},{1,9},{9,1},{17,25},{25,17},{2,10},{10... | collective-permute-start | bytes 294920 | tf_op jit(solution)/shard_map/ppermute | solution.py:331
  201.1 13.5 %collective-permute-start.10 = (bf16[1024,256]{1,0:T(8,128)(2,1)S(1)}, bf16[1024,256]{1,0:T(8,128)(2,1)S(1)}, u32[]{:S(2)}, u32[]{:S(2)}) collective-permute-start(bf16[1024,256]{1,0:T(8,128)(2,1)S(1)} %maximum_select_fusion.2), channel_id=1, source_target_pairs={{0,8},{8,0},{16,24},{24,16},{1,9},{9,1},{17,25},{25,17},{2,10},{10... | collective-permute-start | bytes 1572872 | tf_op jit(solution)/shard_map/ppermute | solution.py:240
  213.4 4.7 %collective-permute-start.16 = (bf16[192,256]{1,0:T(8,128)(2,1)S(1)}, bf16[192,256]{1,0:T(8,128)(2,1)S(1)}, u32[]{:S(2)}, u32[]{:S(2)}) collective-permute-start(bf16[192,256]{1,0:T(8,128)(2,1)S(1)} %add_convert_fusion.5), channel_id=1, source_target_pairs={{0,16},{8,24},{16,0},{24,8},{1,17},{9,25},{17,1},{25,9},{2,18},{10... | collective-permute-start | bytes 294920 | tf_op jit(solution)/shard_map/ppermute | solution.py:331

commit v2 on v1

v2 whole, which is shorter than its diff:
```python
import math

import jax
import jax.numpy as jnp
from jax import lax
from jax.experimental import pallas as pl
from jax.experimental.pallas import tpu as pltpu
from jax.sharding import PartitionSpec as P

INV_TEMP = 20.0
LEARN_RATE = 0.05
EPSILON = 1e-06
LOG2_E = math.log2(math.e)
F32 = jnp.float32
BF16 = jnp.bfloat16
NT = (((1,), (1,)), ((), ()))


def unit_rows(matrix):
    back_norm = 1.0 / jnp.sqrt(jnp.sum(matrix * matrix, axis=-1, keepdims=True) + EPSILON)
    return (matrix * back_norm, back_norm)


def iota(shape, axis):
    return lax.broadcasted_iota(jnp.int32, shape, axis).astype(F32)


def to_sub(row):
    return jnp.transpose(jnp.broadcast_to(row, (128, row.shape[1])))[:, :1]


def to_lane(col):
    return jnp.transpose(jnp.broadcast_to(col, (col.shape[0], 128)))[:1, :]


def one_hot(test):
    return jnp.where(test, 1.0, 0.0).astype(BF16)


def earlier_count(mask):
    total, step = mask, 1
    lane = lax.broadcasted_iota(jnp.int32, mask.shape, 1)
    while step < mask.shape[1]:
        total = total + jnp.where(lane >= step, pltpu.roll(total, step, axis=1), 0.0)
        step *= 2
    return total - mask


def rows_at(start, size):
    return pl.ds(pl.multiple_of(start * size, size), size)


def route_kernel(me_ref, gid_ref, own_ref, table_ref, found_ref, rank_ref, rid_ref, place_ref, send_ref):
    blocks, examples = gid_ref.shape
    table_rows = table_ref.shape[0]
    slots = rid_ref.shape[1]
    chunk = math.gcd(table_rows, 512)
    base = me_ref[0] * table_rows

    def normalize(step, carry):
        part = table_ref[rows_at(step, chunk), :]
        send_ref[rows_at(step, chunk), :] = unit_rows(part)[0].astype(BF16)
        return carry

    lax.fori_loop(0, table_rows // chunk, normalize, 0)
    local = gid_ref[...] - base
    mine = jnp.logical_and(local >= 0, local < table_rows)
    rank = earlier_count(jnp.where(mine, 1.0, 0.0))
    rank_ref[...] = jnp.where(mine, rank, -1.0)
    local = local.astype(F32)

    owner = lax.broadcasted_iota(jnp.int32, (blocks, examples), 0)
    own = own_ref[...]
    named = jnp.logical_and(own >= owner * table_rows, own < (owner + 1) * table_rows)
    count = earlier_count(jnp.where(named, 1.0, 0.0))
    spot = jnp.where(named, count + owner.astype(F32) * slots, 0.0)
    place_ref[...] = jnp.sum(spot, axis=0, keepdims=True)

    for block in range(blocks):
        chosen = iota((slots, examples), 0) == rank_ref[block : block + 1, :]
        wanted = jnp.sum(
            jnp.where(chosen, local[block : block + 1, :], 0.0), axis=1, keepdims=True
        )
        rid_ref[block : block + 1, :] = to_lane(wanted)

    def find(pair, carry):
        ids = [to_sub(rid_ref[pl.ds(2 * pair + core, 1), :]) for core in range(2)]
        pick = one_hot(jnp.concatenate(ids, axis=0) == iota((2 * slots, table_rows), 1))
        got = jnp.dot(pick, send_ref[...], preferred_element_type=F32)
        found_ref[rows_at(pair, 2 * slots), :] = got.astype(BF16)
        return carry

    lax.fori_loop(0, blocks // 2, find, 0)


def neg_ids(part):
    digits = part.astype(F32)
    return digits[:, :1] * 4096.0 + digits[:, 1:2] * 64.0 + digits[:, 2:3]


def owner_kernel(first, me_ref, *refs):
    queries, refs = refs[:2], refs[2:]
    rank_ref, rid_ref, found_any, negs_ref, refs = *refs[:4], refs[4:]
    if first:
        pull_ref, outrid_ref, neg_ref, ids_ref, refs = *refs[:4], refs[4:]
    else:
        prior_ref, pull_ref, outrid_ref, neg_ref, refs = *refs[:4], refs[4:]
    held, found, nsub, exps, copy_sem = refs
    slots = rid_ref.shape[1]
    examples, width = held.shape[1], held.shape[2]
    negs = negs_ref.shape[0]
    chunk = math.gcd(negs, 256)
    copies = []
    for spot in range(2):
        source = rows_at(me_ref[1 + spot], slots)
        there = found.at[spot * slots : (spot + 1) * slots]
        copies.append(pltpu.make_async_copy(found_any.at[source], there, copy_sem.at[2 + spot]))
        copies.append(pltpu.make_async_copy(queries[spot], held.at[spot], copy_sem.at[spot]))
    for copy in copies:
        copy.start()
    base = (me_ref[0] * me_ref[3]).astype(F32)
    nsub[...] = jnp.broadcast_to(neg_ids(negs_ref[:, width:]) - base, nsub.shape)
    if first:
        ids_ref[...] = jnp.transpose(nsub[...])[:1, :]
    ranks = [rank_ref[pl.ds(me_ref[1 + spot], 1), :] for spot in range(2)]
    rids = [rid_ref[pl.ds(me_ref[1 + spot], 1), :] for spot in range(2)]
    rid = jnp.concatenate(rids, axis=1)
    outrid_ref[...] = rid
    for copy in copies:
        copy.wait()
    picked = []
    for spot in range(2):
        pick = one_hot(iota((slots, examples), 0) == ranks[spot])
        picked.append(jnp.dot(pick, held[spot], preferred_element_type=F32))
    query_hat, _ = unit_rows(jnp.concatenate(picked, axis=0))
    query_send = query_hat.astype(BF16)
    s_pos = jnp.sum(query_send.astype(F32) * found[...].astype(F32), axis=1, keepdims=True)
    pos_exp = to_lane(jnp.exp(INV_TEMP * s_pos))
    total = pos_exp
    for step in range(negs // chunk):
        part = pl.ds(step * chunk, chunk)
        scores = lax.dot_general(
            negs_ref[part, :width], query_send, NT, preferred_element_type=F32
        )
        keep = nsub[part, :][:, :1] != rid
        some = jnp.where(keep, jnp.exp2(scores * (INV_TEMP * LOG2_E)), 0.0)
        exps[part, :] = some.astype(BF16)
        total = total + jnp.sum(some, axis=0, keepdims=True)
    scale = 1.0 / total
    scaled = (query_send.astype(F32) * to_sub(scale)).astype(BF16)
    for step in range(negs // chunk):
        part = pl.ds(step * chunk, chunk)
        more = jnp.dot(exps[part, :], scaled, preferred_element_type=F32)
        neg_ref[part, :] = more if first else prior_ref[part, :] + more
    p_pos = to_sub(pos_exp * scale)
    pull_ref[...] = (INV_TEMP * (p_pos - 1.0) * query_hat).astype(BF16)


def scatter_kernel(pieces, start_ref, *refs):
    pulls, rids, outs, held = refs[:pieces], refs[pieces : 2 * pieces], refs[2 * pieces : -1], refs[-1]
    size = pulls[0].shape[0]
    for piece, pull_ref in enumerate(pulls):
        held[piece * size : (piece + 1) * size, :] = pull_ref[...]
    ids = jnp.concatenate([rid_ref[...] for rid_ref in rids], axis=1)
    for side, out_ref in enumerate(outs):
        rows = math.gcd(out_ref.shape[0], 512)
        for step in range(out_ref.shape[0] // rows):
            offset = (start_ref[side] + step * rows).astype(F32)
            put = one_hot(iota((rows, ids.shape[1]), 0) == ids - offset)
            part = jnp.dot(put, held[...], preferred_element_type=F32)
            out_ref[step * rows : (step + 1) * rows, :] = part.astype(BF16)


def home_kernel(me_ref, query_ref, place_ref, gid_ref, back_ref, negs_ref, ids_ref, grad_ref, loss_ref):
    examples, width = query_ref.shape
    spots = back_ref.shape[0]
    pick = one_hot(iota((examples, spots), 1) == to_sub(place_ref[...]))
    pos_e = jnp.dot(pick, back_ref[...], preferred_element_type=F32)
    query_hat, back_norm = unit_rows(query_ref[...].astype(F32))
    query_send = query_hat.astype(BF16)
    s_pos = INV_TEMP * jnp.sum(query_send.astype(F32) * pos_e, axis=1, keepdims=True)
    pos_exp = jnp.exp(s_pos)
    negs = negs_ref[:, :width]
    scores = lax.dot_general(query_send, negs, NT, preferred_element_type=F32)
    local = (gid_ref[...] - me_ref[0] * me_ref[1]).astype(F32)
    keep = ids_ref[...] != to_sub(local)
    part = jnp.where(keep, jnp.exp2(scores * (INV_TEMP * LOG2_E)), 0.0)
    total = pos_exp + jnp.sum(part, axis=1, keepdims=True)
    scale = 1.0 / total
    loss_ref[...] = to_lane(jnp.log(total) - s_pos)
    probs = (part * scale).astype(BF16)
    g_query = INV_TEMP * (
        (pos_exp * scale - 1.0) * pos_e + jnp.dot(probs, negs, preferred_element_type=F32)
    )
    along = jnp.sum(query_hat * g_query, axis=1, keepdims=True)
    grad_ref[...] = ((g_query - query_hat * along) * back_norm).astype(BF16)


def update_kernel(start_ref, table_ref, state_ref, *refs):
    pieces, refs = refs[:-6], refs[-6:]
    neg_ref, row_ref, new_ref, new_state_ref, held, copy_sem = refs
    rows = table_ref.shape[0]
    step = pl.program_id(0)

    @pl.when(step == 0)
    def _():
        size = pieces[0].shape[0]
        copies = [
            pltpu.make_async_copy(
                piece,
                held.at[pl.ds(pl.multiple_of(start_ref[spot], size), size)],
                copy_sem.at[spot],
            )
            for spot, piece in enumerate(pieces)
        ]
        for copy in copies:
            copy.start()
        for copy in copies:
            copy.wait()

    offset = (step * rows).astype(F32)
    put = one_hot(iota((rows, row_ref.shape[1]), 0) == row_ref[...] - offset)
    g_unit = held[rows_at(step, rows), :].astype(F32) + jnp.dot(
        put, neg_ref[...], preferred_element_type=F32
    )
    table = table_ref[...]
    unit, back_norm = unit_rows(table)
    g_row = (g_unit - unit * jnp.sum(unit * g_unit, axis=1, keepdims=True)) * back_norm
    state = to_sub(state_ref[...]) + jnp.mean(g_row * g_row, axis=1, keepdims=True)
    new_state_ref[...] = to_lane(state)
    new_ref[...] = table - g_row * (LEARN_RATE * lax.rsqrt(state))


def whole(ndim=2):
    return pl.BlockSpec(memory_space=pltpu.VMEM)


def flip(name, count, bit):
    return [(index, index ^ (1 << bit)) for index in range(count)]


def add(left, right):
    return (left.astype(F32) + right.astype(F32)).astype(BF16)


def halve(value, name, count, bit):
    half = value.shape[0] // 2
    mine = (lax.axis_index(name) >> bit) & 1
    give = lax.dynamic_slice_in_dim(value, (1 - mine) * half, half, 0)
    keep = lax.dynamic_slice_in_dim(value, mine * half, half, 0)
    return add(keep, lax.ppermute(give, name, flip(name, count, bit)))


def double(value, name, count, bit):
    mine = (lax.axis_index(name) >> bit) & 1
    got = lax.ppermute(value, name, flip(name, count, bit))
    low = jnp.concatenate([value, got], axis=0)
    high = jnp.concatenate([got, value], axis=0)
    return jnp.where(mine == 0, low, high)


def to_all(value, name, count):
    copies = jnp.broadcast_to(value[None], (count, *value.shape))
    return lax.all_to_all(copies, name, split_axis=0, concat_axis=0, tiled=True)


def cost(flops, traffic):
    return pl.CostEstimate(flops=int(flops), bytes_accessed=int(traffic), transcendentals=0)


def on_device(queries, item_table, adagrad_state, pos_owner, pos_row, neg_rows):
    examples, width = queries.shape
    table_rows = item_table.shape[0]
    neg_dev = neg_rows.shape[0]
    items = lax.axis_size("item")
    groups = lax.axis_size("dp")
    bits = groups.bit_length() - 1
    assert groups == 1 << bits and bits > 0
    assert items & (items - 1) == 0 and items > 1
    capacity = 3 * examples // items
    slots = -(-capacity // 128) * 128
    negs = groups * items * neg_dev
    item = lax.axis_index("item")
    group = lax.axis_index("dp")
    smem = pl.BlockSpec(memory_space=pltpu.SMEM)
    anywhere = pl.BlockSpec(memory_space=pl.ANY)

    ring = [(index, (index + 2) % items) for index in range(items)]
    pair = flip("item", items, 0)
    steps, block = [], queries
    for step in range(items // 2):
        if step:
            with jax.named_scope(f"ring{step}"):
                block = lax.ppermute(block, "item", ring)
        with jax.named_scope(f"pair{step}"):
            other = lax.ppermute(block, "item", pair)
        steps.append((block, other, (item - 2 * step) % items, ((item ^ 1) - 2 * step) % items))

    own_gid = pos_owner[:, 0] * table_rows + pos_row
    with jax.named_scope("gids"):
        gids = to_all(own_gid, "item", items)
    my_ids = item * table_rows + neg_rows
    digits = jnp.stack([my_ids // 4096, my_ids // 64 % 64, my_ids % 64], axis=1).astype(BF16)
    my_negs = unit_rows(item_table[neg_rows])[0].astype(BF16)
    my_negs = jnp.concatenate([my_negs, jnp.pad(digits, ((0, 0), (0, 125)))], axis=1)
    with jax.named_scope("negs_item"):
        column_negs = to_all(my_negs, "item", items).reshape(items * neg_dev, width + 128)
    with jax.named_scope("negs_dp"):
        all_negs = to_all(column_negs, "dp", groups).reshape(negs, width + 128)

    found, rank, rid, place = pl.pallas_call(
        route_kernel,
        out_shape=(
            jax.ShapeDtypeStruct((items * slots, width), BF16),
            jax.ShapeDtypeStruct((items, examples), F32),
            jax.ShapeDtypeStruct((items, slots), F32),
            jax.ShapeDtypeStruct((1, examples), F32),
        ),
        in_specs=[smem, whole(), whole(), whole()],
        out_specs=(whole(), whole(), whole(), whole()),
        scratch_shapes=[pltpu.VMEM((table_rows, width), BF16)],
        cost_estimate=cost(2 * items * slots * table_rows * width, 8 * table_rows * width),
        name="route",
    )(item[None], gids, own_gid[None, :], item_table)

    pulls, rids, neg_part = [], [], None
    for step, (block, other, source, other_source) in enumerate(steps):
        first = step == 0
        scalars = jnp.stack([item, source, other_source, jnp.int32(table_rows)])
        out = pl.pallas_call(
            lambda *refs, first=first: owner_kernel(first, *refs),
            out_shape=(
                jax.ShapeDtypeStruct((2 * slots, width), BF16),
                jax.ShapeDtypeStruct((1, 2 * slots), F32),
                jax.ShapeDtypeStruct((negs, width), F32),
            )
            + ((jax.ShapeDtypeStruct((1, negs), F32),) if first else ()),
            in_specs=[smem, anywhere, anywhere, whole(), whole(), anywhere, whole()]
            + ([] if first else [whole()]),
            out_specs=(whole(),) * (4 if first else 3),
            scratch_shapes=[
                pltpu.VMEM((2, examples, width), BF16),
                pltpu.VMEM((2 * slots, width), BF16),
                pltpu.VMEM((negs, 128), F32),
                pltpu.VMEM((negs, 2 * slots), BF16),
                pltpu.SemaphoreType.DMA((4,)),
            ],
            cost_estimate=cost(6 * slots * negs * width * 2, 8 * negs * width),
            name=f"owner{step}",
        )(
            *(scalars, block, other, rank, rid, found, all_negs),
            *(() if first else (neg_part,)),
        )
        pulls.append(out[0])
        rids.append(out[1])
        neg_part = out[2]
        if first:
            local_ids = out[3]

    with jax.named_scope("back"):
        back = lax.all_to_all(
            found.reshape(items, slots, width), "item", split_axis=0, concat_axis=0, tiled=True
        ).reshape(items * slots, width)

    quarter = table_rows // 4
    orders = [list(range(bits)), list(range(bits))[::-1]]
    firsts = [(group >> order[0]) & 1 for order in orders]
    starts = [2 * side * quarter for side in range(2)]

    def scatter(offsets, name):
        return pl.pallas_call(
            lambda *refs: scatter_kernel(len(pulls), *refs),
            out_shape=(jax.ShapeDtypeStruct((quarter, width), BF16),) * 2,
            in_specs=[smem] + [whole()] * (2 * len(pulls)),
            out_specs=(whole(), whole()),
            scratch_shapes=[pltpu.VMEM((items * slots, width), BF16)],
            cost_estimate=cost(4 * items * slots * quarter * width, 4 * quarter * width),
            name=name,
        )(jnp.stack(offsets), *pulls, *rids)

    gives = scatter([start + (1 - mine) * quarter for start, mine in zip(starts, firsts)], "give")
    gots = []
    for side in range(2):
        with jax.named_scope(f"halve{side}"):
            gots.append(
                lax.ppermute(gives[side], "dp", flip("dp", groups, orders[side][0]))
            )
    keeps = scatter([start + mine * quarter for start, mine in zip(starts, firsts)], "keep")
    pieces, places = [], []
    for side, order in enumerate(orders):
        value = add(keeps[side], gots[side])
        for bit in order[1:]:
            value = halve(value, "dp", groups, bit)
        for bit in order[:0:-1]:
            value = double(value, "dp", groups, bit)
        got = lax.ppermute(value, "dp", flip("dp", groups, order[0]))
        pieces += [value, got]
        places += [starts[side] + firsts[side] * quarter, starts[side] + (1 - firsts[side]) * quarter]

    neg_sum = (INV_TEMP * neg_part).astype(BF16).reshape(groups, items, neg_dev, width)
    for bit in range(items.bit_length() - 1):
        split = neg_sum.reshape(groups, neg_sum.shape[1] // 2, 2, neg_dev, width)
        mine = (item >> bit) & 1
        give = lax.dynamic_index_in_dim(split, 1 - mine, 2, keepdims=False)
        keep = lax.dynamic_index_in_dim(split, mine, 2, keepdims=False)
        neg_sum = add(keep, lax.ppermute(give, "item", flip("item", items, bit)))
    neg_sum = neg_sum.reshape(groups * neg_dev, width)
    for bit in range(bits):
        neg_sum = add(neg_sum, lax.ppermute(neg_sum, "dp", flip("dp", groups, bit)))
    neg_spots = lax.dynamic_slice_in_dim(
        local_ids.reshape(groups, items, neg_dev), item, 1, 1
    ).reshape(1, groups * neg_dev)

    chunk = math.gcd(table_rows, 512)
    new_table, new_state = pl.pallas_call(
        update_kernel,
        out_shape=(
            jax.ShapeDtypeStruct((table_rows, width), F32),
            jax.ShapeDtypeStruct((1, table_rows), F32),
        ),
        grid=(table_rows // chunk,),
        in_specs=[
            smem,
            pl.BlockSpec((chunk, width), lambda step: (step, 0)),
            pl.BlockSpec((1, chunk), lambda step: (0, step)),
            *[anywhere] * len(pieces),
            whole(),
            whole(),
        ],
        out_specs=(
            pl.BlockSpec((chunk, width), lambda step: (step, 0)),
            pl.BlockSpec((1, chunk), lambda step: (0, step)),
        ),
        scratch_shapes=[
            pltpu.VMEM((table_rows, width), BF16),
            pltpu.SemaphoreType.DMA((len(pieces),)),
        ],
        cost_estimate=cost(8 * table_rows * width, 10 * table_rows * width),
        name="update",
    )(jnp.stack(places), item_table, adagrad_state[None, :], *pieces, neg_sum, neg_spots)

    part = math.gcd(examples, 256)
    query_grad, example_loss = pl.pallas_call(
        home_kernel,
        out_shape=(
            jax.ShapeDtypeStruct((examples, width), BF16),
            jax.ShapeDtypeStruct((1, examples), F32),
        ),
        grid=(examples // part,),
        in_specs=[
            smem,
            pl.BlockSpec((part, width), lambda step: (step, 0)),
            pl.BlockSpec((1, part), lambda step: (0, step)),
            pl.BlockSpec((1, part), lambda step: (0, step)),
            whole(),
            whole(),
            whole(),
        ],
        out_specs=(
            pl.BlockSpec((part, width), lambda step: (step, 0)),
            pl.BlockSpec((1, part), lambda step: (0, step)),
        ),
        cost_estimate=cost(4 * examples * (negs + items * slots) * width, 8 * negs * width),
        name="home",
    )(
        jnp.stack([item, jnp.int32(table_rows)]),
        *(queries, place, own_gid[None, :], back, all_negs, local_ids),
    )
    return (query_grad, example_loss.reshape(examples), new_table, new_state.reshape(table_rows))


def solution(mesh):
    placed = (
        P(("dp", "item"), None),
        P("item", None),
        P("item"),
        P(("dp", "item"), None),
        P(("dp", "item")),
        P(("dp", "item")),
    )
    return jax.shard_map(
        on_device,
        mesh=mesh,
        in_specs=placed,
        out_specs=(P(("dp", "item"), None), P(("dp", "item")), P("item", None), P("item")),
        check_vma=False,
    )
```

time: 231 us -> 185 us (0.80)
  Pallas kernels: 96.8 us -> 79.8 us
  blocking collectives: 14.8 us -> 0 us
  waiting for transfers between devices: 54 us -> 44.7 us
    all_to_all x1 -> x0, blocking collectives: 14.8 us -> none  [to_all(): return lax.all_to_all(copies, name, split_axis=0, concat_axis=0, tiled=True)]
    pallas_call x1, Pallas kernels: 28.8 us -> 15.3 us  [on_device(): pl.pallas_call(route_kernel, out_shape=(jax.ShapeDtypeStruct((items * slo...]
    all_to_all x1 -> x0, waiting for transfers between devices: 10.8 us -> none  [on_device(): lax.all_to_all(parts, 'item', split_axis=0, concat_axis=0, tiled=True)]
    ppermute x6 -> x11, starting transfers between devices: 9.26 us -> 15.2 us  [the longest x3 4.8 us: on_device(): neg_sum = add(keep, lax.ppermute(give, 'item', flip('item', items, bit)))]
    ppermute x3, waiting for transfers between devices: 11.5 us -> 6.17 us  [on_device(): block = lax.ppermute(block, 'item', ring)]
    another operation x0 -> x10, other arithmetic: none -> 4.96 us  [the longest x4 2.41 us: on_device(): scalars = jnp.stack([item, source, other_source, jnp.int32(table_rows)])]
    pallas_call x2 -> x6, Pallas kernels: 46.8 us -> 41.9 us  [the longest x4 30.7 us: on_device(): pl.pallas_call(lambda *refs, first=first: owner_kernel(first, *refs), out...]
    all_to_all x3, waiting for transfers between devices: 11.1 us -> 15.7 us  [to_all(): return lax.all_to_all(copies, name, split_axis=0, concat_axis=0, tiled=True)]
  transfers between devices with their start and end apart: 22 -> 24, of which waited for: 8 -> 9; matrix products, arithmetic and copies ran while one was open for 8% -> 9% of each run, Pallas kernels for 21% -> 37%
where the time goes in v2:
time: 185 us; the launch traced here: 184 us
  Pallas kernels  79.8 us (43%)
  waiting for transfers between devices  44.7 us (24%)
  starting transfers between devices  37.4 us (20%)
  local copies, waits for them, and re-layouts  10.7 us (6%)
  other arithmetic  10.6 us (6%)
    pallas_call x4, Pallas kernels, on_device(): pl.pallas_call(lambda *refs, first=first: owner_kernel(first, *refs), out...  30.7 us
    all_to_all x3, waiting for transfers between devices, to_all(): return lax.all_to_all(copies, name, split_axis=0, concat_axis=0, tiled=True)  15.7 us
    pallas_call x1, Pallas kernels, on_device(): pl.pallas_call(route_kernel, out_shape=(jax.ShapeDtypeStruct((items * slo...  15.3 us
    all_to_all x3, starting transfers between devices, to_all(): return lax.all_to_all(copies, name, split_axis=0, concat_axis=0, tiled=True)  13.7 us
    pallas_call x1, Pallas kernels, on_device(): pl.pallas_call(update_kernel, out_shape=(jax.ShapeDtypeStruct((table_rows...  12.2 us
    pallas_call x2, Pallas kernels, scatter(): pl.pallas_call(lambda *refs: scatter_kernel(len(pulls), *refs), out_shape...  11.2 us
    pallas_call x1, Pallas kernels, on_device(): pl.pallas_call(home_kernel, out_shape=(jax.ShapeDtypeStruct((examples, wi...  10.4 us
    ppermute x2, waiting for transfers between devices, on_device(): lax.ppermute(gives[side], 'dp', flip('dp', groups, orders[side][0]))  9.72 us
  transfers between devices with their start and end apart: 24, of which 9 were waited for; matrix products, arithmetic and copies ran while one was open for 9% of the time, Pallas kernels for 37%

profile of v2, /device:TPU:0, one launch (start us, length us, event | category | flops | bytes accessed | tf_op | source)
XLA Modules:
  0.0 184.3 jit_solution(15199118697153107269)
XLA Ops:
  0.6 0.7 broadcast_multiply_fusion
  1.4 0.7 add.145
  2.7 6.4 %all-to-all-start = ((s32[8,1,1024]{2,1,0:T(1,128)}), s32[8,1,1024]{2,1,0:T(1,128)S(1)}, u32[]{:S(2)}, u32[]{:S(2)}) async-start(s32[8,1,1024]{2,1,0:T(1,128)} %broadcast_in_dim.14), calls=%async_computation | async-start | bytes 65536 | tf_op jit(solution)/shard_map/gids/all_to_all | solution.py:264
  9.1 2.0 %collective-permute-start.1 = (bf16[1024,256]{1,0:T(8,128)(2,1)}, bf16[1024,256]{1,0:T(8,128)(2,1)}, u32[]{:S(2)}, u32[]{:S(2)}) collective-permute-start(bf16[1024,256]{1,0:T(8,128)(2,1)} %query_ref.1), channel_id=1, source_target_pairs={{0,2},{1,3},{2,4},{3,5},{4,6},{5,7},{6,0},{7,1},{8,10},{9,11},{10,... | collective-permute-start | bytes 1572872 | tf_op jit(solution)/shard_map/ring1/ppermute | solution.py:294
  11.1 0.7 fusion.5
  11.9 2.8 %gather_fusion = f32[48,256]{1,0:T(8,128)S(1)} fusion(f32[4096,256]{1,0:T(8,128)} %table_ref.3, s32[1024]{0:T(1024)S(1)} %pad_clamp_fusion), kind=kCustom, calls=%fused_computation | custom fusion | bytes 98496 | tf_op jit(solution)/shard_map/gather | solution.py:304
  15.0 0.7 broadcast_in_dim.34
  15.7 3.6 %all-to-all-start.2 = ((bf16[8,48,384]{2,1,0:T(8,128)(2,1)}), bf16[8,48,384]{2,1,0:T(8,128)(2,1)S(1)}, u32[]{:S(2)}, u32[]{:S(2)}) async-start(bf16[8,48,384]{2,1,0:T(8,128)(2,1)} %broadcast_in_dim.34), calls=%async_computation.2 | async-start | bytes 589824 | tf_op jit(solution)/shard_map/negs_item/all_to_all | solution.py:264
  20.4 0.7 pad_add_fusion.3.refs_0_
  21.1 5.5 %collective-permute-done.1.refs_1_ = bf16[1024,256]{1,0:T(8,128)(2,1)} collective-permute-done((bf16[1024,256]{1,0:T(8,128)(2,1)}, bf16[1024,256]{1,0:T(8,128)(2,1)}, u32[]{:S(2)}, u32[]{:S(2)}) %collective-permute-start.1) | collective-permute-done | bytes 524320 | tf_op jit(solution)/shard_map/ring1/ppermute | solution.py:294
  27.8 15.6 %all-to-all-done.2 = bf16[8,48,384]{2,1,0:T(8,128)(2,1)S(1)} async-done(((bf16[8,48,384]{2,1,0:T(8,128)(2,1)}), bf16[8,48,384]{2,1,0:T(8,128)(2,1)S(1)}, u32[]{:S(2)}, u32[]{:S(2)}) %all-to-all-start.2) | async-done | bytes 294944 | tf_op jit(solution)/shard_map/negs_item/all_to_all | solution.py:264
  43.4 1.1 broadcast_in_dim.36
  44.5 3.7 %all-to-all-start.3 = ((bf16[4,384,384]{2,1,0:T(8,128)(2,1)}), bf16[4,384,384]{2,1,0:T(8,128)(2,1)S(1)}, u32[]{:S(2)}, u32[]{:S(2)}) async-start(bf16[4,384,384]{2,1,0:T(8,128)(2,1)} %broadcast_in_dim.36), calls=%async_computation.3 | async-start | bytes 2359296 | tf_op jit(solution)/shard_map/negs_dp/all_to_all | solution.py:264
  49.5 0.7 pad_add_fusion.6
  51.3 15.3 %route.1 = (bf16[3072,256]{1,0:T(8,128)(2,1)}, f32[8,1024]{1,0:T(8,128)}, f32[8,384]{1,0:T(8,128)}, f32[1,1024]{1,0:T(1,128)}) custom-call(s32[1]{0:T(128)} %bitcast.me_ref, s32[8,1024]{1,0:T(8,128)} %bitcast.63, s32[1,1024]{1,0:T(1,128)} %bitcast.65, f32[4096,256]{1,0:T(8,128)} %table_ref.3), custom_call_target="tpu_custom_call" | custom-call | flops 6442450944 | bytes 8388608 | tf_op jit(solution)/shard_map/route/pallas_call | solution.py:311
  66.5 0.7 collective-permute-done.5.refs_1_
  67.2 1.0 copy-done.3
  68.3 4.5 %all-to-all-start.1 = ((bf16[8,384,256]{2,1,0:T(8,128)(2,1)}), bf16[8,384,256]{2,1,0:T(8,128)(2,1)S(1)}, u32[]{:S(2)}, u32[]{:S(2)}) async-start(bf16[8,384,256]{2,1,0:T(8,128)(2,1)} %bitcast.52), calls=%async_computation.1 | async-start | bytes 3145728 | tf_op jit(solution)/shard_map/back/all_to_all | solution.py:361
  72.8 7.4 %owner0.1 = (bf16[768,256]{1,0:T(8,128)(2,1)}, f32[1,768]{1,0:T(1,128)}, f32[1536,256]{1,0:T(8,128)}, f32[1,1536]{1,0:T(1,128)}) custom-call(s32[4]{0:T(128)} %pad_add_fusion.3.refs_0_, bf16[1024,256]{1,0:T(8,128)(2,1)} %query_ref.1, bf16[1024,256]{1,0:T(8,128)(2,1)} %collective-permute-done.refs_2_, f32[8,1024]{1,0:T(8,128)} %get-tuple-element.31.refs_3_, ...), custom_call_target="tpu_custom_call" | custom-call | flops 1811939328 | bytes 3145728 | tf_op jit(solution)/shard_map/owner0/pallas_call | solution.py:330
  80.2 0.7 reduce
  81.0 0.7 reshape.71.refs_5_
  81.6 7.7 %owner1.1 = (bf16[768,256]{1,0:T(8,128)(2,1)}, f32[1,768]{1,0:T(1,128)}, f32[1536,256]{1,0:T(8,128)}) custom-call(s32[4]{0:T(128)} %pad_add_fusion.2.refs_0_, bf16[1024,256]{1,0:T(8,128)(2,1)} %collective-permute-done.1.refs_1_, bf16[1024,256]{1,0:T(8,128)(2,1)} %collective-permute-done.2.refs_2_, f32[8,1024]{1,0:T(8,128)} %get-tuple-element.31.refs_3_, ...), custom_call_target="tpu_custom_call" | custom-call | flops 1811939328 | bytes 3145728 | tf_op jit(solution)/shard_map/owner1/pallas_call | solution.py:330
  89.4 7.7 %owner2.1 = (bf16[768,256]{1,0:T(8,128)(2,1)}, f32[1,768]{1,0:T(1,128)}, f32[1536,256]{1,0:T(8,128)}) custom-call(s32[4]{0:T(128)} %pad_add_fusion.1.refs_0_, bf16[1024,256]{1,0:T(8,128)(2,1)} %collective-permute-done.3.refs_1_, bf16[1024,256]{1,0:T(8,128)(2,1)} %collective-permute-done.4.refs_2_, f32[8,1024]{1,0:T(8,128)} %get-tuple-element.31.refs_3_, ...), custom_call_target="tpu_custom_call" | custom-call | flops 1811939328 | bytes 3145728 | tf_op jit(solution)/shard_map/owner2/pallas_call | solution.py:330
  97.1 7.9 %owner3.1 = (bf16[768,256]{1,0:T(8,128)(2,1)}, f32[1,768]{1,0:T(1,128)}, f32[1536,256]{1,0:T(8,128)}) custom-call(s32[4]{0:T(128)} %pad_add_fusion.refs_0_, bf16[1024,256]{1,0:T(8,128)(2,1)} %collective-permute-done.5.refs_1_, bf16[1024,256]{1,0:T(8,128)(2,1)} %collective-permute-done.6.refs_2_, f32[8,1024]{1,0:T(8,128)} %get-tuple-element.31.refs_3_, ...), custom_call_target="tpu_custom_call" | custom-call | flops 1811939328 | bytes 3145728 | tf_op jit(solution)/shard_map/owner3/pallas_call | solution.py:330
  105.0 1.5 multiply_convert_fusion
  106.6 0.8 dynamic-slice_bitcast_fusion
  107.9 5.6 %give.1 = (bf16[1024,256]{1,0:T(8,128)(2,1)}, bf16[1024,256]{1,0:T(8,128)(2,1)}) custom-call(s32[2]{0:T(128)} %get-tuple-element.59.refs_0_, bf16[768,256]{1,0:T(8,128)(2,1)} %get-tuple-element.36.refs_1_, bf16[768,256]{1,0:T(8,128)(2,1)} %get-tuple-element.38.refs_2_, bf16[768,256]{1,0:T(8,128)(2,1)} %get-tuple-element.40.refs_3_, ...), custom_call_target="tpu_custom_call" | custom-call | flops 3221225472 | bytes 1048576 | tf_op jit(solution)/shard_map/give/pallas_call | solution.py:371
  113.4 2.0 %collective-permute-start.7 = (bf16[1024,256]{1,0:T(8,128)(2,1)}, bf16[1024,256]{1,0:T(8,128)(2,1)S(1)}, u32[]{:S(2)}, u32[]{:S(2)}) collective-permute-start(bf16[1024,256]{1,0:T(8,128)(2,1)} %get-tuple-element.48), channel_id=1, source_target_pairs={{0,8},{8,0},{16,24},{24,16},{1,9},{9,1},{17,25},{25,17},{2,10},{10... | collective-permute-start | bytes 1572872 | tf_op jit(solution)/shard_map/halve0/ppermute | solution.py:386
  115.5 5.6 %keep.1 = (bf16[1024,256]{1,0:T(8,128)(2,1)}, bf16[1024,256]{1,0:T(8,128)(2,1)}) custom-call(s32[2]{0:T(128)} %get-tuple-element.58.refs_0_, bf16[768,256]{1,0:T(8,128)(2,1)} %get-tuple-element.36.refs_1_, bf16[768,256]{1,0:T(8,128)(2,1)} %get-tuple-element.38.refs_2_, bf16[768,256]{1,0:T(8,128)(2,1)} %get-tuple-element.40.refs_3_, ...), custom_call_target="tpu_custom_call" | custom-call | flops 3221225472 | bytes 1048576 | tf_op jit(solution)/shard_map/keep/pallas_call | solution.py:371
  121.1 1.5 collective-permute-start.11
  122.7 1.7 collective-permute-start.16
  124.4 3.3 %collective-permute-done.7 = bf16[1024,256]{1,0:T(8,128)(2,1)S(1)} collective-permute-done((bf16[1024,256]{1,0:T(8,128)(2,1)}, bf16[1024,256]{1,0:T(8,128)(2,1)S(1)}, u32[]{:S(2)}, u32[]{:S(2)}) %collective-permute-start.7) | collective-permute-done | bytes 524320 | tf_op jit(solution)/shard_map/halve0/ppermute | solution.py:386
  127.9 1.8 collective-permute-start.8
  129.7 6.4 %collective-permute-done.11 = bf16[1024,256]{1,0:T(8,128)(2,1)S(1)} collective-permute-done((bf16[1024,256]{1,0:T(8,128)(2,1)}, bf16[1024,256]{1,0:T(8,128)(2,1)S(1)}, u32[]{:S(2)}, u32[]{:S(2)}) %collective-permute-start.11) | collective-permute-done | bytes 524320 | tf_op jit(solution)/shard_map/halve1/ppermute | solution.py:386
  136.4 2.6 %collective-permute-start.17 = (bf16[4,1,48,256]{3,2,1,0:T(8,128)(2,1)S(1)}, bf16[4,1,48,256]{3,2,1,0:T(8,128)(2,1)S(1)}, u32[]{:S(2)}, u32[]{:S(2)}) collective-permute-start(bf16[4,1,48,256]{3,2,1,0:T(8,128)(2,1)S(1)} %constant_dynamic-slice_fusion.1), channel_id=1, source_target_pairs={{0,4},{1,5},{2,6},{3,7},{4,0},{5,1},{6,2},{7,3},{8,12},{9,13},{10,... | collective-permute-start | bytes 294920 | tf_op jit(solution)/shard_map/ppermute | solution.py:406
  139.1 2.9 %collective-permute-done.17 = bf16[4,1,48,256]{3,2,1,0:T(8,128)(2,1)S(1)} collective-permute-done((bf16[4,1,48,256]{3,2,1,0:T(8,128)(2,1)S(1)}, bf16[4,1,48,256]{3,2,1,0:T(8,128)(2,1)S(1)}, u32[]{:S(2)}, u32[]{:S(2)}) %collective-permute-start.17) | collective-permute-done | bytes 98336 | tf_op jit(solution)/shard_map/ppermute | solution.py:406
  142.0 1.2 collective-permute-start.18
  143.3 0.9 collective-permute-start.9
  144.2 3.5 %collective-permute-done.12 = bf16[512,256]{1,0:T(8,128)(2,1)S(1)} collective-permute-done((bf16[512,256]{1,0:T(8,128)(2,1)S(1)}, bf16[512,256]{1,0:T(8,128)(2,1)S(1)}, u32[]{:S(2)}, u32[]{:S(2)}) %collective-permute-start.12) | collective-permute-done | bytes 262176 | tf_op jit(solution)/shard_map/ppermute | solution.py:251
  147.9 2.0 %collective-permute-done.18 = bf16[192,256]{1,0:T(8,128)(2,1)S(1)} collective-permute-done((bf16[192,256]{1,0:T(8,128)(2,1)S(1)}, bf16[192,256]{1,0:T(8,128)(2,1)S(1)}, u32[]{:S(2)}, u32[]{:S(2)}) %collective-permute-start.18) | collective-permute-done | bytes 98336 | tf_op jit(solution)/shard_map/ppermute | solution.py:409
  149.9 1.5 collective-permute-start.19
  152.3 4.8 %collective-permute-done.13 = bf16[512,256]{1,0:T(8,128)(2,1)S(1)} collective-permute-done((bf16[512,256]{1,0:T(8,128)(2,1)S(1)}, bf16[512,256]{1,0:T(8,128)(2,1)S(1)}, u32[]{:S(2)}, u32[]{:S(2)}) %collective-permute-start.13) | collective-permute-done | bytes 262176 | tf_op jit(solution)/shard_map/ppermute | solution.py:256
  157.3 1.5 collective-permute-start.14
  158.8 1.1 copy-done.2
  160.0 10.4 %home.1 = (bf16[1024,256]{1,0:T(8,128)(2,1)}, f32[1,1024]{1,0:T(1,128)}) custom-call(s32[2]{0:T(128)} %pad_add_fusion.4.me_ref, bf16[1024,256]{1,0:T(8,128)(2,1)} %query_ref.1, f32[1,1024]{1,0:T(1,128)} %get-tuple-element.29.place_ref, s32[1,1024]{1,0:T(1,128)} %bitcast.66, bf16[3072,256]{1,0:T(8,128)(2,1)} %bitcast.53, bf16[1536,384]{1,0:T(8,128)(2,1)} %bitcast.60, ...), custom_call_target="tpu_custom_call" | custom-call | flops 4831838208 | bytes 3145728 | tf_op jit(solution)/shard_map/home/pallas_call | solution.py:443
  170.4 0.7 add_convert_fusion.4.refs_4_
  171.1 0.8 copy-done.6
  171.9 12.2 %update.1 = (f32[4096,256]{1,0:T(8,128)}, f32[1,4096]{1,0:T(1,128)}) custom-call(s32[4]{0:T(128)} %pad_add_fusion.5.start_ref, f32[4096,256]{1,0:T(8,128)} %table_ref.3, f32[1,4096]{1,0:T(1,128)} %bitcast.64, bf16[1024,256]{1,0:T(8,128)(2,1)} %copy-done, bf16[1024,256]{1,0:T(8,128)(2,1)} %copy-done.6, bf16[1024,256]{1,0:T(8,128)(2,1)} %copy-done.1, ...), custom_call_target="tpu_custom_call" | custom-call | flops 8388608 | bytes 10485760 | tf_op jit(solution)/shard_map/update/pallas_call | solution.py:415
  (71 shorter events, 8.2 us)
Async XLA Ops:
  0.6 18.7 %copy-start.8 = (bf16[1024,256]{1,0:T(8,128)(2,1)S(1)}, bf16[1024,256]{1,0:T(8,128)(2,1)}, u32[]{:S(2)}) copy-start(bf16[1024,256]{1,0:T(8,128)(2,1)} %query_ref.1) | copy-start | bytes 1572868
  2.1 42.5 %copy-start.7 = (s32[1024]{0:T(1024)}, s32[1024]{0:T(1024)S(1)}, u32[]{:S(2)}) copy-start(s32[1024]{0:T(1024)S(1)} %add.145) | copy-start | bytes 12292
  2.7 12.3 %all-to-all-start = ((s32[8,1,1024]{2,1,0:T(1,128)}), s32[8,1,1024]{2,1,0:T(1,128)S(1)}, u32[]{:S(2)}, u32[]{:S(2)}) async-start(s32[8,1,1024]{2,1,0:T(1,128)} %broadcast_in_dim.14), calls=%async_computation | async-start | bytes 65536 | tf_op jit(solution)/shard_map/gids/all_to_all | solution.py:264
  9.1 17.5 %collective-permute-start.1 = (bf16[1024,256]{1,0:T(8,128)(2,1)}, bf16[1024,256]{1,0:T(8,128)(2,1)}, u32[]{:S(2)}, u32[]{:S(2)}) collective-permute-start(bf16[1024,256]{1,0:T(8,128)(2,1)} %query_ref.1), channel_id=1, source_target_pairs={{0,2},{1,3},{2,4},{3,5},{4,6},{5,7},{6,0},{7,1},{8,10},{9,11},{10,... | collective-permute-start | bytes 1572872 | tf_op jit(solution)/shard_map/ring1/ppermute | solution.py:294
  15.7 27.7 %all-to-all-start.2 = ((bf16[8,48,384]{2,1,0:T(8,128)(2,1)}), bf16[8,48,384]{2,1,0:T(8,128)(2,1)S(1)}, u32[]{:S(2)}, u32[]{:S(2)}) async-start(bf16[8,48,384]{2,1,0:T(8,128)(2,1)} %broadcast_in_dim.34), calls=%async_computation.2 | async-start | bytes 589824 | tf_op jit(solution)/shard_map/negs_item/all_to_all | solution.py:264
  19.3 53.5 %collective-permute-start = (bf16[1024,256]{1,0:T(8,128)(2,1)S(1)}, bf16[1024,256]{1,0:T(8,128)(2,1)}, u32[]{:S(2)}, u32[]{:S(2)}) collective-permute-start(bf16[1024,256]{1,0:T(8,128)(2,1)S(1)} %copy-done.8), channel_id=1, source_target_pairs={{0,1},{1,0},{2,3},{3,2},{4,5},{5,4},{6,7},{7,6},{8,9},{9,8},{10,11... | collective-permute-start | bytes 1572872 | tf_op jit(solution)/shard_map/pair0/ppermute | solution.py:296
  26.6 24.2 %collective-permute-start.3 = (bf16[1024,256]{1,0:T(8,128)(2,1)}, bf16[1024,256]{1,0:T(8,128)(2,1)}, u32[]{:S(2)}, u32[]{:S(2)}) collective-permute-start(bf16[1024,256]{1,0:T(8,128)(2,1)} %collective-permute-done.1.refs_1_), channel_id=1, source_target_pairs={{0,2},{1,3},{2,4},{3,5},{4,6},{5,7},{6,0},{7,1},{8,10},{9,11},{10,... | collective-permute-start | bytes 1572872 | tf_op jit(solution)/shard_map/ring2/ppermute | solution.py:294
  44.5 22.7 %all-to-all-start.3 = ((bf16[4,384,384]{2,1,0:T(8,128)(2,1)}), bf16[4,384,384]{2,1,0:T(8,128)(2,1)S(1)}, u32[]{:S(2)}, u32[]{:S(2)}) async-start(bf16[4,384,384]{2,1,0:T(8,128)(2,1)} %broadcast_in_dim.36), calls=%async_computation.3 | async-start | bytes 2359296 | tf_op jit(solution)/shard_map/negs_dp/all_to_all | solution.py:264
  50.7 30.9 %collective-permute-start.2 = (bf16[1024,256]{1,0:T(8,128)(2,1)}, bf16[1024,256]{1,0:T(8,128)(2,1)}, u32[]{:S(2)}, u32[]{:S(2)}) collective-permute-start(bf16[1024,256]{1,0:T(8,128)(2,1)} %collective-permute-done.1.refs_1_), channel_id=1, source_target_pairs={{0,1},{1,0},{2,3},{3,2},{4,5},{5,4},{6,7},{7,6},{8,9},{9,8},{10,11... | collective-permute-start | bytes 1572872 | tf_op jit(solution)/shard_map/pair1/ppermute | solution.py:296
  50.8 38.6 %collective-permute-start.4 = (bf16[1024,256]{1,0:T(8,128)(2,1)}, bf16[1024,256]{1,0:T(8,128)(2,1)}, u32[]{:S(2)}, u32[]{:S(2)}) collective-permute-start(bf16[1024,256]{1,0:T(8,128)(2,1)} %collective-permute-done.3.refs_1_), channel_id=1, source_target_pairs={{0,1},{1,0},{2,3},{3,2},{4,5},{5,4},{6,7},{7,6},{8,9},{9,8},{10,11... | collective-permute-start | bytes 1572872 | tf_op jit(solution)/shard_map/pair2/ppermute | solution.py:296
  51.3 15.9 %collective-permute-start.5 = (bf16[1024,256]{1,0:T(8,128)(2,1)}, bf16[1024,256]{1,0:T(8,128)(2,1)}, u32[]{:S(2)}, u32[]{:S(2)}) collective-permute-start(bf16[1024,256]{1,0:T(8,128)(2,1)} %collective-permute-done.3.refs_1_), channel_id=1, source_target_pairs={{0,2},{1,3},{2,4},{3,5},{4,6},{5,7},{6,0},{7,1},{8,10},{9,11},{10,... | collective-permute-start | bytes 1572872 | tf_op jit(solution)/shard_map/ring3/ppermute | solution.py:294
  67.2 29.9 %collective-permute-start.6 = (bf16[1024,256]{1,0:T(8,128)(2,1)}, bf16[1024,256]{1,0:T(8,128)(2,1)}, u32[]{:S(2)}, u32[]{:S(2)}) collective-permute-start(bf16[1024,256]{1,0:T(8,128)(2,1)} %collective-permute-done.5.refs_1_), channel_id=1, source_target_pairs={{0,1},{1,0},{2,3},{3,2},{4,5},{5,4},{6,7},{7,6},{8,9},{9,8},{10,11... | collective-permute-start | bytes 1572872 | tf_op jit(solution)/shard_map/pair3/ppermute | solution.py:296
  67.2 1.0 copy-start.3
  68.3 90.6 %all-to-all-start.1 = ((bf16[8,384,256]{2,1,0:T(8,128)(2,1)}), bf16[8,384,256]{2,1,0:T(8,128)(2,1)S(1)}, u32[]{:S(2)}, u32[]{:S(2)}) async-start(bf16[8,384,256]{2,1,0:T(8,128)(2,1)} %bitcast.52), calls=%async_computation.1 | async-start | bytes 3145728 | tf_op jit(solution)/shard_map/back/all_to_all | solution.py:361
  107.4 15.2 %collective-permute-start.15 = (bf16[4,4,48,256]{3,2,1,0:T(8,128)(2,1)}, bf16[4,4,48,256]{3,2,1,0:T(8,128)(2,1)S(1)}, u32[]{:S(2)}, u32[]{:S(2)}) collective-permute-start(bf16[4,4,48,256]{3,2,1,0:T(8,128)(2,1)} %dynamic-slice_bitcast_fusion), channel_id=1, source_target_pairs={{0,1},{1,0},{2,3},{3,2},{4,5},{5,4},{6,7},{7,6},{8,9},{9,8},{10,11... | collective-permute-start | bytes 1179656 | tf_op jit(solution)/shard_map/ppermute | solution.py:406
  113.4 14.3 %collective-permute-start.7 = (bf16[1024,256]{1,0:T(8,128)(2,1)}, bf16[1024,256]{1,0:T(8,128)(2,1)S(1)}, u32[]{:S(2)}, u32[]{:S(2)}) collective-permute-start(bf16[1024,256]{1,0:T(8,128)(2,1)} %get-tuple-element.48), channel_id=1, source_target_pairs={{0,8},{8,0},{16,24},{24,16},{1,9},{9,1},{17,25},{25,17},{2,10},{10... | collective-permute-start | bytes 1572872 | tf_op jit(solution)/shard_map/halve0/ppermute | solution.py:386
  121.1 6.7 %copy-start.5 = (bf16[1024,256]{1,0:T(8,128)(2,1)S(1)}, bf16[1024,256]{1,0:T(8,128)(2,1)}, u32[]{:S(2)}) copy-start(bf16[1024,256]{1,0:T(8,128)(2,1)} %get-tuple-element.47) | copy-start | bytes 1572868
  121.1 15.1 %copy-start.4 = (bf16[1024,256]{1,0:T(8,128)(2,1)S(1)}, bf16[1024,256]{1,0:T(8,128)(2,1)}, u32[]{:S(2)}) copy-start(bf16[1024,256]{1,0:T(8,128)(2,1)} %get-tuple-element.49) | copy-start | bytes 1572868
  121.1 15.1 %collective-permute-start.11 = (bf16[1024,256]{1,0:T(8,128)(2,1)}, bf16[1024,256]{1,0:T(8,128)(2,1)S(1)}, u32[]{:S(2)}, u32[]{:S(2)}) collective-permute-start(bf16[1024,256]{1,0:T(8,128)(2,1)} %get-tuple-element.50), channel_id=1, source_target_pairs={{0,16},{8,24},{16,0},{24,8},{1,17},{9,25},{17,1},{25,9},{2,18},{10... | collective-permute-start | bytes 1572872 | tf_op jit(solution)/shard_map/halve1/ppermute | solution.py:386
  122.7 13.5 %collective-permute-start.16 = (bf16[4,2,48,256]{3,2,1,0:T(8,128)(2,1)S(1)}, bf16[4,2,48,256]{3,2,1,0:T(8,128)(2,1)S(1)}, u32[]{:S(2)}, u32[]{:S(2)}) collective-permute-start(bf16[4,2,48,256]{3,2,1,0:T(8,128)(2,1)S(1)} %dynamic-slice_bitcast_fusion.1), channel_id=1, source_target_pairs={{0,2},{1,3},{2,0},{3,1},{4,6},{5,7},{6,4},{7,5},{8,10},{9,11},{10,... | collective-permute-start | bytes 589832 | tf_op jit(solution)/shard_map/ppermute | solution.py:406
  127.9 15.3 %collective-permute-start.8 = (bf16[512,256]{1,0:T(8,128)(2,1)S(1)}, bf16[512,256]{1,0:T(8,128)(2,1)S(1)}, u32[]{:S(2)}, u32[]{:S(2)}) collective-permute-start(bf16[512,256]{1,0:T(8,128)(2,1)S(1)} %constant_dynamic-slice_fusion.3), channel_id=1, source_target_pairs={{0,16},{8,24},{16,0},{24,8},{1,17},{9,25},{17,1},{25,9},{2,18},{10... | collective-permute-start | bytes 786440 | tf_op jit(solution)/shard_map/ppermute | solution.py:251
  136.4 5.6 %collective-permute-start.17 = (bf16[4,1,48,256]{3,2,1,0:T(8,128)(2,1)S(1)}, bf16[4,1,48,256]{3,2,1,0:T(8,128)(2,1)S(1)}, u32[]{:S(2)}, u32[]{:S(2)}) collective-permute-start(bf16[4,1,48,256]{3,2,1,0:T(8,128)(2,1)S(1)} %constant_dynamic-slice_fusion.1), channel_id=1, source_target_pairs={{0,4},{1,5},{2,6},{3,7},{4,0},{5,1},{6,2},{7,3},{8,12},{9,13},{10,... | collective-permute-start | bytes 294920 | tf_op jit(solution)/shard_map/ppermute | solution.py:406
  139.0 8.7 %collective-permute-start.12 = (bf16[512,256]{1,0:T(8,128)(2,1)S(1)}, bf16[512,256]{1,0:T(8,128)(2,1)S(1)}, u32[]{:S(2)}, u32[]{:S(2)}) collective-permute-start(bf16[512,256]{1,0:T(8,128)(2,1)S(1)} %constant_dynamic-slice_fusion.2), channel_id=1, source_target_pairs={{0,8},{8,0},{16,24},{24,16},{1,9},{9,1},{17,25},{25,17},{2,10},{10... | collective-permute-start | bytes 786440 | tf_op jit(solution)/shard_map/ppermute | solution.py:251
  142.0 7.8 %collective-permute-start.18 = (bf16[192,256]{1,0:T(8,128)(2,1)S(1)}, bf16[192,256]{1,0:T(8,128)(2,1)S(1)}, u32[]{:S(2)}, u32[]{:S(2)}) collective-permute-start(bf16[192,256]{1,0:T(8,128)(2,1)S(1)} %bitcast.62), channel_id=1, source_target_pairs={{0,8},{8,0},{16,24},{24,16},{1,9},{9,1},{17,25},{25,17},{2,10},{10... | collective-permute-start | bytes 294920 | tf_op jit(solution)/shard_map/ppermute | solution.py:409
  143.3 8.1 %collective-permute-start.9 = (bf16[512,256]{1,0:T(8,128)(2,1)S(1)}, bf16[512,256]{1,0:T(8,128)(2,1)S(1)}, u32[]{:S(2)}, u32[]{:S(2)}) collective-permute-start(bf16[512,256]{1,0:T(8,128)(2,1)S(1)} %add_convert_fusion.3), channel_id=1, source_target_pairs={{0,16},{8,24},{16,0},{24,8},{1,17},{9,25},{17,1},{25,9},{2,18},{10... | collective-permute-start | bytes 786440 | tf_op jit(solution)/shard_map/ppermute | solution.py:256
  147.8 9.2 %collective-permute-start.13 = (bf16[512,256]{1,0:T(8,128)(2,1)S(1)}, bf16[512,256]{1,0:T(8,128)(2,1)S(1)}, u32[]{:S(2)}, u32[]{:S(2)}) collective-permute-start(bf16[512,256]{1,0:T(8,128)(2,1)S(1)} %add_convert_fusion.2), channel_id=1, source_target_pairs={{0,8},{8,0},{16,24},{24,16},{1,9},{9,1},{17,25},{25,17},{2,10},{10... | collective-permute-start | bytes 786440 | tf_op jit(solution)/shard_map/ppermute | solution.py:256
  149.9 20.6 %collective-permute-start.19 = (bf16[192,256]{1,0:T(8,128)(2,1)S(1)}, bf16[192,256]{1,0:T(8,128)(2,1)S(1)}, u32[]{:S(2)}, u32[]{:S(2)}) collective-permute-start(bf16[192,256]{1,0:T(8,128)(2,1)S(1)} %add_convert_fusion.5), channel_id=1, source_target_pairs={{0,16},{8,24},{16,0},{24,8},{1,17},{9,25},{17,1},{25,9},{2,18},{10... | collective-permute-start | bytes 294920 | tf_op jit(solution)/shard_map/ppermute | solution.py:409
  151.6 18.8 %copy-start = (bf16[1024,256]{1,0:T(8,128)(2,1)}, bf16[1024,256]{1,0:T(8,128)(2,1)S(1)}, u32[]{:S(2)}) copy-start(bf16[1024,256]{1,0:T(8,128)(2,1)S(1)} %maximum_select_fusion.refs_0_) | copy-start | bytes 1572868
  151.6 19.4 %collective-permute-start.10 = (bf16[1024,256]{1,0:T(8,128)(2,1)S(1)}, bf16[1024,256]{1,0:T(8,128)(2,1)S(1)}, u32[]{:S(2)}, u32[]{:S(2)}) collective-permute-start(bf16[1024,256]{1,0:T(8,128)(2,1)S(1)} %maximum_select_fusion.refs_0_), channel_id=1, source_target_pairs={{0,8},{8,0},{16,24},{24,16},{1,9},{9,1},{17,25},{25,17},{2,10},{10... | collective-permute-start | bytes 1572872 | tf_op jit(solution)/shard_map/ppermute | solution.py:396
  157.3 13.1 %copy-start.1 = (bf16[1024,256]{1,0:T(8,128)(2,1)}, bf16[1024,256]{1,0:T(8,128)(2,1)S(1)}, u32[]{:S(2)}) copy-start(bf16[1024,256]{1,0:T(8,128)(2,1)S(1)} %maximum_select_fusion.1.refs_2_) | copy-start | bytes 1572868
  157.3 13.8 %collective-permute-start.14 = (bf16[1024,256]{1,0:T(8,128)(2,1)S(1)}, bf16[1024,256]{1,0:T(8,128)(2,1)}, u32[]{:S(2)}, u32[]{:S(2)}) collective-permute-start(bf16[1024,256]{1,0:T(8,128)(2,1)S(1)} %maximum_select_fusion.1.refs_2_), channel_id=1, source_target_pairs={{0,16},{8,24},{16,0},{24,8},{1,17},{9,25},{17,1},{25,9},{2,18},{10... | collective-permute-start | bytes 1572872 | tf_op jit(solution)/shard_map/ppermute | solution.py:396
  158.8 1.1 copy-start.2
  171.1 0.8 copy-start.6

commit v3 on v2

v3 whole, which is shorter than its diff:
```python
import math

import jax
import jax.numpy as jnp
from jax import lax
from jax.experimental import pallas as pl
from jax.experimental.pallas import tpu as pltpu
from jax.sharding import PartitionSpec as P

INV_TEMP = 20.0
LEARN_RATE = 0.05
EPSILON = 1e-06
LOG2_E = math.log2(math.e)
F32 = jnp.float32
BF16 = jnp.bfloat16
NT = (((1,), (1,)), ((), ()))


def unit_rows(matrix):
    back_norm = 1.0 / jnp.sqrt(jnp.sum(matrix * matrix, axis=-1, keepdims=True) + EPSILON)
    return (matrix * back_norm, back_norm)


def iota(shape, axis):
    return lax.broadcasted_iota(jnp.int32, shape, axis).astype(F32)


def to_sub(row):
    return jnp.transpose(jnp.broadcast_to(row, (8, row.shape[1])))[:, :1]


def to_lane(col):
    return jnp.transpose(jnp.broadcast_to(col, (col.shape[0], 128)))[:1, :]


def one_hot(test):
    return jnp.where(test, 1.0, 0.0).astype(BF16)


def earlier_count(mask):
    total, step = mask, 1
    lane = lax.broadcasted_iota(jnp.int32, mask.shape, 1)
    while step < mask.shape[1]:
        total = total + jnp.where(lane >= step, pltpu.roll(total, step, axis=1), 0.0)
        step *= 2
    return total - mask


def rows_at(start, size):
    return pl.ds(pl.multiple_of(start * size, size), size)


def route_kernel(gid_ref, own_ref, rows_ref, rank_ref, rid_ref, place_ref):
    blocks, examples = gid_ref.shape
    slots = rid_ref.shape[1]
    table_rows = rows_ref[0]
    local = gid_ref[...] - lax.axis_index("item") * table_rows
    mine = jnp.logical_and(local >= 0, local < table_rows)
    rank = earlier_count(jnp.where(mine, 1.0, 0.0))
    rank_ref[...] = jnp.where(mine, rank, -1.0)
    local = local.astype(F32)

    owner = lax.broadcasted_iota(jnp.int32, (blocks, examples), 0)
    own = own_ref[...]
    named = jnp.logical_and(own >= owner * table_rows, own < (owner + 1) * table_rows)
    count = earlier_count(jnp.where(named, 1.0, 0.0))
    spot = jnp.where(named, count + owner.astype(F32) * slots, 0.0)
    place_ref[...] = jnp.sum(spot, axis=0, keepdims=True)

    for block in range(blocks):
        chosen = iota((slots, examples), 0) == rank_ref[block : block + 1, :]
        wanted = jnp.sum(
            jnp.where(chosen, local[block : block + 1, :], 0.0), axis=1, keepdims=True
        )
        rid_ref[block : block + 1, :] = to_lane(wanted).astype(jnp.int32)


def norm_kernel(table_ref, send_ref):
    send_ref[...] = unit_rows(table_ref[...])[0].astype(BF16)


def find_kernel(start, rid_ref, send_ref, *refs):
    found_ref = refs[-1]
    table_rows = send_ref.shape[0]
    first = 2 * (start + pl.program_id(0))
    ids = [to_sub(rid_ref[pl.ds(first + core, 1), :].astype(F32)) for core in range(2)]
    pick = one_hot(jnp.concatenate(ids, axis=0) == iota((1, table_rows), 1))
    found_ref[...] = jnp.dot(pick, send_ref[...], preferred_element_type=F32).astype(BF16)


def neg_ids(part):
    digits = part.astype(F32)
    return digits[:, :1] * 4096.0 + digits[:, 1:2] * 64.0 + digits[:, 2:3]


def ring_source(spot, items):
    item = lax.axis_index("item")
    return lax.rem((item ^ (spot % 2)) - 2 * (spot // 2) + items, items)


def owner_kernel(table_rows, *refs):
    pairs, groups = lax.axis_size("item") // 2, lax.axis_size("dp")
    queries, refs = refs[: 2 * pairs], refs[2 * pairs :]
    columns, refs = refs[:groups], refs[groups:]
    rank_ref, rid_ref, found_any, refs = *refs[:3], refs[3:]
    pull_ref, outrid_ref, part_ref, ids_ref, negs_ref, refs = *refs[:5], refs[5:]
    held, found, nsub, exps, neg_ref, copy_sem = refs
    slots = rid_ref.shape[1]
    examples, width = held.shape[1], held.shape[2]
    negs = negs_ref.shape[0]
    chunk = math.gcd(negs, 256)
    both = 2 * slots
    size = negs // groups
    copies = [
        pltpu.make_async_copy(
            column,
            negs_ref.at[rows_at(lax.axis_index("dp") ^ other, size)],
            copy_sem.at[4 * pairs + other],
        )
        for other, column in enumerate(columns)
    ]
    for spot, query in enumerate(queries):
        source = rows_at(ring_source(spot, 2 * pairs), slots)
        there = found.at[spot * slots : (spot + 1) * slots]
        copies.append(
            pltpu.make_async_copy(query, held.at[spot], copy_sem.at[2 * spot + 1])
        )
        copies.append(
            pltpu.make_async_copy(found_any.at[source], there, copy_sem.at[2 * spot])
        )
    for copy in copies:
        copy.start()
    base = (lax.axis_index("item") * table_rows).astype(F32)
    for spot in range(2 * pairs):
        part = slice(spot * slots, (spot + 1) * slots)
        rid = rid_ref[pl.ds(ring_source(spot, 2 * pairs), 1), :]
        outrid_ref[:, part] = rid.astype(F32)
    for copy in copies:
        copy.wait()
    nsub[...] = jnp.broadcast_to(neg_ids(negs_ref[:, width:]) - base, nsub.shape)
    ids_ref[...] = jnp.transpose(nsub[...])[:1, :]

    def one_pair(pair, fresh):
        rid = outrid_ref[:, rows_at(pair, both)]
        picked = []
        for core in range(2):
            rank = rank_ref[pl.ds(ring_source(2 * pair + core, 2 * pairs), 1), :]
            pick = one_hot(iota((slots, examples), 0) == rank)
            picked.append(jnp.dot(pick, held[2 * pair + core], preferred_element_type=F32))
        query_hat, _ = unit_rows(jnp.concatenate(picked, axis=0))
        query_send = query_hat.astype(BF16)
        pos_e = found[rows_at(pair, both), :].astype(F32)
        s_pos = jnp.sum(query_send.astype(F32) * pos_e, axis=1, keepdims=True)
        pos_exp = to_lane(jnp.exp(INV_TEMP * s_pos))
        total = pos_exp
        for step in range(negs // chunk):
            part = pl.ds(step * chunk, chunk)
            scores = lax.dot_general(
                negs_ref[part, :width], query_send, NT, preferred_element_type=F32
            )
            keep = nsub[part, :][:, :1] != rid
            some = jnp.where(keep, jnp.exp2(scores * (INV_TEMP * LOG2_E)), 0.0)
            exps[part, :] = some.astype(BF16)
            total = total + jnp.sum(some, axis=0, keepdims=True)
        scale = 1.0 / total
        scaled = (query_send.astype(F32) * to_sub(scale)).astype(BF16)
        for step in range(negs // chunk):
            part = pl.ds(step * chunk, chunk)
            more = jnp.dot(exps[part, :], scaled, preferred_element_type=F32)
            if fresh:
                neg_ref[part, :] = more
            else:
                neg_ref[part, :] += more
        p_pos = to_sub(pos_exp * scale)
        pull = (INV_TEMP * (p_pos - 1.0) * query_hat).astype(BF16)
        pull_ref[rows_at(pair, both), :] = pull

    one_pair(0, True)
    if pairs > 1:

        def more_pairs(pair, carry):
            one_pair(pair, False)
            return carry

        lax.fori_loop(1, pairs, more_pairs, 0)
    part_ref[...] = (INV_TEMP * neg_ref[...]).astype(BF16)


def scatter_kernel(keep, bits, pull_ref, rid_ref, *outs):
    ids = rid_ref[...]
    for side, out_ref in enumerate(outs):
        quarter = out_ref.shape[0]
        rows = math.gcd(quarter, 512)
        mine = (lax.axis_index("dp") >> bits[side]) & 1
        start = (2 * side + (mine if keep else 1 - mine)) * quarter
        for step in range(out_ref.shape[0] // rows):
            offset = (start + step * rows).astype(F32)
            put = one_hot(iota((rows, ids.shape[1]), 0) == ids - offset)
            part = jnp.dot(put, pull_ref[...], preferred_element_type=F32)
            out_ref[step * rows : (step + 1) * rows, :] = part.astype(BF16)


def home_kernel(table_rows, query_ref, place_ref, gid_ref, back_ref, negs_ref, ids_ref, *refs):
    grad_ref, loss_ref = refs[-2:]
    examples, width = query_ref.shape
    spots = back_ref.shape[0]
    pick = one_hot(iota((examples, spots), 1) == to_sub(place_ref[...]))
    pos_e = jnp.dot(pick, back_ref[...], preferred_element_type=F32)
    query_hat, back_norm = unit_rows(query_ref[...].astype(F32))
    query_send = query_hat.astype(BF16)
    s_pos = INV_TEMP * jnp.sum(query_send.astype(F32) * pos_e, axis=1, keepdims=True)
    pos_exp = jnp.exp(s_pos)
    negs = negs_ref[:, :width]
    scores = lax.dot_general(query_send, negs, NT, preferred_element_type=F32)
    local = (gid_ref[...] - lax.axis_index("item") * table_rows).astype(F32)
    keep = ids_ref[...] != to_sub(local)
    part = jnp.where(keep, jnp.exp2(scores * (INV_TEMP * LOG2_E)), 0.0)
    total = pos_exp + jnp.sum(part, axis=1, keepdims=True)
    scale = 1.0 / total
    loss_ref[...] = to_lane(jnp.log(total) - s_pos)
    probs = (part * scale).astype(BF16)
    g_query = INV_TEMP * (
        (pos_exp * scale - 1.0) * pos_e + jnp.dot(probs, negs, preferred_element_type=F32)
    )
    along = jnp.sum(query_hat * g_query, axis=1, keepdims=True)
    grad_ref[...] = ((g_query - query_hat * along) * back_norm).astype(BF16)


def update_kernel(rest, start_ref, table_ref, state_ref, *refs):
    low_ref, high_ref, neg_ref, row_ref = refs[:4]
    new_ref, new_state_ref = refs[-2:]
    rows = table_ref.shape[0]
    step = pl.program_id(0)
    half = pl.num_programs(0) // 2
    offset = (update_block(rest, step, start_ref, half) * rows).astype(F32)
    put = one_hot(iota((rows, row_ref.shape[1]), 0) == row_ref[...] - offset)
    pull = jnp.where(step < half, low_ref[...].astype(F32), high_ref[...].astype(F32))
    g_unit = pull + jnp.dot(put, neg_ref[...], preferred_element_type=F32)
    table = table_ref[...]
    unit, back_norm = unit_rows(table)
    g_row = (g_unit - unit * jnp.sum(unit * g_unit, axis=1, keepdims=True)) * back_norm
    state = to_sub(state_ref[...]) + jnp.mean(g_row * g_row, axis=1, keepdims=True)
    new_state_ref[...] = to_lane(state)
    new_ref[...] = table - g_row * (LEARN_RATE * lax.rsqrt(state))


def update_block(rest, step, start_ref, half):
    low, high = start_ref[2 * rest], start_ref[2 * rest + 1]
    return jnp.where(step < half, low + step, high + step - half)


def whole():
    return pl.BlockSpec(memory_space=pltpu.VMEM)


def flip(count, bit):
    return [(index, index ^ (1 << bit)) for index in range(count)]


def add(left, right):
    return (left.astype(F32) + right.astype(F32)).astype(BF16)


def halve(value, name, count, bit):
    half = value.shape[0] // 2
    mine = (lax.axis_index(name) >> bit) & 1
    give = lax.dynamic_slice_in_dim(value, (1 - mine) * half, half, 0)
    keep = lax.dynamic_slice_in_dim(value, mine * half, half, 0)
    return add(keep, lax.ppermute(give, name, flip(count, bit)))


def double(value, name, count, bit):
    mine = (lax.axis_index(name) >> bit) & 1
    got = lax.ppermute(value, name, flip(count, bit))
    low = jnp.concatenate([value, got], axis=0)
    high = jnp.concatenate([got, value], axis=0)
    return jnp.where(mine == 0, low, high)


def to_digits(values, axis):
    digits = [values // 4096, values // 64 % 64, values % 64]
    return jnp.concatenate(digits, axis=axis).astype(BF16)


def to_all(value, name, count):
    copies = jnp.broadcast_to(value[None], (count, *value.shape))
    return lax.all_to_all(copies, name, split_axis=0, concat_axis=0, tiled=True)


def cost(flops, traffic):
    return pl.CostEstimate(flops=int(flops), bytes_accessed=int(traffic), transcendentals=0)


def on_device(queries, item_table, adagrad_state, pos_owner, pos_row, neg_rows):
    examples, width = queries.shape
    table_rows = item_table.shape[0]
    neg_dev = neg_rows.shape[0]
    items = lax.axis_size("item")
    groups = lax.axis_size("dp")
    bits = groups.bit_length() - 1
    assert groups == 1 << bits and bits > 0
    assert items & (items - 1) == 0 and items > 1
    capacity = 3 * examples // items
    slots = -(-capacity // 128) * 128
    negs = groups * items * neg_dev
    item = lax.axis_index("item")
    group = lax.axis_index("dp")
    smem = pl.BlockSpec(memory_space=pltpu.SMEM)
    anywhere = pl.BlockSpec(memory_space=pl.ANY)

    ring = [(index, (index + 2) % items) for index in range(items)]
    pair = flip(items, 0)
    steps, block = [], queries
    for step in range(items // 2):
        if step:
            block = lax.ppermute(block, "item", ring)
        other = lax.ppermute(block, "item", pair)
        steps.append((block, other))

    own_gid = pos_owner[:, 0] * table_rows + pos_row
    my_ids = item * table_rows + neg_rows
    lanes = -(-3 * examples // neg_dev)
    side_width = -(-(64 + lanes) // 128) * 128
    spread = jnp.pad(to_digits(own_gid, 0), (0, lanes * neg_dev - 3 * examples))
    payload = jnp.concatenate(
        [
            unit_rows(item_table[neg_rows])[0].astype(BF16),
            jnp.pad(to_digits(my_ids[:, None], 1), ((0, 0), (0, side_width - 3 - lanes))),
            spread.reshape(neg_dev, lanes),
        ],
        axis=1,
    )
    column = to_all(payload, "item", items)
    spread = column[:, :, width + side_width - lanes :].astype(jnp.int32)
    spread = spread.reshape(items, neg_dev * lanes)[:, : 3 * examples]
    spread = spread.reshape(items, 3, examples)
    gids = spread[:, 0] * 4096 + spread[:, 1] * 64 + spread[:, 2]
    column_negs = [column.reshape(items * neg_dev, width + side_width)]
    for other in range(1, groups):
        column_negs.append(
            lax.ppermute(column_negs[0], "dp", [(at, at ^ other) for at in range(groups)])
        )

    rank, rid, place = pl.pallas_call(
        route_kernel,
        out_shape=(
            jax.ShapeDtypeStruct((items, examples), F32),
            jax.ShapeDtypeStruct((items, slots), jnp.int32),
            jax.ShapeDtypeStruct((1, examples), F32),
        ),
        in_specs=[whole(), whole(), smem],
        out_specs=(whole(), whole(), whole()),
        cost_estimate=cost(2**32, 6 * table_rows * width),
        name="route",
    )(gids, own_gid[None, :], jnp.full((1,), table_rows, jnp.int32))
    chunk = math.gcd(table_rows, 512)
    tall = pl.BlockSpec((chunk, width), lambda step: (step, 0))
    send = pl.pallas_call(
        norm_kernel,
        out_shape=jax.ShapeDtypeStruct((table_rows, width), BF16),
        grid=(table_rows // chunk,),
        in_specs=[tall],
        out_specs=tall,
        cost_estimate=cost(2**32, 6 * table_rows * width),
        name="norm",
    )(item_table)
    found = ()
    for side in range(2):
        start = side * items // 4
        found = (
            pl.pallas_call(
                lambda *refs, start=start: find_kernel(start, *refs),
                out_shape=jax.ShapeDtypeStruct((items * slots, width), BF16),
                grid=(items // 4,),
                in_specs=[whole(), whole()] + [anywhere] * len(found),
                out_specs=pl.BlockSpec(
                    (2 * slots, width), lambda step, start=start: (start + step, 0)
                ),
                input_output_aliases={2: 0} if found else {},
                cost_estimate=cost(2**32, 8 * table_rows * width),
            )(rid, send, *found),
        )
    found = found[0]

    blocks = [block for step in steps for block in step]
    pull, out_rid, neg_part, local_ids, all_negs = pl.pallas_call(
        lambda *refs: owner_kernel(table_rows, *refs),
        out_shape=(
            jax.ShapeDtypeStruct((items * slots, width), BF16),
            jax.ShapeDtypeStruct((1, items * slots), F32),
            jax.ShapeDtypeStruct((negs, width), BF16),
            jax.ShapeDtypeStruct((1, negs), F32),
            jax.ShapeDtypeStruct((negs, width + side_width), BF16),
        ),
        in_specs=[anywhere] * (items + groups) + [whole(), whole(), anywhere],
        out_specs=(whole(),) * 5,
        scratch_shapes=[
            pltpu.VMEM((items, examples, width), BF16),
            pltpu.VMEM((items * slots, width), BF16),
            pltpu.VMEM((negs, 128), F32),
            pltpu.VMEM((negs, 2 * slots), BF16),
            pltpu.VMEM((negs, width), F32),
            pltpu.SemaphoreType.DMA((2 * items + groups,)),
        ],
        cost_estimate=cost(8 * items * slots * negs * width, 8 * negs * width),
        name="owner",
    )(*blocks, *column_negs, rank, rid, found)
    back = lax.all_to_all(
        found.reshape(items, slots, width), "item", split_axis=0, concat_axis=0, tiled=True
    ).reshape(items * slots, width)

    quarter = table_rows // 4
    orders = [list(range(bits)), list(range(bits))[::-1]]
    firsts = [(group >> order[0]) & 1 for order in orders]
    starts = [2 * side * quarter for side in range(2)]

    def scatter(keep):
        bits_used = [order[0] for order in orders]
        return pl.pallas_call(
            lambda *refs: scatter_kernel(keep, bits_used, *refs),
            out_shape=(jax.ShapeDtypeStruct((quarter, width), BF16),) * 2,
            in_specs=[whole(), whole()],
            out_specs=(whole(), whole()),
            cost_estimate=cost(4 * items * slots * quarter * width, 4 * quarter * width),
            name="keep" if keep else "give",
        )(pull, out_rid)

    gives = scatter(False)
    gots = []
    for side in range(2):
        gots.append(lax.ppermute(gives[side], "dp", flip(groups, orders[side][0])))
    keeps = scatter(True)
    values, others = [], []
    for side, order in enumerate(orders):
        value = add(keeps[side], gots[side])
        for level in range(1, bits):
            value = halve(value, "dp", groups, order[level])
        for level in range(bits - 1, 0, -1):
            value = double(value, "dp", groups, order[level])
        values.append(value)
        others.append(lax.ppermute(value, "dp", flip(groups, order[0])))

    neg_sum = neg_part.reshape(groups, items, neg_dev, width)
    for bit in range(items.bit_length() - 1):
        split = neg_sum.reshape(groups, neg_sum.shape[1] // 2, 2, neg_dev, width)
        mine = (item >> bit) & 1
        give = lax.dynamic_index_in_dim(split, 1 - mine, 2, keepdims=False)
        keep = lax.dynamic_index_in_dim(split, mine, 2, keepdims=False)
        neg_sum = add(keep, lax.ppermute(give, "item", flip(items, bit)))
    neg_sum = neg_sum.reshape(groups * neg_dev, width)
    for bit in range(bits):
        neg_sum = add(neg_sum, lax.ppermute(neg_sum, "dp", flip(groups, bit)))
    neg_spots = lax.dynamic_slice_in_dim(
        local_ids.reshape(groups, items, neg_dev), item, 1, 1
    ).reshape(1, groups * neg_dev)

    chunk = math.gcd(quarter, 512)
    per = quarter // chunk
    updated = ()
    places = jnp.stack(
        [
            (start + (first ^ rest) * quarter) // chunk
            for rest in range(2)
            for start, first in zip(starts, firsts)
        ]
    )
    for rest, pieces in enumerate((values, others)):
        tall = pl.BlockSpec(
            (chunk, width), lambda step, at, rest=rest: (update_block(rest, step, at, per), 0)
        )
        flat = pl.BlockSpec(
            (1, chunk), lambda step, at, rest=rest: (0, update_block(rest, step, at, per))
        )
        updated = pl.pallas_call(
            lambda *refs, rest=rest: update_kernel(rest, *refs),
            out_shape=(
                jax.ShapeDtypeStruct((table_rows, width), F32),
                jax.ShapeDtypeStruct((1, table_rows), F32),
            ),
            grid_spec=pltpu.PrefetchScalarGridSpec(
                num_scalar_prefetch=1,
                grid=(2 * per,),
                in_specs=[
                    tall,
                    flat,
                    pl.BlockSpec((chunk, width), lambda step, _: (jnp.minimum(step, per - 1), 0)),
                    pl.BlockSpec((chunk, width), lambda step, _: (jnp.maximum(step - per, 0), 0)),
                    whole(),
                    whole(),
                    *[anywhere] * len(updated),
                ],
                out_specs=(tall, flat),
            ),
            input_output_aliases={7: 0, 8: 1} if updated else {},
            cost_estimate=cost(2**32, 5 * table_rows * width),
            name="update_rest" if rest else "update_own",
        )(places, item_table, adagrad_state[None, :], *pieces, neg_sum, neg_spots, *updated)
    new_table, new_state = updated

    part = math.gcd(examples // 2, 256)
    per = examples // 2 // part
    homes = ()
    for side in range(2):
        tall = pl.BlockSpec((part, width), lambda step, side=side: (side * per + step, 0))
        flat = pl.BlockSpec((1, part), lambda step, side=side: (0, side * per + step))
        homes = pl.pallas_call(
            lambda *refs: home_kernel(table_rows, *refs),
            out_shape=(
                jax.ShapeDtypeStruct((examples, width), BF16),
                jax.ShapeDtypeStruct((1, examples), F32),
            ),
            grid=(per,),
            in_specs=[tall, flat, flat, whole(), whole(), whole()] + [anywhere] * len(homes),
            out_specs=(tall, flat),
            input_output_aliases={6: 0, 7: 1} if homes else {},
            cost_estimate=cost(2**32, 8 * negs * width),
        )(queries, place, own_gid[None, :], back, all_negs, local_ids, *homes)
    query_grad, example_loss = homes
    return (query_grad, example_loss.reshape(examples), new_table, new_state.reshape(table_rows))


def solution(mesh):
    placed = (
        P(("dp", "item"), None),
        P("item", None),
        P("item"),
        P(("dp", "item"), None),
        P(("dp", "item")),
        P(("dp", "item")),
    )

    return jax.shard_map(
        on_device,
        mesh=mesh,
        in_specs=placed,
        out_specs=(P(("dp", "item"), None), P(("dp", "item")), P("item", None), P("item")),
        check_vma=False,
    )
```

time: 185 us -> 169 us (0.914)
  waiting for transfers between devices: 44.7 us -> 38 us
  starting transfers between devices: 37.4 us -> 31.4 us
  other arithmetic: 10.6 us -> 8.41 us
    all_to_all x3 -> x1, waiting for transfers between devices: 15.7 us -> 1.01 us  [to_all(): return lax.all_to_all(copies, name, split_axis=0, concat_axis=0, tiled=True)]
    ppermute x3, waiting for transfers between devices: 6.17 us -> 20.4 us  [on_device(): block = lax.ppermute(block, 'item', ring)]
    all_to_all x3 -> x1, starting transfers between devices: 13.7 us -> 3.98 us  [to_all(): return lax.all_to_all(copies, name, split_axis=0, concat_axis=0, tiled=True)]
    ppermute x13 -> x16, waiting for transfers between devices: 22.8 us -> 16.6 us  [the longest x2 5.09 us: on_device(): neg_sum = add(neg_sum, lax.ppermute(neg_sum, 'dp', flip(groups, bit)))]
    another operation x10 -> x4, other arithmetic: 4.96 us -> 1.43 us  [the longest x4 2.41 us: on_device(): scalars = jnp.stack([item, source, other_source, jnp.int32(table_rows)])]
    ppermute x3, starting transfers between devices: 2.03 us -> 5.18 us  [on_device(): block = lax.ppermute(block, 'item', ring)]
    convert_element_type x9, other arithmetic: 1.3 us -> 3.43 us  [add(): return (left.astype(F32) + right.astype(F32)).astype(BF16)]
    ppermute x13 -> x16, starting transfers between devices: 16.2 us -> 18 us  [the longest x3 5.58 us: on_device(): lax.ppermute(column_negs[0], 'dp', [(at, at ^ other) for at in range(grou...]
  transfers between devices with their start and end apart: 24 -> 25, of which waited for: 9 -> 8; matrix products, arithmetic and copies ran while one was open for 9% -> 9% of each run, Pallas kernels for 37% -> 43%
where the time goes in v3:
time: 169 us; the launch traced here: 167 us
  Pallas kernels  79.2 us (47%)
  waiting for transfers between devices  38 us (22%)
  starting transfers between devices  31.4 us (19%)
  local copies, waits for them, and re-layouts  9.4 us (6%)
  other arithmetic  8.41 us (5%)
    ppermute x3, waiting for transfers between devices, on_device(): block = lax.ppermute(block, 'item', ring)  20.4 us
    pallas_call x1, Pallas kernels, on_device(): pl.pallas_call(lambda *refs: owner_kernel(table_rows, *refs), out_shape=(...  17.4 us
    pallas_call x2, Pallas kernels, on_device(): pl.pallas_call(lambda *refs, rest=rest: update_kernel(rest, *refs), out_s...  14.3 us
    pallas_call x2, Pallas kernels, on_device(): pl.pallas_call(lambda *refs, start=start: find_kernel(start, *refs), out_...  13.2 us
    pallas_call x2, Pallas kernels, on_device(): pl.pallas_call(lambda *refs: home_kernel(table_rows, *refs), out_shape=(j...  12.9 us
    pallas_call x2, Pallas kernels, scatter(): pl.pallas_call(lambda *refs: scatter_kernel(keep, bits_used, *refs), out_...  11.3 us
    pallas_call x1, Pallas kernels, on_device(): pl.pallas_call(norm_kernel, out_shape=jax.ShapeDtypeStruct((table_rows, w...  6.71 us
    ppermute x3, starting transfers between devices, on_device(): lax.ppermute(column_negs[0], 'dp', [(at, at ^ other) for at in range(grou...  5.58 us
  transfers between devices with their start and end apart: 25, of which 8 were waited for; matrix products, arithmetic and copies ran while one was open for 9% of the time, Pallas kernels for 43%

profile of v3, /device:TPU:0, one launch (start us, length us, event | category | flops | bytes accessed | tf_op | source)
XLA Modules:
  0.0 167.3 jit_solution(5922329689873310883)
XLA Ops:
  0.6 3.1 %collective-permute-start.1 = (bf16[1024,256]{1,0:T(8,128)(2,1)}, bf16[1024,256]{1,0:T(8,128)(2,1)S(1)}, u32[]{:S(2)}, u32[]{:S(2)}) collective-permute-start(bf16[1024,256]{1,0:T(8,128)(2,1)} %refs_0_.5), channel_id=1, source_target_pairs={{0,2},{1,3},{2,4},{3,5},{4,6},{5,7},{6,0},{7,1},{8,10},{9,11},{10,... | collective-permute-start | bytes 1572872 | tf_op jit(solution)/shard_map/ppermute | solution.py:316
  3.7 0.7 fusion.16
  4.4 0.7 broadcast_multiply_fusion
  5.1 0.7 fusion.9
  5.9 2.8 %gather_fusion = f32[48,256]{1,0:T(8,128)S(1)} fusion(f32[4096,256]{1,0:T(8,128)} %refs_1_.3, s32[1024]{0:T(1024)S(1)} %pad_clamp_fusion), kind=kCustom, calls=%fused_computation | custom fusion | bytes 98496 | tf_op jit(solution)/shard_map/gather | solution.py:327
  9.3 0.7 broadcast_in_dim.9
  10.1 4.0 %all-to-all-start = ((bf16[8,48,384]{2,1,0:T(8,128)(2,1)}), bf16[8,48,384]{2,1,0:T(8,128)(2,1)S(1)}, u32[]{:S(2)}, u32[]{:S(2)}) async-start(bf16[8,48,384]{2,1,0:T(8,128)(2,1)} %broadcast_in_dim.9), calls=%async_computation | async-start | bytes 589824 | tf_op jit(solution)/shard_map/all_to_all | solution.py:287
  14.0 6.7 %norm.1.refs_1_ = bf16[4096,256]{1,0:T(8,128)(2,1)} custom-call(f32[4096,256]{1,0:T(8,128)} %refs_1_.3), custom_call_target="tpu_custom_call" | custom-call | flops 4294967296 | bytes 6291456 | tf_op jit(solution)/shard_map/norm/pallas_call | solution.py:358
  20.8 2.1 %collective-permute-start.3 = (bf16[1024,256]{1,0:T(8,128)(2,1)S(1)}, bf16[1024,256]{1,0:T(8,128)(2,1)S(1)}, u32[]{:S(2)}, u32[]{:S(2)}) collective-permute-start(bf16[1024,256]{1,0:T(8,128)(2,1)S(1)} %collective-permute-done.1.refs_2_), channel_id=1, source_target_pairs={{0,2},{1,3},{2,4},{3,5},{4,6},{5,7},{6,0},{7,1},{8,10},{9,11},{10,... | collective-permute-start | bytes 1572872 | tf_op jit(solution)/shard_map/ppermute | solution.py:316
  22.8 0.6 pad_add_fusion.refs_0_
  23.4 1.0 all-to-all-done
  24.7 2.5 %collective-permute-start.9 = (bf16[384,384]{1,0:T(8,128)(2,1)S(1)}, bf16[384,384]{1,0:T(8,128)(2,1)S(1)}, u32[]{:S(2)}, u32[]{:S(2)}) collective-permute-start(bf16[384,384]{1,0:T(8,128)(2,1)S(1)} %bitcast.46), channel_id=1, source_target_pairs={{0,24},{8,16},{16,8},{24,0},{1,25},{9,17},{17,9},{25,1},{2,26},{10... | collective-permute-start | bytes 884744 | tf_op jit(solution)/shard_map/ppermute | solution.py:341
  27.3 9.7 %collective-permute-done.3.refs_4_ = bf16[1024,256]{1,0:T(8,128)(2,1)S(1)} collective-permute-done((bf16[1024,256]{1,0:T(8,128)(2,1)S(1)}, bf16[1024,256]{1,0:T(8,128)(2,1)S(1)}, u32[]{:S(2)}, u32[]{:S(2)}) %collective-permute-start.3) | collective-permute-done | bytes 524320 | tf_op jit(solution)/shard_map/ppermute | solution.py:316
  36.9 0.7 fusion.6.gid_ref
  37.6 3.4 %route.1 = (f32[8,1024]{1,0:T(8,128)}, s32[8,384]{1,0:T(8,128)}, f32[1,1024]{1,0:T(1,128)}) custom-call(s32[8,1024]{1,0:T(8,128)} %fusion.6.gid_ref, s32[1,1024]{1,0:T(1,128)} %bitcast.51, s32[1]{0:T(128)} %constant.153.clone.1.rows_ref), custom_call_target="tpu_custom_call" | custom-call | flops 4294967296 | bytes 6291456 | tf_op jit(solution)/shard_map/route/pallas_call | solution.py:344
  41.6 10.7 %collective-permute-done.5.refs_6_ = bf16[1024,256]{1,0:T(8,128)(2,1)} collective-permute-done((bf16[1024,256]{1,0:T(8,128)(2,1)S(1)}, bf16[1024,256]{1,0:T(8,128)(2,1)}, u32[]{:S(2)}, u32[]{:S(2)}) %collective-permute-start.5) | collective-permute-done | bytes 524320 | tf_op jit(solution)/shard_map/ppermute | solution.py:316
  52.3 6.6 %shard_map.93.refs_2_ = bf16[3072,256]{1,0:T(8,128)(2,1)} custom-call(s32[8,384]{1,0:T(8,128)} %get-tuple-element.25.refs_0_.refs_13_, bf16[4096,256]{1,0:T(8,128)(2,1)} %norm.1.refs_1_), custom_call_target="tpu_custom_call" | custom-call | flops 4294967296 | bytes 8388608 | tf_op jit(solution)/shard_map/pallas_call | solution.py:371
  58.9 1.5 collective-permute-start.8
  60.5 1.5 collective-permute-start.7
  62.0 6.6 %shard_map.94.refs_14_ = bf16[3072,256]{1,0:T(8,128)(2,1)} custom-call(s32[8,384]{1,0:T(8,128)} %get-tuple-element.25.refs_0_.refs_13_, bf16[4096,256]{1,0:T(8,128)(2,1)} %norm.1.refs_1_, bf16[3072,256]{1,0:T(8,128)(2,1)} %shard_map.93.refs_2_), custom_call_target="tpu_custom_call", output_to_operand_aliasing={{}: (2, {})} | custom-call | flops 4294967296 | bytes 8388608 | tf_op jit(solution)/shard_map/pallas_call | solution.py:371
  68.6 3.8 %all-to-all-start.1 = ((bf16[8,384,256]{2,1,0:T(8,128)(2,1)}), bf16[8,384,256]{2,1,0:T(8,128)(2,1)S(1)}, u32[]{:S(2)}, u32[]{:S(2)}) async-start(bf16[8,384,256]{2,1,0:T(8,128)(2,1)} %bitcast.41), calls=%async_computation.1 | async-start | bytes 3145728 | tf_op jit(solution)/shard_map/all_to_all | solution.py:408
  72.4 17.4 %owner.1 = (bf16[3072,256]{1,0:T(8,128)(2,1)}, f32[1,3072]{1,0:T(1,128)}, bf16[1536,256]{1,0:T(8,128)(2,1)}, f32[1,1536]{1,0:T(1,128)}, bf16[1536,384]{1,0:T(8,128)(2,1)}) custom-call(bf16[1024,256]{1,0:T(8,128)(2,1)} %refs_0_.5, bf16[1024,256]{1,0:T(8,128)(2,1)} %copy-done.8, bf16[1024,256]{1,0:T(8,128)(2,1)} %copy-done.7, ...), custom_call_target="tpu_custom_call" | custom-call | flops 9663676416 | bytes 3145728 | tf_op jit(solution)/shard_map/owner/pallas_call | solution.py:386
  89.8 0.7 reduce
  90.6 1.8 %dynamic-slice_bitcast_fusion = bf16[4,4,48,256]{3,2,1,0:T(8,128)(2,1)} fusion(bf16[4,4,2,48,256]{4,3,2,1,0:T(8,128)(2,1)} %bitcast.44, s32[]{:T(128)S(6)} %select_n.138), kind=kLoop, calls=%fused_computation.11 | loop fusion | bytes 786436 | tf_op jit(solution)/shard_map/jit(dynamic_index_in_dim)/squeeze | solution.py:447
  92.6 5.6 %give.1 = (bf16[1024,256]{1,0:T(8,128)(2,1)}, bf16[1024,256]{1,0:T(8,128)(2,1)}) custom-call(bf16[3072,256]{1,0:T(8,128)(2,1)} %get-tuple-element.33.refs_0_, f32[1,3072]{1,0:T(1,128)} %get-tuple-element.34.refs_1_), custom_call_target="tpu_custom_call" | custom-call | flops 3221225472 | bytes 1048576 | tf_op jit(solution)/shard_map/give/pallas_call | solution.py:419
  98.2 0.7 reshape.126.refs_6_
  99.9 5.6 %keep.1 = (bf16[1024,256]{1,0:T(8,128)(2,1)}, bf16[1024,256]{1,0:T(8,128)(2,1)}) custom-call(bf16[3072,256]{1,0:T(8,128)(2,1)} %get-tuple-element.33.refs_0_, f32[1,3072]{1,0:T(1,128)} %get-tuple-element.34.refs_1_), custom_call_target="tpu_custom_call" | custom-call | flops 3221225472 | bytes 1048576 | tf_op jit(solution)/shard_map/keep/pallas_call | solution.py:419
  105.6 1.2 fusion
  106.8 1.7 %collective-permute-start.19 = (bf16[4,2,48,256]{3,2,1,0:T(8,128)(2,1)S(1)}, bf16[4,2,48,256]{3,2,1,0:T(8,128)(2,1)S(1)}, u32[]{:S(2)}, u32[]{:S(2)}) collective-permute-start(bf16[4,2,48,256]{3,2,1,0:T(8,128)(2,1)S(1)} %dynamic-slice_bitcast_fusion.1), channel_id=1, source_target_pairs={{0,2},{1,3},{2,0},{3,1},{4,6},{5,7},{6,4},{7,5},{8,10},{9,11},{10,... | collective-permute-start | bytes 589832 | tf_op jit(solution)/shard_map/ppermute | solution.py:449
  108.5 4.8 %collective-permute-done.10 = bf16[1024,256]{1,0:T(8,128)(2,1)S(1)} collective-permute-done((bf16[1024,256]{1,0:T(8,128)(2,1)}, bf16[1024,256]{1,0:T(8,128)(2,1)S(1)}, u32[]{:S(2)}, u32[]{:S(2)}) %collective-permute-start.10) | collective-permute-done | bytes 524320 | tf_op jit(solution)/shard_map/ppermute | solution.py:431
  113.2 1.2 add_convert_fusion.1
  115.3 2.7 %collective-permute-start.20 = (bf16[4,1,48,256]{3,2,1,0:T(8,128)(2,1)S(1)}, bf16[4,1,48,256]{3,2,1,0:T(8,128)(2,1)S(1)}, u32[]{:S(2)}, u32[]{:S(2)}) collective-permute-start(bf16[4,1,48,256]{3,2,1,0:T(8,128)(2,1)S(1)} %constant_dynamic-slice_fusion.1), channel_id=1, source_target_pairs={{0,4},{1,5},{2,6},{3,7},{4,0},{5,1},{6,2},{7,3},{8,12},{9,13},{10,... | collective-permute-start | bytes 294920 | tf_op jit(solution)/shard_map/ppermute | solution.py:449
  118.0 0.6 collective-permute-start.15
  118.6 3.8 %collective-permute-done.20 = bf16[4,1,48,256]{3,2,1,0:T(8,128)(2,1)S(1)} collective-permute-done((bf16[4,1,48,256]{3,2,1,0:T(8,128)(2,1)S(1)}, bf16[4,1,48,256]{3,2,1,0:T(8,128)(2,1)S(1)}, u32[]{:S(2)}, u32[]{:S(2)}) %collective-permute-start.20) | collective-permute-done | bytes 98336 | tf_op jit(solution)/shard_map/ppermute | solution.py:449
  123.1 1.6 collective-permute-start.12
  124.7 2.7 %collective-permute-done.21 = bf16[192,256]{1,0:T(8,128)(2,1)S(1)} collective-permute-done((bf16[192,256]{1,0:T(8,128)(2,1)S(1)}, bf16[192,256]{1,0:T(8,128)(2,1)S(1)}, u32[]{:S(2)}, u32[]{:S(2)}) %collective-permute-start.21) | collective-permute-done | bytes 98336 | tf_op jit(solution)/shard_map/ppermute | solution.py:452
  127.4 1.6 collective-permute-start.22
  129.7 2.4 %collective-permute-done.22 = bf16[192,256]{1,0:T(8,128)(2,1)S(1)} collective-permute-done((bf16[192,256]{1,0:T(8,128)(2,1)S(1)}, bf16[192,256]{1,0:T(8,128)(2,1)S(1)}, u32[]{:S(2)}, u32[]{:S(2)}) %collective-permute-start.22) | collective-permute-done | bytes 98336 | tf_op jit(solution)/shard_map/ppermute | solution.py:452
  132.1 0.7 add_convert_fusion.4.refs_5_
  133.0 1.1 collective-permute-start.13
  134.2 2.9 %collective-permute-done.16 = bf16[512,256]{1,0:T(8,128)(2,1)S(1)} collective-permute-done((bf16[512,256]{1,0:T(8,128)(2,1)S(1)}, bf16[512,256]{1,0:T(8,128)(2,1)S(1)}, u32[]{:S(2)}, u32[]{:S(2)}) %collective-permute-start.16) | collective-permute-done | bytes 262176 | tf_op jit(solution)/shard_map/ppermute | solution.py:274
  137.4 0.7 copy-done.5
  138.1 7.2 %update_own.1 = (f32[4096,256]{1,0:T(8,128)}, f32[1,4096]{1,0:T(1,128)}) custom-call(s32[4]{0:T(128)} %pad_add_fusion.refs_0_, f32[4096,256]{1,0:T(8,128)} %refs_1_.3, f32[1,4096]{1,0:T(1,128)} %bitcast.56, bf16[1024,256]{1,0:T(8,128)(2,1)} %copy-done.4, bf16[1024,256]{1,0:T(8,128)(2,1)} %copy-done.5, bf16[192,256]{1,0:T(8,128)(2,1)} %add_convert_fusion.4.refs_5_, ...), custom_call_target="tpu_custom_call" | custom-call | flops 4294967296 | bytes 5242880 | tf_op jit(solution)/shard_map/update_own/pallas_call | solution.py:474
  145.3 1.2 copy-done
  146.4 6.4 %shard_map.95 = (bf16[1024,256]{1,0:T(8,128)(2,1)}, f32[1,1024]{1,0:T(1,128)}) custom-call(bf16[1024,256]{1,0:T(8,128)(2,1)} %refs_0_.5, f32[1,1024]{1,0:T(1,128)} %get-tuple-element.24.refs_1_, s32[1,1024]{1,0:T(1,128)} %bitcast.52, bf16[3072,256]{1,0:T(8,128)(2,1)} %bitcast.39, bf16[1536,384]{1,0:T(8,128)(2,1)} %get-tuple-element.27.refs_4_, ...), custom_call_target="tpu_custom_call" | custom-call | flops 4294967296 | bytes 3145728 | tf_op jit(solution)/shard_map/pallas_call | solution.py:506
  152.9 6.5 %shard_map.96 = (bf16[1024,256]{1,0:T(8,128)(2,1)}, f32[1,1024]{1,0:T(1,128)}) custom-call(bf16[1024,256]{1,0:T(8,128)(2,1)} %refs_0_.5, f32[1,1024]{1,0:T(1,128)} %get-tuple-element.24.refs_1_, s32[1,1024]{1,0:T(1,128)} %bitcast.53, bf16[3072,256]{1,0:T(8,128)(2,1)} %bitcast.40, ...), custom_call_target="tpu_custom_call", output_to_operand_aliasing={{0}: (6, {}), {1}: (7, {})} | custom-call | flops 4294967296 | bytes 3145728 | tf_op jit(solution)/shard_map/pallas_call | solution.py:506
  159.4 0.8 copy-done.10
  160.1 7.2 %update_rest.1 = (f32[4096,256]{1,0:T(8,128)}, f32[1,4096]{1,0:T(1,128)}) custom-call(s32[4]{0:T(128)} %pad_add_fusion.refs_0_, f32[4096,256]{1,0:T(8,128)} %refs_1_.3, f32[1,4096]{1,0:T(1,128)} %bitcast.57, bf16[1024,256]{1,0:T(8,128)(2,1)} %copy-done.10, ...), custom_call_target="tpu_custom_call", output_to_operand_aliasing={{0}: (7, {}), {1}: (8, {})} | custom-call | flops 4294967296 | bytes 5242880 | tf_op jit(solution)/shard_map/update_rest/pallas_call | solution.py:474
  (79 shorter events, 5.7 us)
Async XLA Ops:
  0.6 20.1 %collective-permute-start.1 = (bf16[1024,256]{1,0:T(8,128)(2,1)}, bf16[1024,256]{1,0:T(8,128)(2,1)S(1)}, u32[]{:S(2)}, u32[]{:S(2)}) collective-permute-start(bf16[1024,256]{1,0:T(8,128)(2,1)} %refs_0_.5), channel_id=1, source_target_pairs={{0,2},{1,3},{2,4},{3,5},{4,6},{5,7},{6,0},{7,1},{8,10},{9,11},{10,... | collective-permute-start | bytes 1572872 | tf_op jit(solution)/shard_map/ppermute | solution.py:316
  3.7 55.2 %collective-permute-start = (bf16[1024,256]{1,0:T(8,128)(2,1)}, bf16[1024,256]{1,0:T(8,128)(2,1)S(1)}, u32[]{:S(2)}, u32[]{:S(2)}) collective-permute-start(bf16[1024,256]{1,0:T(8,128)(2,1)} %refs_0_.5), channel_id=1, source_target_pairs={{0,1},{1,0},{2,3},{3,2},{4,5},{5,4},{6,7},{7,6},{8,9},{9,8},{10,11... | collective-permute-start | bytes 1572872 | tf_op jit(solution)/shard_map/ppermute | solution.py:317
  5.8 14.9 %copy-start.6 = (s32[1024]{0:T(1024)}, s32[1024]{0:T(1024)S(1)}, u32[]{:S(2)}) copy-start(s32[1024]{0:T(1024)S(1)} %get-tuple-element.45) | copy-start | bytes 12292
  10.1 14.4 %all-to-all-start = ((bf16[8,48,384]{2,1,0:T(8,128)(2,1)}), bf16[8,48,384]{2,1,0:T(8,128)(2,1)S(1)}, u32[]{:S(2)}, u32[]{:S(2)}) async-start(bf16[8,48,384]{2,1,0:T(8,128)(2,1)} %broadcast_in_dim.9), calls=%async_computation | async-start | bytes 589824 | tf_op jit(solution)/shard_map/all_to_all | solution.py:287
  20.8 20.3 %copy-start.7 = (bf16[1024,256]{1,0:T(8,128)(2,1)}, bf16[1024,256]{1,0:T(8,128)(2,1)S(1)}, u32[]{:S(2)}) copy-start(bf16[1024,256]{1,0:T(8,128)(2,1)S(1)} %collective-permute-done.1.refs_2_) | copy-start | bytes 1572868
  20.8 16.2 %collective-permute-start.3 = (bf16[1024,256]{1,0:T(8,128)(2,1)S(1)}, bf16[1024,256]{1,0:T(8,128)(2,1)S(1)}, u32[]{:S(2)}, u32[]{:S(2)}) collective-permute-start(bf16[1024,256]{1,0:T(8,128)(2,1)S(1)} %collective-permute-done.1.refs_2_), channel_id=1, source_target_pairs={{0,2},{1,3},{2,4},{3,5},{4,6},{5,7},{6,0},{7,1},{8,10},{9,11},{10,... | collective-permute-start | bytes 1572872 | tf_op jit(solution)/shard_map/ppermute | solution.py:316
  24.5 36.0 %copy-start.3 = (bf16[8,48,384]{2,1,0:T(8,128)(2,1)}, bf16[8,48,384]{2,1,0:T(8,128)(2,1)S(1)}, u32[]{:S(2)}) copy-start(bf16[8,48,384]{2,1,0:T(8,128)(2,1)S(1)} %all-to-all-done) | copy-start | bytes 884740
  24.7 35.7 %collective-permute-start.9 = (bf16[384,384]{1,0:T(8,128)(2,1)S(1)}, bf16[384,384]{1,0:T(8,128)(2,1)S(1)}, u32[]{:S(2)}, u32[]{:S(2)}) collective-permute-start(bf16[384,384]{1,0:T(8,128)(2,1)S(1)} %bitcast.46), channel_id=1, source_target_pairs={{0,24},{8,16},{16,8},{24,0},{1,25},{9,17},{17,9},{25,1},{2,26},{10... | collective-permute-start | bytes 884744 | tf_op jit(solution)/shard_map/ppermute | solution.py:341
  36.9 4.1 %copy-start.9 = (bf16[1024,256]{1,0:T(8,128)(2,1)}, bf16[1024,256]{1,0:T(8,128)(2,1)S(1)}, u32[]{:S(2)}) copy-start(bf16[1024,256]{1,0:T(8,128)(2,1)S(1)} %collective-permute-done.3.refs_4_) | copy-start | bytes 1572868
  36.9 15.4 %collective-permute-start.5 = (bf16[1024,256]{1,0:T(8,128)(2,1)S(1)}, bf16[1024,256]{1,0:T(8,128)(2,1)}, u32[]{:S(2)}, u32[]{:S(2)}) collective-permute-start(bf16[1024,256]{1,0:T(8,128)(2,1)S(1)} %collective-permute-done.3.refs_4_), channel_id=1, source_target_pairs={{0,2},{1,3},{2,4},{3,5},{4,6},{5,7},{6,0},{7,1},{8,10},{9,11},{10,... | collective-permute-start | bytes 1572872 | tf_op jit(solution)/shard_map/ppermute | solution.py:316
  41.1 31.3 %collective-permute-start.2 = (bf16[1024,256]{1,0:T(8,128)(2,1)S(1)}, bf16[1024,256]{1,0:T(8,128)(2,1)}, u32[]{:S(2)}, u32[]{:S(2)}) collective-permute-start(bf16[1024,256]{1,0:T(8,128)(2,1)S(1)} %collective-permute-done.1.refs_2_), channel_id=1, source_target_pairs={{0,1},{1,0},{2,3},{3,2},{4,5},{5,4},{6,7},{7,6},{8,9},{9,8},{10,11... | collective-permute-start | bytes 1572872 | tf_op jit(solution)/shard_map/ppermute | solution.py:317
  41.1 31.3 %collective-permute-start.4 = (bf16[1024,256]{1,0:T(8,128)(2,1)S(1)}, bf16[1024,256]{1,0:T(8,128)(2,1)}, u32[]{:S(2)}, u32[]{:S(2)}) collective-permute-start(bf16[1024,256]{1,0:T(8,128)(2,1)S(1)} %collective-permute-done.3.refs_4_), channel_id=1, source_target_pairs={{0,1},{1,0},{2,3},{3,2},{4,5},{5,4},{6,7},{7,6},{8,9},{9,8},{10,11... | collective-permute-start | bytes 1572872 | tf_op jit(solution)/shard_map/ppermute | solution.py:317
  52.3 20.1 %collective-permute-start.6 = (bf16[1024,256]{1,0:T(8,128)(2,1)}, bf16[1024,256]{1,0:T(8,128)(2,1)}, u32[]{:S(2)}, u32[]{:S(2)}) collective-permute-start(bf16[1024,256]{1,0:T(8,128)(2,1)} %collective-permute-done.5.refs_6_), channel_id=1, source_target_pairs={{0,1},{1,0},{2,3},{3,2},{4,5},{5,4},{6,7},{7,6},{8,9},{9,8},{10,11... | collective-permute-start | bytes 1572872 | tf_op jit(solution)/shard_map/ppermute | solution.py:317
  58.9 9.7 %copy-start.8 = (bf16[1024,256]{1,0:T(8,128)(2,1)}, bf16[1024,256]{1,0:T(8,128)(2,1)S(1)}, u32[]{:S(2)}) copy-start(bf16[1024,256]{1,0:T(8,128)(2,1)S(1)} %collective-permute-done.refs_1_) | copy-start | bytes 1572868
  58.9 13.4 %collective-permute-start.8 = (bf16[384,384]{1,0:T(8,128)(2,1)S(1)}, bf16[384,384]{1,0:T(8,128)(2,1)}, u32[]{:S(2)}, u32[]{:S(2)}) collective-permute-start(bf16[384,384]{1,0:T(8,128)(2,1)S(1)} %bitcast.47), channel_id=1, source_target_pairs={{0,16},{8,24},{16,0},{24,8},{1,17},{9,25},{17,1},{25,9},{2,18},{10... | collective-permute-start | bytes 884744 | tf_op jit(solution)/shard_map/ppermute | solution.py:341
  60.4 8.1 %copy-start.11 = (bf16[384,384]{1,0:T(8,128)(2,1)}, bf16[384,384]{1,0:T(8,128)(2,1)S(1)}, u32[]{:S(2)}) copy-start(bf16[384,384]{1,0:T(8,128)(2,1)S(1)} %collective-permute-done.9.refs_11_) | copy-start | bytes 884740
  60.5 11.9 %collective-permute-start.7 = (bf16[384,384]{1,0:T(8,128)(2,1)S(1)}, bf16[384,384]{1,0:T(8,128)(2,1)}, u32[]{:S(2)}, u32[]{:S(2)}) collective-permute-start(bf16[384,384]{1,0:T(8,128)(2,1)S(1)} %bitcast.48), channel_id=1, source_target_pairs={{0,8},{8,0},{16,24},{24,16},{1,9},{9,1},{17,25},{25,17},{2,10},{10... | collective-permute-start | bytes 884744 | tf_op jit(solution)/shard_map/ppermute | solution.py:341
  68.6 76.7 %all-to-all-start.1 = ((bf16[8,384,256]{2,1,0:T(8,128)(2,1)}), bf16[8,384,256]{2,1,0:T(8,128)(2,1)S(1)}, u32[]{:S(2)}, u32[]{:S(2)}) async-start(bf16[8,384,256]{2,1,0:T(8,128)(2,1)} %bitcast.41), calls=%async_computation.1 | async-start | bytes 3145728 | tf_op jit(solution)/shard_map/all_to_all | solution.py:408
  92.4 13.2 %collective-permute-start.18 = (bf16[4,4,48,256]{3,2,1,0:T(8,128)(2,1)}, bf16[4,4,48,256]{3,2,1,0:T(8,128)(2,1)}, u32[]{:S(2)}, u32[]{:S(2)}) collective-permute-start(bf16[4,4,48,256]{3,2,1,0:T(8,128)(2,1)} %dynamic-slice_bitcast_fusion), channel_id=1, source_target_pairs={{0,1},{1,0},{2,3},{3,2},{4,5},{5,4},{6,7},{7,6},{8,9},{9,8},{10,11... | collective-permute-start | bytes 1179656 | tf_op jit(solution)/shard_map/ppermute | solution.py:449
  98.9 14.3 %collective-permute-start.10 = (bf16[1024,256]{1,0:T(8,128)(2,1)}, bf16[1024,256]{1,0:T(8,128)(2,1)S(1)}, u32[]{:S(2)}, u32[]{:S(2)}) collective-permute-start(bf16[1024,256]{1,0:T(8,128)(2,1)} %get-tuple-element.36), channel_id=1, source_target_pairs={{0,8},{8,0},{16,24},{24,16},{1,9},{9,1},{17,25},{25,17},{2,10},{10... | collective-permute-start | bytes 1572872 | tf_op jit(solution)/shard_map/ppermute | solution.py:431
  99.4 6.1 %copy-start.1 = (bf16[1536,256]{1,0:T(8,128)(2,1)S(1)}, bf16[1536,256]{1,0:T(8,128)(2,1)}, u32[]{:S(2)}) copy-start(bf16[1536,256]{1,0:T(8,128)(2,1)} %get-tuple-element.39) | copy-start | bytes 2359300
  99.4 15.6 %collective-permute-start.14 = (bf16[1024,256]{1,0:T(8,128)(2,1)}, bf16[1024,256]{1,0:T(8,128)(2,1)S(1)}, u32[]{:S(2)}, u32[]{:S(2)}) collective-permute-start(bf16[1024,256]{1,0:T(8,128)(2,1)} %get-tuple-element.38), channel_id=1, source_target_pairs={{0,16},{8,24},{16,0},{24,8},{1,17},{9,25},{17,1},{25,9},{2,18},{10... | collective-permute-start | bytes 1572872 | tf_op jit(solution)/shard_map/ppermute | solution.py:431
  105.6 9.5 %copy-start.2 = (bf16[1024,256]{1,0:T(8,128)(2,1)S(1)}, bf16[1024,256]{1,0:T(8,128)(2,1)}, u32[]{:S(2)}) copy-start(bf16[1024,256]{1,0:T(8,128)(2,1)} %get-tuple-element.37) | copy-start | bytes 1572868
  106.8 8.4 %collective-permute-start.19 = (bf16[4,2,48,256]{3,2,1,0:T(8,128)(2,1)S(1)}, bf16[4,2,48,256]{3,2,1,0:T(8,128)(2,1)S(1)}, u32[]{:S(2)}, u32[]{:S(2)}) collective-permute-start(bf16[4,2,48,256]{3,2,1,0:T(8,128)(2,1)S(1)} %dynamic-slice_bitcast_fusion.1), channel_id=1, source_target_pairs={{0,2},{1,3},{2,0},{3,1},{4,6},{5,7},{6,4},{7,5},{8,10},{9,11},{10,... | collective-permute-start | bytes 589832 | tf_op jit(solution)/shard_map/ppermute | solution.py:449
  114.5 8.6 %collective-permute-start.11 = (bf16[512,256]{1,0:T(8,128)(2,1)S(1)}, bf16[512,256]{1,0:T(8,128)(2,1)S(1)}, u32[]{:S(2)}, u32[]{:S(2)}) collective-permute-start(bf16[512,256]{1,0:T(8,128)(2,1)S(1)} %constant_dynamic-slice_fusion.3), channel_id=1, source_target_pairs={{0,16},{8,24},{16,0},{24,8},{1,17},{9,25},{17,1},{25,9},{2,18},{10... | collective-permute-start | bytes 786440 | tf_op jit(solution)/shard_map/ppermute | solution.py:269
  115.3 7.1 %collective-permute-start.20 = (bf16[4,1,48,256]{3,2,1,0:T(8,128)(2,1)S(1)}, bf16[4,1,48,256]{3,2,1,0:T(8,128)(2,1)S(1)}, u32[]{:S(2)}, u32[]{:S(2)}) collective-permute-start(bf16[4,1,48,256]{3,2,1,0:T(8,128)(2,1)S(1)} %constant_dynamic-slice_fusion.1), channel_id=1, source_target_pairs={{0,4},{1,5},{2,6},{3,7},{4,0},{5,1},{6,2},{7,3},{8,12},{9,13},{10,... | collective-permute-start | bytes 294920 | tf_op jit(solution)/shard_map/ppermute | solution.py:449
  118.0 11.0 %collective-permute-start.15 = (bf16[512,256]{1,0:T(8,128)(2,1)S(1)}, bf16[512,256]{1,0:T(8,128)(2,1)S(1)}, u32[]{:S(2)}, u32[]{:S(2)}) collective-permute-start(bf16[512,256]{1,0:T(8,128)(2,1)S(1)} %constant_dynamic-slice_fusion.2), channel_id=1, source_target_pairs={{0,8},{8,0},{16,24},{24,16},{1,9},{9,1},{17,25},{25,17},{2,10},{10... | collective-permute-start | bytes 786440 | tf_op jit(solution)/shard_map/ppermute | solution.py:269
  122.5 4.9 %collective-permute-start.21 = (bf16[192,256]{1,0:T(8,128)(2,1)S(1)}, bf16[192,256]{1,0:T(8,128)(2,1)S(1)}, u32[]{:S(2)}, u32[]{:S(2)}) collective-permute-start(bf16[192,256]{1,0:T(8,128)(2,1)S(1)} %bitcast.50), channel_id=1, source_target_pairs={{0,8},{8,0},{16,24},{24,16},{1,9},{9,1},{17,25},{25,17},{2,10},{10... | collective-permute-start | bytes 294920 | tf_op jit(solution)/shard_map/ppermute | solution.py:452
  123.1 9.6 %collective-permute-start.12 = (bf16[512,256]{1,0:T(8,128)(2,1)S(1)}, bf16[512,256]{1,0:T(8,128)(2,1)S(1)}, u32[]{:S(2)}, u32[]{:S(2)}) collective-permute-start(bf16[512,256]{1,0:T(8,128)(2,1)S(1)} %add_convert_fusion.3), channel_id=1, source_target_pairs={{0,16},{8,24},{16,0},{24,8},{1,17},{9,25},{17,1},{25,9},{2,18},{10... | collective-permute-start | bytes 786440 | tf_op jit(solution)/shard_map/ppermute | solution.py:274
  127.4 4.7 %collective-permute-start.22 = (bf16[192,256]{1,0:T(8,128)(2,1)S(1)}, bf16[192,256]{1,0:T(8,128)(2,1)S(1)}, u32[]{:S(2)}, u32[]{:S(2)}) collective-permute-start(bf16[192,256]{1,0:T(8,128)(2,1)S(1)} %add_convert_fusion.5), channel_id=1, source_target_pairs={{0,16},{8,24},{16,0},{24,8},{1,17},{9,25},{17,1},{25,9},{2,18},{10... | collective-permute-start | bytes 294920 | tf_op jit(solution)/shard_map/ppermute | solution.py:452
  129.1 8.0 %collective-permute-start.16 = (bf16[512,256]{1,0:T(8,128)(2,1)S(1)}, bf16[512,256]{1,0:T(8,128)(2,1)S(1)}, u32[]{:S(2)}, u32[]{:S(2)}) collective-permute-start(bf16[512,256]{1,0:T(8,128)(2,1)S(1)} %add_convert_fusion.2), channel_id=1, source_target_pairs={{0,8},{8,0},{16,24},{24,16},{1,9},{9,1},{17,25},{25,17},{2,10},{10... | collective-permute-start | bytes 786440 | tf_op jit(solution)/shard_map/ppermute | solution.py:274
  133.0 4.4 %copy-start.4 = (bf16[1024,256]{1,0:T(8,128)(2,1)}, bf16[1024,256]{1,0:T(8,128)(2,1)S(1)}, u32[]{:S(2)}) copy-start(bf16[1024,256]{1,0:T(8,128)(2,1)S(1)} %maximum_select_fusion.refs_3_) | copy-start | bytes 1572868
  133.0 26.3 %collective-permute-start.13 = (bf16[1024,256]{1,0:T(8,128)(2,1)S(1)}, bf16[1024,256]{1,0:T(8,128)(2,1)S(1)}, u32[]{:S(2)}, u32[]{:S(2)}) collective-permute-start(bf16[1024,256]{1,0:T(8,128)(2,1)S(1)} %maximum_select_fusion.refs_3_), channel_id=1, source_target_pairs={{0,8},{8,0},{16,24},{24,16},{1,9},{9,1},{17,25},{25,17},{2,10},{10... | collective-permute-start | bytes 1572872 | tf_op jit(solution)/shard_map/ppermute | solution.py:441
  137.3 0.8 copy-start.5
  137.3 22.0 %collective-permute-start.17 = (bf16[1024,256]{1,0:T(8,128)(2,1)S(1)}, bf16[1024,256]{1,0:T(8,128)(2,1)}, u32[]{:S(2)}, u32[]{:S(2)}) collective-permute-start(bf16[1024,256]{1,0:T(8,128)(2,1)S(1)} %maximum_select_fusion.1.refs_4_), channel_id=1, source_target_pairs={{0,16},{8,24},{16,0},{24,8},{1,17},{9,25},{17,1},{25,9},{2,18},{10... | collective-permute-start | bytes 1572872 | tf_op jit(solution)/shard_map/ppermute | solution.py:441
  145.3 1.2 copy-start
  159.4 0.8 copy-start.10

commit v4 on v3

--- a/solution.py
+++ b/solution.py
@@ -186,16 +186,14 @@
     part_ref[...] = (INV_TEMP * neg_ref[...]).astype(BF16)
 
 
-def scatter_kernel(keep, bits, pull_ref, rid_ref, *outs):
+def scatter_kernel(others, pull_ref, rid_ref, *outs):
     ids = rid_ref[...]
-    for side, out_ref in enumerate(outs):
-        quarter = out_ref.shape[0]
-        rows = math.gcd(quarter, 512)
-        mine = (lax.axis_index("dp") >> bits[side]) & 1
-        start = (2 * side + (mine if keep else 1 - mine)) * quarter
+    for other, out_ref in zip(others, outs):
+        rows = math.gcd(out_ref.shape[0], 512)
+        start = (lax.axis_index("dp") ^ other) * out_ref.shape[0]
         for step in range(out_ref.shape[0] // rows):
             offset = (start + step * rows).astype(F32)
-            put = one_hot(iota((rows, ids.shape[1]), 0) == ids - offset)
+            put = one_hot(iota((rows, 1), 0) == ids - offset)
             part = jnp.dot(put, pull_ref[...], preferred_element_type=F32)
             out_ref[step * rows : (step + 1) * rows, :] = part.astype(BF16)
 
@@ -226,16 +224,18 @@
     grad_ref[...] = ((g_query - query_hat * along) * back_norm).astype(BF16)
 
 
-def update_kernel(rest, start_ref, table_ref, state_ref, *refs):
-    low_ref, high_ref, neg_ref, row_ref = refs[:4]
-    new_ref, new_state_ref = refs[-2:]
+def update_kernel(first, count, place_ref, table_ref, state_ref, *refs):
+    pieces, refs = refs[:count], refs[count:]
+    neg_ref, row_ref, new_ref, new_state_ref = *refs[:2], *refs[-2:]
     rows = table_ref.shape[0]
     step = pl.program_id(0)
-    half = pl.num_programs(0) // 2
-    offset = (update_block(rest, step, start_ref, half) * rows).astype(F32)
-    put = one_hot(iota((rows, row_ref.shape[1]), 0) == row_ref[...] - offset)
-    pull = jnp.where(step < half, low_ref[...].astype(F32), high_ref[...].astype(F32))
-    g_unit = pull + jnp.dot(put, neg_ref[...], preferred_element_type=F32)
+    per = pl.num_programs(0) // count
+    offset = (update_block(first, per, step, place_ref) * rows).astype(F32)
+    put = one_hot(iota((rows, 1), 0) == row_ref[...] - offset)
+    g_unit = pieces[0][...].astype(F32)
+    for spot in range(1, count):
+        g_unit = jnp.where(step >= spot * per, pieces[spot][...].astype(F32), g_unit)
+    g_unit = g_unit + jnp.dot(put, neg_ref[...], preferred_element_type=F32)
     table = table_ref[...]
     unit, back_norm = unit_rows(table)
     g_row = (g_unit - unit * jnp.sum(unit * g_unit, axis=1, keepdims=True)) * back_norm
@@ -244,9 +244,8 @@
     new_ref[...] = table - g_row * (LEARN_RATE * lax.rsqrt(state))
 
 
-def update_block(rest, step, start_ref, half):
-    low, high = start_ref[2 * rest], start_ref[2 * rest + 1]
-    return jnp.where(step < half, low + step, high + step - half)
+def update_block(first, per, step, place_ref):
+    return place_ref[first + step // per] + step % per
 
 
 def whole():
@@ -261,20 +260,8 @@
     return (left.astype(F32) + right.astype(F32)).astype(BF16)
 
 
-def halve(value, name, count, bit):
-    half = value.shape[0] // 2
-    mine = (lax.axis_index(name) >> bit) & 1
-    give = lax.dynamic_slice_in_dim(value, (1 - mine) * half, half, 0)
-    keep = lax.dynamic_slice_in_dim(value, mine * half, half, 0)
-    return add(keep, lax.ppermute(give, name, flip(count, bit)))
-
-
-def double(value, name, count, bit):
-    mine = (lax.axis_index(name) >> bit) & 1
-    got = lax.ppermute(value, name, flip(count, bit))
-    low = jnp.concatenate([value, got], axis=0)
-    high = jnp.concatenate([got, value], axis=0)
-    return jnp.where(mine == 0, low, high)
+def add(left, right):
+    return (left.astype(F32) + right.astype(F32)).astype(BF16)
 
 
 def to_digits(values, axis):
@@ -297,8 +284,7 @@
     neg_dev = neg_rows.shape[0]
     items = lax.axis_size("item")
     groups = lax.axis_size("dp")
-    bits = groups.bit_length() - 1
-    assert groups == 1 << bits and bits > 0
+    assert groups & (groups - 1) == 0 and groups > 1
     assert items & (items - 1) == 0 and items > 1
     capacity = 3 * examples // items
     slots = -(-capacity // 128) * 128
@@ -365,19 +351,18 @@
         name="norm",
     )(item_table)
     found = ()
-    for side in range(2):
-        start = side * items // 4
+    for start, count in ((0, 1), (1, items // 2 - 1)):
         found = (
             pl.pallas_call(
                 lambda *refs, start=start: find_kernel(start, *refs),
                 out_shape=jax.ShapeDtypeStruct((items * slots, width), BF16),
-                grid=(items // 4,),
+                grid=(count,),
                 in_specs=[whole(), whole()] + [anywhere] * len(found),
                 out_specs=pl.BlockSpec(
                     (2 * slots, width), lambda step, start=start: (start + step, 0)
                 ),
                 input_output_aliases={2: 0} if found else {},
-                cost_estimate=cost(2**32, 8 * table_rows * width),
+                cost_estimate=cost(count * 2**31, 8 * table_rows * width),
             )(rid, send, *found),
         )
     found = found[0]
@@ -409,36 +394,34 @@
         found.reshape(items, slots, width), "item", split_axis=0, concat_axis=0, tiled=True
     ).reshape(items * slots, width)
 
-    quarter = table_rows // 4
-    orders = [list(range(bits)), list(range(bits))[::-1]]
-    firsts = [(group >> order[0]) & 1 for order in orders]
-    starts = [2 * side * quarter for side in range(2)]
-
-    def scatter(keep):
-        bits_used = [order[0] for order in orders]
+    assert table_rows % groups == 0
+    quarter = table_rows // groups
+    ways = [[(at, at ^ other) for at in range(groups)] for other in range(groups)]
+
+    def scatter(others):
         return pl.pallas_call(
-            lambda *refs: scatter_kernel(keep, bits_used, *refs),
-            out_shape=(jax.ShapeDtypeStruct((quarter, width), BF16),) * 2,
+            lambda *refs: scatter_kernel(others, *refs),
+            out_shape=(jax.ShapeDtypeStruct((quarter, width), BF16),) * len(others),
             in_specs=[whole(), whole()],
-            out_specs=(whole(), whole()),
-            cost_estimate=cost(4 * items * slots * quarter * width, 4 * quarter * width),
-            name="keep" if keep else "give",
+            out_specs=(whole(),) * len(others),
+            cost_estimate=cost(
+                2 * len(others) * items * slots * quarter * width, 4 * quarter * width
+            ),
         )(pull, out_rid)
 
-    gives = scatter(False)
     gots = []
-    for side in range(2):
-        gots.append(lax.ppermute(gives[side], "dp", flip(groups, orders[side][0])))
-    keeps = scatter(True)
-    values, others = [], []
-    for side, order in enumerate(orders):
-        value = add(keeps[side], gots[side])
-        for level in range(1, bits):
-            value = halve(value, "dp", groups, order[level])
-        for level in range(bits - 1, 0, -1):
-            value = double(value, "dp", groups, order[level])
-        values.append(value)
-        others.append(lax.ppermute(value, "dp", flip(groups, order[0])))
+    near, far = list(range(1, groups - 1)), [groups - 1, 0]
+    gives = scatter(near) if near else ()
+    for other, give in zip(near, gives):
+        gots.append(lax.ppermute(give, "dp", ways[other]))
+    give, total = scatter(far)
+    gots.append(lax.ppermute(give, "dp", ways[groups - 1]))
+    total = total.astype(F32)
+    for got in gots:
+        total = total + got.astype(F32)
+    values = [total.astype(BF16)]
+    for other in range(1, groups):
+        values.append(lax.ppermute(values[0], "dp", ways[other]))
 
     neg_sum = neg_part.reshape(groups, items, neg_dev, width)
     for bit in range(items.bit_length() - 1):
@@ -448,8 +431,13 @@
         keep = lax.dynamic_index_in_dim(split, mine, 2, keepdims=False)
         neg_sum = add(keep, lax.ppermute(give, "item", flip(items, bit)))
     neg_sum = neg_sum.reshape(groups * neg_dev, width)
-    for bit in range(bits):
-        neg_sum = add(neg_sum, lax.ppermute(neg_sum, "dp", flip(groups, bit)))
+    neg_parts = [neg_sum]
+    for other in range(1, groups):
+        neg_parts.append(lax.ppermute(neg_sum, "dp", ways[other]))
+    neg_parts = [part.astype(F32) for part in neg_parts]
+    while len(neg_parts) > 1:
+        neg_parts = [low + high for low, high in zip(neg_parts[::2], neg_parts[1::2])]
+    neg_sum = neg_parts[0].astype(BF16)
     neg_spots = lax.dynamic_slice_in_dim(
         local_ids.reshape(groups, items, neg_dev), item, 1, 1
     ).reshape(1, groups * neg_dev)
@@ -457,43 +445,41 @@
     chunk = math.gcd(quarter, 512)
     per = quarter // chunk
     updated = ()
-    places = jnp.stack(
-        [
-            (start + (first ^ rest) * quarter) // chunk
-            for rest in range(2)
-            for start, first in zip(starts, firsts)
-        ]
-    )
-    for rest, pieces in enumerate((values, others)):
+    places = jnp.stack([(group ^ other) * per for other in range(groups)])
+    for first, last in ((0, 1), (1, groups - 1), (groups - 1, groups)):
+        pieces = values[first:last]
+        if not pieces:
+            continue
+        count = len(pieces)
         tall = pl.BlockSpec(
-            (chunk, width), lambda step, at, rest=rest: (update_block(rest, step, at, per), 0)
+            (chunk, width), lambda step, at, first=first: (update_block(first, per, step, at), 0)
         )
         flat = pl.BlockSpec(
-            (1, chunk), lambda step, at, rest=rest: (0, update_block(rest, step, at, per))
+            (1, chunk), lambda step, at, first=first: (0, update_block(first, per, step, at))
         )
         updated = pl.pallas_call(
-            lambda *refs, rest=rest: update_kernel(rest, *refs),
+            lambda *refs, first=first, count=count: update_kernel(first, count, *refs),
             out_shape=(
                 jax.ShapeDtypeStruct((table_rows, width), F32),
                 jax.ShapeDtypeStruct((1, table_rows), F32),
             ),
             grid_spec=pltpu.PrefetchScalarGridSpec(
                 num_scalar_prefetch=1,
-                grid=(2 * per,),
-                in_specs=[
-                    tall,
-                    flat,
-                    pl.BlockSpec((chunk, width), lambda step, _: (jnp.minimum(step, per - 1), 0)),
-                    pl.BlockSpec((chunk, width), lambda step, _: (jnp.maximum(step - per, 0), 0)),
-                    whole(),
-                    whole(),
-                    *[anywhere] * len(updated),
-                ],
+                grid=(count * per,),
+                in_specs=[tall, flat]
+                + [
+                    pl.BlockSpec(
+                        (chunk, width),
+                        lambda step, _, spot=spot: (jnp.clip(step - spot * per, 0, per - 1), 0),
+                    )
+                    for spot in range(count)
+                ]
+                + [whole(), whole()]
+                + [anywhere] * len(updated),
                 out_specs=(tall, flat),
             ),
-            input_output_aliases={7: 0, 8: 1} if updated else {},
+            input_output_aliases={5 + count: 0, 6 + count: 1} if updated else {},
             cost_estimate=cost(2**32, 5 * table_rows * width),
-            name="update_rest" if rest else "update_own",
         )(places, item_table, adagrad_state[None, :], *pieces, neg_sum, neg_spots, *updated)
     new_table, new_state = updated
 

time: 169 us -> 182 us (1.077)
  waiting for transfers between devices: 38 us -> 49.8 us
  Pallas kernels: 79.2 us -> 81.4 us
    ppermute x3, waiting for transfers between devices: 3.8 us -> 18.6 us  [on_device(): neg_sum = add(keep, lax.ppermute(give, 'item', flip(items, bit)))]
    ppermute x10 -> x9, waiting for transfers between devices: 12.8 us -> 9.9 us  [the longest x3 8.91 us: on_device(): values.append(lax.ppermute(values[0], 'dp', ways[other]))]
    ppermute x10 -> x9, starting transfers between devices: 7.76 us -> 10.6 us  [the longest x3 3.55 us: on_device(): neg_parts.append(lax.ppermute(neg_sum, 'dp', ways[other]))]
    ppermute x3, waiting for transfers between devices: 20.4 us -> 18.1 us  [on_device(): block = lax.ppermute(block, 'item', ring)]
    pallas_call x4 -> x5, Pallas kernels: 25.6 us -> 27.8 us  [the longest x3 16.5 us: on_device(): pl.pallas_call(lambda *refs, first=first, count=count: update_kernel(firs...]
    convert_element_type x9 -> x3, other arithmetic: 3.43 us -> 1.19 us  [add(): return (left.astype(F32) + right.astype(F32)).astype(BF16)]
    all_to_all x1, waiting for transfers between devices: 1.01 us -> 3.2 us  [to_all(): return lax.all_to_all(copies, name, split_axis=0, concat_axis=0, tiled=True)]
    convert_element_type x0 -> x2, other arithmetic: none -> 2.15 us  [the longest x1 1.46 us: on_device(): values = [total.astype(BF16)]]
  transfers between devices with their start and end apart: 25 -> 24, of which waited for: 8 -> 9; matrix products, arithmetic and copies ran while one was open for 9% -> 7% of each run, Pallas kernels for 43% -> 28%
where the time goes in v4:
time: 182 us; the launch traced here: 181 us
  Pallas kernels  81.4 us (45%)
  waiting for transfers between devices  49.8 us (27%)
  starting transfers between devices  32.6 us (18%)
  local copies, waits for them, and re-layouts  8.88 us (5%)
  other arithmetic  7.09 us (4%)
    ppermute x3, waiting for transfers between devices, on_device(): neg_sum = add(keep, lax.ppermute(give, 'item', flip(items, bit)))  18.6 us
    ppermute x3, waiting for transfers between devices, on_device(): block = lax.ppermute(block, 'item', ring)  18.1 us
    pallas_call x1, Pallas kernels, on_device(): pl.pallas_call(lambda *refs: owner_kernel(table_rows, *refs), out_shape=(...  17.1 us
    pallas_call x3, Pallas kernels, on_device(): pl.pallas_call(lambda *refs, first=first, count=count: update_kernel(firs...  16.5 us
    pallas_call x2, Pallas kernels, on_device(): pl.pallas_call(lambda *refs, start=start: find_kernel(start, *refs), out_...  13.4 us
    pallas_call x2, Pallas kernels, on_device(): pl.pallas_call(lambda *refs: home_kernel(table_rows, *refs), out_shape=(j...  12.9 us
    pallas_call x2, Pallas kernels, scatter(): pl.pallas_call(lambda *refs: scatter_kernel(others, *refs), out_shape=(ja...  11.3 us
    ppermute x3, waiting for transfers between devices, on_device(): values.append(lax.ppermute(values[0], 'dp', ways[other]))  8.91 us
  transfers between devices with their start and end apart: 24, of which 9 were waited for; matrix products, arithmetic and copies ran while one was open for 7% of the time, Pallas kernels for 28%

profile of v4, /device:TPU:0, one launch (start us, length us, event | category | flops | bytes accessed | tf_op | source)
XLA Modules:
  0.0 180.7 jit_solution(1032487065299200476)
XLA Ops:
  0.6 3.1 %collective-permute-start.1 = (bf16[1024,256]{1,0:T(8,128)(2,1)}, bf16[1024,256]{1,0:T(8,128)(2,1)S(1)}, u32[]{:S(2)}, u32[]{:S(2)}) collective-permute-start(bf16[1024,256]{1,0:T(8,128)(2,1)} %refs_0_.5), channel_id=1, source_target_pairs={{0,2},{1,3},{2,4},{3,5},{4,6},{5,7},{6,0},{7,1},{8,10},{9,11},{10,... | collective-permute-start | bytes 1572872 | tf_op jit(solution)/shard_map/ppermute | solution.py:302
  3.7 0.7 fusion.16
  4.4 0.7 broadcast_multiply_fusion
  5.1 0.7 fusion.9
  6.2 2.8 %gather_fusion = f32[48,256]{1,0:T(8,128)S(1)} fusion(f32[4096,256]{1,0:T(8,128)} %refs_1_.5, s32[1024]{0:T(1024)S(1)} %pad_clamp_fusion), kind=kCustom, calls=%fused_computation | custom fusion | bytes 98496 | tf_op jit(solution)/shard_map/gather | solution.py:313
  9.3 0.7 broadcast_in_dim.9
  10.1 3.9 %all-to-all-start = ((bf16[8,48,384]{2,1,0:T(8,128)(2,1)}), bf16[8,48,384]{2,1,0:T(8,128)(2,1)S(1)}, u32[]{:S(2)}, u32[]{:S(2)}) async-start(bf16[8,48,384]{2,1,0:T(8,128)(2,1)} %broadcast_in_dim.9), calls=%async_computation | async-start | bytes 589824 | tf_op jit(solution)/shard_map/all_to_all | solution.py:274
  14.4 6.7 %norm.1.refs_1_ = bf16[4096,256]{1,0:T(8,128)(2,1)} custom-call(f32[4096,256]{1,0:T(8,128)} %refs_1_.5), custom_call_target="tpu_custom_call" | custom-call | flops 4294967296 | bytes 6291456 | tf_op jit(solution)/shard_map/norm/pallas_call | solution.py:344
  21.1 3.2 %all-to-all-done = bf16[8,48,384]{2,1,0:T(8,128)(2,1)S(1)} async-done(((bf16[8,48,384]{2,1,0:T(8,128)(2,1)}), bf16[8,48,384]{2,1,0:T(8,128)(2,1)S(1)}, u32[]{:S(2)}, u32[]{:S(2)}) %all-to-all-start) | async-done | bytes 294944 | tf_op jit(solution)/shard_map/all_to_all | solution.py:274
  24.3 2.4 %collective-permute-start.9 = (bf16[384,384]{1,0:T(8,128)(2,1)S(1)}, bf16[384,384]{1,0:T(8,128)(2,1)}, u32[]{:S(2)}, u32[]{:S(2)}) collective-permute-start(bf16[384,384]{1,0:T(8,128)(2,1)S(1)} %bitcast.45), channel_id=1, source_target_pairs={{0,24},{8,16},{16,8},{24,0},{1,25},{9,17},{17,9},{25,1},{2,26},{10... | collective-permute-start | bytes 884744 | tf_op jit(solution)/shard_map/ppermute | solution.py:327
  28.2 0.6 fusion.6.gid_ref
  28.8 13.2 %collective-permute-done.3.refs_4_ = bf16[1024,256]{1,0:T(8,128)(2,1)S(1)} collective-permute-done((bf16[1024,256]{1,0:T(8,128)(2,1)S(1)}, bf16[1024,256]{1,0:T(8,128)(2,1)S(1)}, u32[]{:S(2)}, u32[]{:S(2)}) %collective-permute-start.3) | collective-permute-done | bytes 524320 | tf_op jit(solution)/shard_map/ppermute | solution.py:302
  42.1 3.4 %route.1 = (f32[8,1024]{1,0:T(8,128)}, s32[8,384]{1,0:T(8,128)}, f32[1,1024]{1,0:T(1,128)}) custom-call(s32[8,1024]{1,0:T(8,128)} %fusion.6.gid_ref, s32[1,1024]{1,0:T(1,128)} %bitcast.52, s32[1]{0:T(128)} %constant.120.clone.1.rows_ref), custom_call_target="tpu_custom_call" | custom-call | flops 4294967296 | bytes 6291456 | tf_op jit(solution)/shard_map/route/pallas_call | solution.py:330
  45.5 4.5 %shard_map.93.refs_2_ = bf16[3072,256]{1,0:T(8,128)(2,1)} custom-call(s32[8,384]{1,0:T(8,128)} %get-tuple-element.27.refs_0_.refs_13_, bf16[4096,256]{1,0:T(8,128)(2,1)} %norm.1.refs_1_), custom_call_target="tpu_custom_call" | custom-call | flops 2147483648 | bytes 8388608 | tf_op jit(solution)/shard_map/pallas_call | solution.py:356
  50.5 4.9 %collective-permute-done.5.refs_6_ = bf16[1024,256]{1,0:T(8,128)(2,1)S(1)} collective-permute-done((bf16[1024,256]{1,0:T(8,128)(2,1)S(1)}, bf16[1024,256]{1,0:T(8,128)(2,1)S(1)}, u32[]{:S(2)}, u32[]{:S(2)}) %collective-permute-start.5) | collective-permute-done | bytes 524320 | tf_op jit(solution)/shard_map/ppermute | solution.py:302
  55.4 8.9 %shard_map.94.refs_14_ = bf16[3072,256]{1,0:T(8,128)(2,1)} custom-call(s32[8,384]{1,0:T(8,128)} %get-tuple-element.27.refs_0_.refs_13_, bf16[4096,256]{1,0:T(8,128)(2,1)} %norm.1.refs_1_, bf16[3072,256]{1,0:T(8,128)(2,1)} %shard_map.93.refs_2_), custom_call_target="tpu_custom_call", output_to_operand_aliasing={{}: (2, {})} | custom-call | flops 6442450944 | bytes 8388608 | tf_op jit(solution)/shard_map/pallas_call | solution.py:356
  64.4 0.8 copy-done.10
  65.4 17.1 %owner.1 = (bf16[3072,256]{1,0:T(8,128)(2,1)}, f32[1,3072]{1,0:T(1,128)}, bf16[1536,256]{1,0:T(8,128)(2,1)}, f32[1,1536]{1,0:T(1,128)}, bf16[1536,384]{1,0:T(8,128)(2,1)}) custom-call(bf16[1024,256]{1,0:T(8,128)(2,1)} %refs_0_.5, bf16[1024,256]{1,0:T(8,128)(2,1)} %copy-done.7, bf16[1024,256]{1,0:T(8,128)(2,1)} %copy-done.6, bf16[1024,256]{1,0:T(8,128)(2,1)} %copy-done.10, ...), custom_call_target="tpu_custom_call" | custom-call | flops 9663676416 | bytes 3145728 | tf_op jit(solution)/shard_map/owner/pallas_call | solution.py:371
  82.5 1.0 dynamic-slice_bitcast_fusion
  83.9 0.6 pad_add_fusion.refs_0_
  84.5 3.8 %all-to-all-start.1 = ((bf16[8,384,256]{2,1,0:T(8,128)(2,1)}), bf16[8,384,256]{2,1,0:T(8,128)(2,1)S(1)}, u32[]{:S(2)}, u32[]{:S(2)}) async-start(bf16[8,384,256]{2,1,0:T(8,128)(2,1)} %bitcast.6), calls=%async_computation.1 | async-start | bytes 3145728 | tf_op jit(solution)/shard_map/all_to_all | solution.py:393
  88.4 5.7 %shard_map.98 = (bf16[1024,256]{1,0:T(8,128)(2,1)}, bf16[1024,256]{1,0:T(8,128)(2,1)}) custom-call(bf16[3072,256]{1,0:T(8,128)(2,1)} %get-tuple-element.35.refs_0_, f32[1,3072]{1,0:T(1,128)} %get-tuple-element.36.refs_1_), custom_call_target="tpu_custom_call" | custom-call | flops 3221225472 | bytes 1048576 | tf_op jit(solution)/shard_map/pallas_call | solution.py:402
  94.1 1.5 collective-permute-start.10
  95.6 1.5 collective-permute-start.11
  97.1 1.1 fusion
  98.2 1.8 collective-permute-start.15
  100.0 5.6 %shard_map.97 = (bf16[1024,256]{1,0:T(8,128)(2,1)}, bf16[1024,256]{1,0:T(8,128)(2,1)}) custom-call(bf16[3072,256]{1,0:T(8,128)(2,1)} %get-tuple-element.35.refs_0_, f32[1,3072]{1,0:T(1,128)} %get-tuple-element.36.refs_1_), custom_call_target="tpu_custom_call" | custom-call | flops 3221225472 | bytes 1048576 | tf_op jit(solution)/shard_map/pallas_call | solution.py:402
  106.1 12.6 %collective-permute-done.15 = bf16[4,2,48,256]{3,2,1,0:T(8,128)(2,1)S(1)} collective-permute-done((bf16[4,2,48,256]{3,2,1,0:T(8,128)(2,1)S(1)}, bf16[4,2,48,256]{3,2,1,0:T(8,128)(2,1)S(1)}, u32[]{:S(2)}, u32[]{:S(2)}) %collective-permute-start.15) | collective-permute-done | bytes 196640 | tf_op jit(solution)/shard_map/ppermute | solution.py:432
  118.8 4.6 %collective-permute-start.16 = (bf16[4,1,48,256]{3,2,1,0:T(8,128)(2,1)S(1)}, bf16[4,1,48,256]{3,2,1,0:T(8,128)(2,1)S(1)}, u32[]{:S(2)}, u32[]{:S(2)}) collective-permute-start(bf16[4,1,48,256]{3,2,1,0:T(8,128)(2,1)S(1)} %constant_dynamic-slice_fusion.1), channel_id=1, source_target_pairs={{0,4},{1,5},{2,6},{3,7},{4,0},{5,1},{6,2},{7,3},{8,12},{9,13},{10,... | collective-permute-start | bytes 294920 | tf_op jit(solution)/shard_map/ppermute | solution.py:432
  123.4 0.6 reshape.126.refs_5_.refs_6_
  124.0 6.0 %collective-permute-done.16 = bf16[4,1,48,256]{3,2,1,0:T(8,128)(2,1)S(1)} collective-permute-done((bf16[4,1,48,256]{3,2,1,0:T(8,128)(2,1)S(1)}, bf16[4,1,48,256]{3,2,1,0:T(8,128)(2,1)S(1)}, u32[]{:S(2)}, u32[]{:S(2)}) %collective-permute-start.16) | collective-permute-done | bytes 98336 | tf_op jit(solution)/shard_map/ppermute | solution.py:432
  130.1 1.6 collective-permute-start.18
  131.7 1.5 collective-permute-start.17
  133.6 1.5 add_convert_fusion.refs_3_
  135.1 1.6 collective-permute-start.21
  136.7 1.5 collective-permute-start.20
  138.7 1.0 collective-permute-done.19
  139.7 0.7 add_convert_fusion.1.refs_4_.refs_5_
  140.4 4.7 %shard_map.99 = (f32[4096,256]{1,0:T(8,128)}, f32[1,4096]{1,0:T(1,128)}) custom-call(s32[4]{0:T(128)} %pad_add_fusion.refs_0_, f32[4096,256]{1,0:T(8,128)} %refs_1_.5, f32[1,4096]{1,0:T(1,128)} %bitcast.57, bf16[1024,256]{1,0:T(8,128)(2,1)} %copy-done.2, bf16[192,256]{1,0:T(8,128)(2,1)} %add_convert_fusion.1.refs_4_.refs_5_, f32[1,192]{1,0:T(1,128)} %reshape.126.refs_5_.refs_6_), custom_call_target="tpu_custom_call" | custom-call | flops 4294967296 | bytes 5242880 | tf_op jit(solution)/shard_map/pallas_call | solution.py:460
  145.0 5.4 %collective-permute-done.21.refs_4_ = bf16[1024,256]{1,0:T(8,128)(2,1)S(1)} collective-permute-done((bf16[1024,256]{1,0:T(8,128)(2,1)S(1)}, bf16[1024,256]{1,0:T(8,128)(2,1)S(1)}, u32[]{:S(2)}, u32[]{:S(2)}) %collective-permute-start.21) | collective-permute-done | bytes 524320 | tf_op jit(solution)/shard_map/ppermute | solution.py:424
  150.4 1.2 collective-permute-done.20.refs_3_
  151.6 7.2 %shard_map.100 = (f32[4096,256]{1,0:T(8,128)}, f32[1,4096]{1,0:T(1,128)}) custom-call(s32[4]{0:T(128)} %pad_add_fusion.refs_0_, f32[4096,256]{1,0:T(8,128)} %refs_1_.5, f32[1,4096]{1,0:T(1,128)} %bitcast.58, bf16[1024,256]{1,0:T(8,128)(2,1)} %collective-permute-done.20.refs_3_, ...), custom_call_target="tpu_custom_call", output_to_operand_aliasing={{0}: (7, {}), {1}: (8, {})} | custom-call | flops 4294967296 | bytes 5242880 | tf_op jit(solution)/shard_map/pallas_call | solution.py:460
  158.8 2.3 %collective-permute-done.13.refs_3_ = bf16[1024,256]{1,0:T(8,128)(2,1)S(1)} collective-permute-done((bf16[1024,256]{1,0:T(8,128)(2,1)S(1)}, bf16[1024,256]{1,0:T(8,128)(2,1)S(1)}, u32[]{:S(2)}, u32[]{:S(2)}) %collective-permute-start.13) | collective-permute-done | bytes 524320 | tf_op jit(solution)/shard_map/ppermute | solution.py:424
  161.1 0.8 copy-done.12
  161.9 4.7 %shard_map.101 = (f32[4096,256]{1,0:T(8,128)}, f32[1,4096]{1,0:T(1,128)}) custom-call(s32[4]{0:T(128)} %pad_add_fusion.refs_0_, f32[4096,256]{1,0:T(8,128)} %refs_1_.5, f32[1,4096]{1,0:T(1,128)} %bitcast.59, bf16[1024,256]{1,0:T(8,128)(2,1)} %copy-done.12, ...), custom_call_target="tpu_custom_call", output_to_operand_aliasing={{0}: (6, {}), {1}: (7, {})} | custom-call | flops 4294967296 | bytes 5242880 | tf_op jit(solution)/shard_map/pallas_call | solution.py:460
  166.6 1.2 copy-done
  167.8 6.4 %shard_map.95 = (bf16[1024,256]{1,0:T(8,128)(2,1)}, f32[1,1024]{1,0:T(1,128)}) custom-call(bf16[1024,256]{1,0:T(8,128)(2,1)} %refs_0_.5, f32[1,1024]{1,0:T(1,128)} %get-tuple-element.26.refs_1_, s32[1,1024]{1,0:T(1,128)} %bitcast.53, bf16[3072,256]{1,0:T(8,128)(2,1)} %bitcast.39, bf16[1536,384]{1,0:T(8,128)(2,1)} %get-tuple-element.29.refs_4_, ...), custom_call_target="tpu_custom_call" | custom-call | flops 4294967296 | bytes 3145728 | tf_op jit(solution)/shard_map/pallas_call | solution.py:492
  174.2 6.5 %shard_map.96 = (bf16[1024,256]{1,0:T(8,128)(2,1)}, f32[1,1024]{1,0:T(1,128)}) custom-call(bf16[1024,256]{1,0:T(8,128)(2,1)} %refs_0_.5, f32[1,1024]{1,0:T(1,128)} %get-tuple-element.26.refs_1_, s32[1,1024]{1,0:T(1,128)} %bitcast.54, bf16[3072,256]{1,0:T(8,128)(2,1)} %bitcast.40, ...), custom_call_target="tpu_custom_call", output_to_operand_aliasing={{0}: (6, {}), {1}: (7, {})} | custom-call | flops 4294967296 | bytes 3145728 | tf_op jit(solution)/shard_map/pallas_call | solution.py:492
  (74 shorter events, 5.4 us)
Async XLA Ops:
  0.6 27.2 %collective-permute-start.1 = (bf16[1024,256]{1,0:T(8,128)(2,1)}, bf16[1024,256]{1,0:T(8,128)(2,1)S(1)}, u32[]{:S(2)}, u32[]{:S(2)}) collective-permute-start(bf16[1024,256]{1,0:T(8,128)(2,1)} %refs_0_.5), channel_id=1, source_target_pairs={{0,2},{1,3},{2,4},{3,5},{4,6},{5,7},{6,0},{7,1},{8,10},{9,11},{10,... | collective-permute-start | bytes 1572872 | tf_op jit(solution)/shard_map/ppermute | solution.py:302
  5.8 15.3 %copy-start.4 = (s32[1024]{0:T(1024)}, s32[1024]{0:T(1024)S(1)}, u32[]{:S(2)}) copy-start(s32[1024]{0:T(1024)S(1)} %get-tuple-element.49) | copy-start | bytes 12292
  10.1 14.3 %all-to-all-start = ((bf16[8,48,384]{2,1,0:T(8,128)(2,1)}), bf16[8,48,384]{2,1,0:T(8,128)(2,1)S(1)}, u32[]{:S(2)}, u32[]{:S(2)}) async-start(bf16[8,48,384]{2,1,0:T(8,128)(2,1)} %broadcast_in_dim.9), calls=%async_computation | async-start | bytes 589824 | tf_op jit(solution)/shard_map/all_to_all | solution.py:274
  13.9 36.0 %collective-permute-start = (bf16[1024,256]{1,0:T(8,128)(2,1)}, bf16[1024,256]{1,0:T(8,128)(2,1)S(1)}, u32[]{:S(2)}, u32[]{:S(2)}) collective-permute-start(bf16[1024,256]{1,0:T(8,128)(2,1)} %refs_0_.5), channel_id=1, source_target_pairs={{0,1},{1,0},{2,3},{3,2},{4,5},{5,4},{6,7},{7,6},{8,9},{9,8},{10,11... | collective-permute-start | bytes 1572872 | tf_op jit(solution)/shard_map/ppermute | solution.py:303
  24.3 21.2 %copy-start.3 = (bf16[8,48,384]{2,1,0:T(8,128)(2,1)}, bf16[8,48,384]{2,1,0:T(8,128)(2,1)S(1)}, u32[]{:S(2)}) copy-start(bf16[8,48,384]{2,1,0:T(8,128)(2,1)S(1)} %all-to-all-done) | copy-start | bytes 884740
  24.3 25.7 %collective-permute-start.9 = (bf16[384,384]{1,0:T(8,128)(2,1)S(1)}, bf16[384,384]{1,0:T(8,128)(2,1)}, u32[]{:S(2)}, u32[]{:S(2)}) collective-permute-start(bf16[384,384]{1,0:T(8,128)(2,1)S(1)} %bitcast.45), channel_id=1, source_target_pairs={{0,24},{8,16},{16,8},{24,0},{1,25},{9,17},{17,9},{25,1},{2,26},{10... | collective-permute-start | bytes 884744 | tf_op jit(solution)/shard_map/ppermute | solution.py:327
  26.8 37.5 %collective-permute-start.8 = (bf16[384,384]{1,0:T(8,128)(2,1)S(1)}, bf16[384,384]{1,0:T(8,128)(2,1)}, u32[]{:S(2)}, u32[]{:S(2)}) collective-permute-start(bf16[384,384]{1,0:T(8,128)(2,1)S(1)} %bitcast.46), channel_id=1, source_target_pairs={{0,16},{8,24},{16,0},{24,8},{1,17},{9,25},{17,1},{25,9},{2,18},{10... | collective-permute-start | bytes 884744 | tf_op jit(solution)/shard_map/ppermute | solution.py:327
  27.3 37.0 %collective-permute-start.7 = (bf16[384,384]{1,0:T(8,128)(2,1)S(1)}, bf16[384,384]{1,0:T(8,128)(2,1)}, u32[]{:S(2)}, u32[]{:S(2)}) collective-permute-start(bf16[384,384]{1,0:T(8,128)(2,1)S(1)} %bitcast.47), channel_id=1, source_target_pairs={{0,8},{8,0},{16,24},{24,16},{1,9},{9,1},{17,25},{25,17},{2,10},{10... | collective-permute-start | bytes 884744 | tf_op jit(solution)/shard_map/ppermute | solution.py:327
  27.8 22.1 %copy-start.6 = (bf16[1024,256]{1,0:T(8,128)(2,1)}, bf16[1024,256]{1,0:T(8,128)(2,1)S(1)}, u32[]{:S(2)}) copy-start(bf16[1024,256]{1,0:T(8,128)(2,1)S(1)} %collective-permute-done.1.refs_2_) | copy-start | bytes 1572868
  27.8 14.2 %collective-permute-start.3 = (bf16[1024,256]{1,0:T(8,128)(2,1)S(1)}, bf16[1024,256]{1,0:T(8,128)(2,1)S(1)}, u32[]{:S(2)}, u32[]{:S(2)}) collective-permute-start(bf16[1024,256]{1,0:T(8,128)(2,1)S(1)} %collective-permute-done.1.refs_2_), channel_id=1, source_target_pairs={{0,2},{1,3},{2,4},{3,5},{4,6},{5,7},{6,0},{7,1},{8,10},{9,11},{10,... | collective-permute-start | bytes 1572872 | tf_op jit(solution)/shard_map/ppermute | solution.py:302
  42.0 8.0 %copy-start.8 = (bf16[1024,256]{1,0:T(8,128)(2,1)}, bf16[1024,256]{1,0:T(8,128)(2,1)S(1)}, u32[]{:S(2)}) copy-start(bf16[1024,256]{1,0:T(8,128)(2,1)S(1)} %collective-permute-done.3.refs_4_) | copy-start | bytes 1572868
  42.1 13.4 %collective-permute-start.5 = (bf16[1024,256]{1,0:T(8,128)(2,1)S(1)}, bf16[1024,256]{1,0:T(8,128)(2,1)S(1)}, u32[]{:S(2)}, u32[]{:S(2)}) collective-permute-start(bf16[1024,256]{1,0:T(8,128)(2,1)S(1)} %collective-permute-done.3.refs_4_), channel_id=1, source_target_pairs={{0,2},{1,3},{2,4},{3,5},{4,6},{5,7},{6,0},{7,1},{8,10},{9,11},{10,... | collective-permute-start | bytes 1572872 | tf_op jit(solution)/shard_map/ppermute | solution.py:302
  50.0 14.4 %copy-start.7 = (bf16[1024,256]{1,0:T(8,128)(2,1)}, bf16[1024,256]{1,0:T(8,128)(2,1)S(1)}, u32[]{:S(2)}) copy-start(bf16[1024,256]{1,0:T(8,128)(2,1)S(1)} %collective-permute-done.refs_1_) | copy-start | bytes 1572868
  50.0 14.4 %collective-permute-start.2 = (bf16[1024,256]{1,0:T(8,128)(2,1)S(1)}, bf16[1024,256]{1,0:T(8,128)(2,1)S(1)}, u32[]{:S(2)}, u32[]{:S(2)}) collective-permute-start(bf16[1024,256]{1,0:T(8,128)(2,1)S(1)} %collective-permute-done.1.refs_2_), channel_id=1, source_target_pairs={{0,1},{1,0},{2,3},{3,2},{4,5},{5,4},{6,7},{7,6},{8,9},{9,8},{10,11... | collective-permute-start | bytes 1572872 | tf_op jit(solution)/shard_map/ppermute | solution.py:303
  50.1 14.3 %collective-permute-start.4 = (bf16[1024,256]{1,0:T(8,128)(2,1)S(1)}, bf16[1024,256]{1,0:T(8,128)(2,1)S(1)}, u32[]{:S(2)}, u32[]{:S(2)}) collective-permute-start(bf16[1024,256]{1,0:T(8,128)(2,1)S(1)} %collective-permute-done.3.refs_4_), channel_id=1, source_target_pairs={{0,1},{1,0},{2,3},{3,2},{4,5},{5,4},{6,7},{7,6},{8,9},{9,8},{10,11... | collective-permute-start | bytes 1572872 | tf_op jit(solution)/shard_map/ppermute | solution.py:303
  55.4 8.9 %copy-start.9 = (bf16[1024,256]{1,0:T(8,128)(2,1)}, bf16[1024,256]{1,0:T(8,128)(2,1)S(1)}, u32[]{:S(2)}) copy-start(bf16[1024,256]{1,0:T(8,128)(2,1)S(1)} %collective-permute-done.5.refs_6_) | copy-start | bytes 1572868
  55.4 9.0 %collective-permute-start.6 = (bf16[1024,256]{1,0:T(8,128)(2,1)S(1)}, bf16[1024,256]{1,0:T(8,128)(2,1)}, u32[]{:S(2)}, u32[]{:S(2)}) collective-permute-start(bf16[1024,256]{1,0:T(8,128)(2,1)S(1)} %collective-permute-done.5.refs_6_), channel_id=1, source_target_pairs={{0,1},{1,0},{2,3},{3,2},{4,5},{5,4},{6,7},{7,6},{8,9},{9,8},{10,11... | collective-permute-start | bytes 1572872 | tf_op jit(solution)/shard_map/ppermute | solution.py:303
  64.4 0.8 copy-start.10
  64.4 1.0 copy-start.11
  82.5 5.8 %copy-start.5 = (f32[1,1536]{1,0:T(1,128)S(1)}, f32[1,1536]{1,0:T(1,128)}, u32[]{:S(2)}) copy-start(f32[1,1536]{1,0:T(1,128)} %get-tuple-element.30.refs_5_) | copy-start | bytes 18436
  83.5 13.6 %collective-permute-start.14 = (bf16[4,4,48,256]{3,2,1,0:T(8,128)(2,1)S(1)}, bf16[4,4,48,256]{3,2,1,0:T(8,128)(2,1)}, u32[]{:S(2)}, u32[]{:S(2)}) collective-permute-start(bf16[4,4,48,256]{3,2,1,0:T(8,128)(2,1)S(1)} %dynamic-slice_bitcast_fusion), channel_id=1, source_target_pairs={{0,1},{1,0},{2,3},{3,2},{4,5},{5,4},{6,7},{7,6},{8,9},{9,8},{10,11... | collective-permute-start | bytes 1179656 | tf_op jit(solution)/shard_map/ppermute | solution.py:432
  84.5 82.1 %all-to-all-start.1 = ((bf16[8,384,256]{2,1,0:T(8,128)(2,1)}), bf16[8,384,256]{2,1,0:T(8,128)(2,1)S(1)}, u32[]{:S(2)}, u32[]{:S(2)}) async-start(bf16[8,384,256]{2,1,0:T(8,128)(2,1)} %bitcast.6), calls=%async_computation.1 | async-start | bytes 3145728 | tf_op jit(solution)/shard_map/all_to_all | solution.py:393
  88.4 8.7 %copy-start.1 = (bf16[1536,256]{1,0:T(8,128)(2,1)S(1)}, bf16[1536,256]{1,0:T(8,128)(2,1)}, u32[]{:S(2)}) copy-start(bf16[1536,256]{1,0:T(8,128)(2,1)} %get-tuple-element.41) | copy-start | bytes 2359300
  94.1 39.0 %collective-permute-start.10 = (bf16[1024,256]{1,0:T(8,128)(2,1)}, bf16[1024,256]{1,0:T(8,128)(2,1)S(1)}, u32[]{:S(2)}, u32[]{:S(2)}) collective-permute-start(bf16[1024,256]{1,0:T(8,128)(2,1)} %get-tuple-element.38), channel_id=1, source_target_pairs={{0,8},{8,0},{16,24},{24,16},{1,9},{9,1},{17,25},{25,17},{2,10},{10... | collective-permute-start | bytes 1572872 | tf_op jit(solution)/shard_map/ppermute | solution.py:416
  95.6 38.1 %collective-permute-start.11 = (bf16[1024,256]{1,0:T(8,128)(2,1)}, bf16[1024,256]{1,0:T(8,128)(2,1)}, u32[]{:S(2)}, u32[]{:S(2)}) collective-permute-start(bf16[1024,256]{1,0:T(8,128)(2,1)} %get-tuple-element.39), channel_id=1, source_target_pairs={{0,16},{8,24},{16,0},{24,8},{1,17},{9,25},{17,1},{25,9},{2,18},{10... | collective-permute-start | bytes 1572872 | tf_op jit(solution)/shard_map/ppermute | solution.py:416
  98.2 20.5 %collective-permute-start.15 = (bf16[4,2,48,256]{3,2,1,0:T(8,128)(2,1)S(1)}, bf16[4,2,48,256]{3,2,1,0:T(8,128)(2,1)S(1)}, u32[]{:S(2)}, u32[]{:S(2)}) collective-permute-start(bf16[4,2,48,256]{3,2,1,0:T(8,128)(2,1)S(1)} %dynamic-slice_bitcast_fusion.1), channel_id=1, source_target_pairs={{0,2},{1,3},{2,0},{3,1},{4,6},{5,7},{6,4},{7,5},{8,10},{9,11},{10,... | collective-permute-start | bytes 589832 | tf_op jit(solution)/shard_map/ppermute | solution.py:432
  105.6 28.0 %collective-permute-start.12 = (bf16[1024,256]{1,0:T(8,128)(2,1)}, bf16[1024,256]{1,0:T(8,128)(2,1)S(1)}, u32[]{:S(2)}, u32[]{:S(2)}) collective-permute-start(bf16[1024,256]{1,0:T(8,128)(2,1)} %get-tuple-element.40), channel_id=1, source_target_pairs={{0,24},{8,16},{16,8},{24,0},{1,25},{9,17},{17,9},{25,1},{2,26},{10... | collective-permute-start | bytes 1572872 | tf_op jit(solution)/shard_map/ppermute | solution.py:418
  118.8 11.3 %collective-permute-start.16 = (bf16[4,1,48,256]{3,2,1,0:T(8,128)(2,1)S(1)}, bf16[4,1,48,256]{3,2,1,0:T(8,128)(2,1)S(1)}, u32[]{:S(2)}, u32[]{:S(2)}) collective-permute-start(bf16[4,1,48,256]{3,2,1,0:T(8,128)(2,1)S(1)} %constant_dynamic-slice_fusion.1), channel_id=1, source_target_pairs={{0,4},{1,5},{2,6},{3,7},{4,0},{5,1},{6,2},{7,3},{8,12},{9,13},{10,... | collective-permute-start | bytes 294920 | tf_op jit(solution)/shard_map/ppermute | solution.py:432
  130.1 8.1 %collective-permute-start.18 = (bf16[192,256]{1,0:T(8,128)(2,1)S(1)}, bf16[192,256]{1,0:T(8,128)(2,1)S(1)}, u32[]{:S(2)}, u32[]{:S(2)}) collective-permute-start(bf16[192,256]{1,0:T(8,128)(2,1)S(1)} %bitcast.49), channel_id=1, source_target_pairs={{0,16},{8,24},{16,0},{24,8},{1,17},{9,25},{17,1},{25,9},{2,18},{10... | collective-permute-start | bytes 294920 | tf_op jit(solution)/shard_map/ppermute | solution.py:436
  131.7 7.0 %collective-permute-start.17 = (bf16[192,256]{1,0:T(8,128)(2,1)S(1)}, bf16[192,256]{1,0:T(8,128)(2,1)S(1)}, u32[]{:S(2)}, u32[]{:S(2)}) collective-permute-start(bf16[192,256]{1,0:T(8,128)(2,1)S(1)} %bitcast.50), channel_id=1, source_target_pairs={{0,8},{8,0},{16,24},{24,16},{1,9},{9,1},{17,25},{25,17},{2,10},{10... | collective-permute-start | bytes 294920 | tf_op jit(solution)/shard_map/ppermute | solution.py:436
  133.2 6.5 %collective-permute-start.19 = (bf16[192,256]{1,0:T(8,128)(2,1)S(1)}, bf16[192,256]{1,0:T(8,128)(2,1)S(1)}, u32[]{:S(2)}, u32[]{:S(2)}) collective-permute-start(bf16[192,256]{1,0:T(8,128)(2,1)S(1)} %bitcast.51), channel_id=1, source_target_pairs={{0,24},{8,16},{16,8},{24,0},{1,25},{9,17},{17,9},{25,1},{2,26},{10... | collective-permute-start | bytes 294920 | tf_op jit(solution)/shard_map/ppermute | solution.py:436
  135.1 5.3 %copy-start.2 = (bf16[1024,256]{1,0:T(8,128)(2,1)}, bf16[1024,256]{1,0:T(8,128)(2,1)S(1)}, u32[]{:S(2)}) copy-start(bf16[1024,256]{1,0:T(8,128)(2,1)S(1)} %add_convert_fusion.refs_3_) | copy-start | bytes 1572868
  135.1 15.3 %collective-permute-start.21 = (bf16[1024,256]{1,0:T(8,128)(2,1)S(1)}, bf16[1024,256]{1,0:T(8,128)(2,1)S(1)}, u32[]{:S(2)}, u32[]{:S(2)}) collective-permute-start(bf16[1024,256]{1,0:T(8,128)(2,1)S(1)} %add_convert_fusion.refs_3_), channel_id=1, source_target_pairs={{0,16},{8,24},{16,0},{24,8},{1,17},{9,25},{17,1},{25,9},{2,18},{10... | collective-permute-start | bytes 1572872 | tf_op jit(solution)/shard_map/ppermute | solution.py:424
  136.7 14.9 %collective-permute-start.20 = (bf16[1024,256]{1,0:T(8,128)(2,1)S(1)}, bf16[1024,256]{1,0:T(8,128)(2,1)}, u32[]{:S(2)}, u32[]{:S(2)}) collective-permute-start(bf16[1024,256]{1,0:T(8,128)(2,1)S(1)} %add_convert_fusion.refs_3_), channel_id=1, source_target_pairs={{0,8},{8,0},{16,24},{24,16},{1,9},{9,1},{17,25},{25,17},{2,10},{10... | collective-permute-start | bytes 1572872 | tf_op jit(solution)/shard_map/ppermute | solution.py:424
  138.2 22.9 %collective-permute-start.13 = (bf16[1024,256]{1,0:T(8,128)(2,1)S(1)}, bf16[1024,256]{1,0:T(8,128)(2,1)S(1)}, u32[]{:S(2)}, u32[]{:S(2)}) collective-permute-start(bf16[1024,256]{1,0:T(8,128)(2,1)S(1)} %add_convert_fusion.refs_3_), channel_id=1, source_target_pairs={{0,24},{8,16},{16,8},{24,0},{1,25},{9,17},{17,9},{25,1},{2,26},{10... | collective-permute-start | bytes 1572872 | tf_op jit(solution)/shard_map/ppermute | solution.py:424
  150.4 1.2 copy-start.13
  161.1 0.8 copy-start.12
  166.6 1.2 copy-start

commit v5 on v4

--- a/solution.py
+++ b/solution.py
@@ -17,7 +17,7 @@
 
 
 def unit_rows(matrix):
-    back_norm = 1.0 / jnp.sqrt(jnp.sum(matrix * matrix, axis=-1, keepdims=True) + EPSILON)
+    back_norm = lax.rsqrt(jnp.sum(matrix * matrix, axis=-1, keepdims=True) + EPSILON)
     return (matrix * back_norm, back_norm)
 
 
@@ -103,12 +103,12 @@
     queries, refs = refs[: 2 * pairs], refs[2 * pairs :]
     columns, refs = refs[:groups], refs[groups:]
     rank_ref, rid_ref, found_any, refs = *refs[:3], refs[3:]
-    pull_ref, outrid_ref, part_ref, ids_ref, negs_ref, refs = *refs[:5], refs[5:]
+    pull_ref, outrid_ref, part_ref, ids_ref, negs_ref, spots_ref, refs = *refs[:6], refs[6:]
     held, found, nsub, exps, neg_ref, copy_sem = refs
     slots = rid_ref.shape[1]
     examples, width = held.shape[1], held.shape[2]
     negs = negs_ref.shape[0]
-    chunk = math.gcd(negs, 256)
+    chunk = math.gcd(negs, 768)
     both = 2 * slots
     size = negs // groups
     copies = [
@@ -139,6 +139,15 @@
         copy.wait()
     nsub[...] = jnp.broadcast_to(neg_ids(negs_ref[:, width:]) - base, nsub.shape)
     ids_ref[...] = jnp.transpose(nsub[...])[:1, :]
+    mine = negs // groups // (2 * pairs)
+    own = [
+        nsub[rows_at(group * 2 * pairs + lax.axis_index("item"), mine), :]
+        for group in range(groups)
+    ]
+    spare = spots_ref.shape[1] - groups * mine
+    if spare:
+        own.append(jnp.full((spare, 128), -1.0, F32))
+    spots_ref[...] = jnp.transpose(jnp.concatenate(own, axis=0))[:1, :]
 
     def one_pair(pair, fresh):
         rid = outrid_ref[:, rows_at(pair, both)]
@@ -189,7 +198,7 @@
 def scatter_kernel(others, pull_ref, rid_ref, *outs):
     ids = rid_ref[...]
     for other, out_ref in zip(others, outs):
-        rows = math.gcd(out_ref.shape[0], 512)
+        rows = math.gcd(out_ref.shape[0], 1024)
         start = (lax.axis_index("dp") ^ other) * out_ref.shape[0]
         for step in range(out_ref.shape[0] // rows):
             offset = (start + step * rows).astype(F32)
@@ -231,7 +240,7 @@
     step = pl.program_id(0)
     per = pl.num_programs(0) // count
     offset = (update_block(first, per, step, place_ref) * rows).astype(F32)
-    put = one_hot(iota((rows, 1), 0) == row_ref[...] - offset)
+    put = one_hot(iota((rows, 1), 0) == row_ref[:, : neg_ref.shape[0]] - offset)
     g_unit = pieces[0][...].astype(F32)
     for spot in range(1, count):
         g_unit = jnp.where(step >= spot * per, pieces[spot][...].astype(F32), g_unit)
@@ -368,7 +377,7 @@
     found = found[0]
 
     blocks = [block for step in steps for block in step]
-    pull, out_rid, neg_part, local_ids, all_negs = pl.pallas_call(
+    pull, out_rid, neg_part, local_ids, all_negs, neg_spots = pl.pallas_call(
         lambda *refs: owner_kernel(table_rows, *refs),
         out_shape=(
             jax.ShapeDtypeStruct((items * slots, width), BF16),
@@ -376,9 +385,10 @@
             jax.ShapeDtypeStruct((negs, width), BF16),
             jax.ShapeDtypeStruct((1, negs), F32),
             jax.ShapeDtypeStruct((negs, width + side_width), BF16),
+            jax.ShapeDtypeStruct((1, -(-groups * neg_dev // 128) * 128), F32),
         ),
         in_specs=[anywhere] * (items + groups) + [whole(), whole(), anywhere],
-        out_specs=(whole(),) * 5,
+        out_specs=(whole(),) * 6,
         scratch_shapes=[
             pltpu.VMEM((items, examples, width), BF16),
             pltpu.VMEM((items * slots, width), BF16),
@@ -420,8 +430,17 @@
     for got in gots:
         total = total + got.astype(F32)
     values = [total.astype(BF16)]
-    for other in range(1, groups):
+    for other in near:
         values.append(lax.ppermute(values[0], "dp", ways[other]))
+    tails = []
+    if near:
+        middle = quarter // 2
+        for other, half in ((near[0], slice(0, middle)), (near[-1], slice(middle, quarter))):
+            tails.append(
+                lax.ppermute(values[other][half], "dp", ways[(groups - 1) ^ other])
+            )
+    else:
+        tails.append(lax.ppermute(values[0], "dp", ways[groups - 1]))
 
     neg_sum = neg_part.reshape(groups, items, neg_dev, width)
     for bit in range(items.bit_length() - 1):
@@ -438,24 +457,22 @@
     while len(neg_parts) > 1:
         neg_parts = [low + high for low, high in zip(neg_parts[::2], neg_parts[1::2])]
     neg_sum = neg_parts[0].astype(BF16)
-    neg_spots = lax.dynamic_slice_in_dim(
-        local_ids.reshape(groups, items, neg_dev), item, 1, 1
-    ).reshape(1, groups * neg_dev)
-
-    chunk = math.gcd(quarter, 512)
-    per = quarter // chunk
     updated = ()
-    places = jnp.stack([(group ^ other) * per for other in range(groups)])
-    for first, last in ((0, 1), (1, groups - 1), (groups - 1, groups)):
-        pieces = values[first:last]
+    size = quarter // len(tails)
+    chunk = math.gcd(size, 512)
+    places = [(group ^ other) * (quarter // chunk) for other in range(groups)]
+    places += [places[-1] + part * (size // chunk) for part in range(1, len(tails))]
+    places = jnp.stack(places)
+    for first, pieces in ((0, values[:1]), (1, values[1:]), (groups - 1, tails)):
         if not pieces:
             continue
         count = len(pieces)
+        per = pieces[0].shape[0] // chunk
         tall = pl.BlockSpec(
-            (chunk, width), lambda step, at, first=first: (update_block(first, per, step, at), 0)
+            (chunk, width), lambda step, at, first=first, per=per: (update_block(first, per, step, at), 0)
         )
         flat = pl.BlockSpec(
-            (1, chunk), lambda step, at, first=first: (0, update_block(first, per, step, at))
+            (1, chunk), lambda step, at, first=first, per=per: (0, update_block(first, per, step, at))
         )
         updated = pl.pallas_call(
             lambda *refs, first=first, count=count: update_kernel(first, count, *refs),
@@ -470,7 +487,10 @@
                 + [
                     pl.BlockSpec(
                         (chunk, width),
-                        lambda step, _, spot=spot: (jnp.clip(step - spot * per, 0, per - 1), 0),
+                        lambda step, _, spot=spot, per=per: (
+                            jnp.clip(step - spot * per, 0, per - 1),
+                            0,
+                        ),
                     )
                     for spot in range(count)
                 ]
@@ -483,25 +503,21 @@
         )(places, item_table, adagrad_state[None, :], *pieces, neg_sum, neg_spots, *updated)
     new_table, new_state = updated
 
-    part = math.gcd(examples // 2, 256)
-    per = examples // 2 // part
-    homes = ()
-    for side in range(2):
-        tall = pl.BlockSpec((part, width), lambda step, side=side: (side * per + step, 0))
-        flat = pl.BlockSpec((1, part), lambda step, side=side: (0, side * per + step))
-        homes = pl.pallas_call(
-            lambda *refs: home_kernel(table_rows, *refs),
-            out_shape=(
-                jax.ShapeDtypeStruct((examples, width), BF16),
-                jax.ShapeDtypeStruct((1, examples), F32),
-            ),
-            grid=(per,),
-            in_specs=[tall, flat, flat, whole(), whole(), whole()] + [anywhere] * len(homes),
-            out_specs=(tall, flat),
-            input_output_aliases={6: 0, 7: 1} if homes else {},
-            cost_estimate=cost(2**32, 8 * negs * width),
-        )(queries, place, own_gid[None, :], back, all_negs, local_ids, *homes)
-    query_grad, example_loss = homes
+    part = math.gcd(examples, 512)
+    tall = pl.BlockSpec((part, width), lambda step: (step, 0))
+    flat = pl.BlockSpec((1, part), lambda step: (0, step))
+    query_grad, example_loss = pl.pallas_call(
+        lambda *refs: home_kernel(table_rows, *refs),
+        out_shape=(
+            jax.ShapeDtypeStruct((examples, width), BF16),
+            jax.ShapeDtypeStruct((1, examples), F32),
+        ),
+        grid=(examples // part,),
+        in_specs=[tall, flat, flat, whole(), whole(), whole()],
+        out_specs=(tall, flat),
+        cost_estimate=cost(2**33, 8 * negs * width),
+        name="home",
+    )(queries, place, own_gid[None, :], back, all_negs, local_ids)
     return (query_grad, example_loss.reshape(examples), new_table, new_state.reshape(table_rows))
 
 

time: 182 us -> 173 us (0.951)
  Pallas kernels: 81.4 us -> 75.9 us
  waiting for transfers between devices: 49.8 us -> 45.8 us
  starting transfers between devices: 32.6 us -> 34.7 us
    ppermute x3 -> x2, waiting for transfers between devices: 8.91 us -> 4.52 us  [on_device(): values.append(lax.ppermute(values[0], 'dp', ways[other]))]
    pallas_call x2 -> x1, Pallas kernels: 12.9 us -> 9.27 us  [on_device(): pl.pallas_call(lambda *refs: home_kernel(table_rows, *refs), out_shape=(j...]
    ppermute x0 -> x2, starting transfers between devices: none -> 2.51 us  [on_device(): lax.ppermute(values[other][half], 'dp', ways[groups - 1 ^ other])]
  transfers between devices with their start and end apart: 24 -> 25, of which waited for: 9 -> 7; matrix products, arithmetic and copies ran while one was open for 7% -> 7% of each run, Pallas kernels for 28% -> 32%
where the time goes in v5:
time: 173 us; the launch traced here: 172 us
  Pallas kernels  75.9 us (44%)
  waiting for transfers between devices  45.8 us (26%)
  starting transfers between devices  34.7 us (20%)
  local copies, waits for them, and re-layouts  8.53 us (5%)
  other arithmetic  6.46 us (4%)
    ppermute x3, waiting for transfers between devices, on_device(): neg_sum = add(keep, lax.ppermute(give, 'item', flip(items, bit)))  18.4 us
    ppermute x3, waiting for transfers between devices, on_device(): block = lax.ppermute(block, 'item', ring)  18.1 us
    pallas_call x3, Pallas kernels, on_device(): pl.pallas_call(lambda *refs, first=first, count=count: update_kernel(firs...  15.9 us
    pallas_call x1, Pallas kernels, on_device(): pl.pallas_call(lambda *refs: owner_kernel(table_rows, *refs), out_shape=(...  15.7 us
    pallas_call x2, Pallas kernels, on_device(): pl.pallas_call(lambda *refs, start=start: find_kernel(start, *refs), out_...  13.4 us
    pallas_call x2, Pallas kernels, scatter(): pl.pallas_call(lambda *refs: scatter_kernel(others, *refs), out_shape=(ja...  11.6 us
    pallas_call x1, Pallas kernels, on_device(): pl.pallas_call(lambda *refs: home_kernel(table_rows, *refs), out_shape=(j...  9.27 us
    ppermute x3, starting transfers between devices, on_device(): neg_sum = add(keep, lax.ppermute(give, 'item', flip(items, bit)))  6.73 us
  transfers between devices with their start and end apart: 25, of which 7 were waited for; matrix products, arithmetic and copies ran while one was open for 7% of the time, Pallas kernels for 32%

profile of v5, /device:TPU:0, one launch (start us, length us, event | category | flops | bytes accessed | tf_op | source)
XLA Modules:
  0.0 172.4 jit_solution(11697649941244400867)
XLA Ops:
  0.6 3.1 %collective-permute-start.1 = (bf16[1024,256]{1,0:T(8,128)(2,1)}, bf16[1024,256]{1,0:T(8,128)(2,1)S(1)}, u32[]{:S(2)}, u32[]{:S(2)}) collective-permute-start(bf16[1024,256]{1,0:T(8,128)(2,1)} %refs_0_.3), channel_id=1, source_target_pairs={{0,2},{1,3},{2,4},{3,5},{4,6},{5,7},{6,0},{7,1},{8,10},{9,11},{10,... | collective-permute-start | bytes 1572872 | tf_op jit(solution)/shard_map/ppermute | solution.py:311
  3.7 0.7 fusion.16
  4.4 0.7 broadcast_multiply_fusion
  5.1 0.7 fusion.9
  6.2 2.8 %gather_fusion = f32[48,256]{1,0:T(8,128)S(1)} fusion(f32[4096,256]{1,0:T(8,128)} %refs_1_.5, s32[1024]{0:T(1024)S(1)} %pad_clamp_fusion), kind=kCustom, calls=%fused_computation | custom fusion | bytes 98496 | tf_op jit(solution)/shard_map/gather | solution.py:322
  9.3 0.7 broadcast_in_dim.9
  10.1 3.9 %all-to-all-start = ((bf16[8,48,384]{2,1,0:T(8,128)(2,1)}), bf16[8,48,384]{2,1,0:T(8,128)(2,1)S(1)}, u32[]{:S(2)}, u32[]{:S(2)}) async-start(bf16[8,48,384]{2,1,0:T(8,128)(2,1)} %broadcast_in_dim.9), calls=%async_computation | async-start | bytes 589824 | tf_op jit(solution)/shard_map/all_to_all | solution.py:283
  14.4 6.6 %norm.1.refs_1_ = bf16[4096,256]{1,0:T(8,128)(2,1)} custom-call(f32[4096,256]{1,0:T(8,128)} %refs_1_.5), custom_call_target="tpu_custom_call" | custom-call | flops 4294967296 | bytes 6291456 | tf_op jit(solution)/shard_map/norm/pallas_call | solution.py:353
  21.0 3.3 %all-to-all-done = bf16[8,48,384]{2,1,0:T(8,128)(2,1)S(1)} async-done(((bf16[8,48,384]{2,1,0:T(8,128)(2,1)}), bf16[8,48,384]{2,1,0:T(8,128)(2,1)S(1)}, u32[]{:S(2)}, u32[]{:S(2)}) %all-to-all-start) | async-done | bytes 294944 | tf_op jit(solution)/shard_map/all_to_all | solution.py:283
  24.3 2.4 %collective-permute-start.9 = (bf16[384,384]{1,0:T(8,128)(2,1)S(1)}, bf16[384,384]{1,0:T(8,128)(2,1)S(1)}, u32[]{:S(2)}, u32[]{:S(2)}) collective-permute-start(bf16[384,384]{1,0:T(8,128)(2,1)S(1)} %bitcast.42), channel_id=1, source_target_pairs={{0,24},{8,16},{16,8},{24,0},{1,25},{9,17},{17,9},{25,1},{2,26},{10... | collective-permute-start | bytes 884744 | tf_op jit(solution)/shard_map/ppermute | solution.py:336
  27.3 0.5 collective-permute-start.7
  28.2 0.6 fusion.6.gid_ref
  28.8 13.2 %collective-permute-done.3.refs_4_ = bf16[1024,256]{1,0:T(8,128)(2,1)S(1)} collective-permute-done((bf16[1024,256]{1,0:T(8,128)(2,1)S(1)}, bf16[1024,256]{1,0:T(8,128)(2,1)S(1)}, u32[]{:S(2)}, u32[]{:S(2)}) %collective-permute-start.3) | collective-permute-done | bytes 524320 | tf_op jit(solution)/shard_map/ppermute | solution.py:311
  42.1 3.4 %route.1 = (f32[8,1024]{1,0:T(8,128)}, s32[8,384]{1,0:T(8,128)}, f32[1,1024]{1,0:T(1,128)}) custom-call(s32[8,1024]{1,0:T(8,128)} %fusion.6.gid_ref, s32[1,1024]{1,0:T(1,128)} %bitcast.49, s32[1]{0:T(128)} %constant.118.clone.1.rows_ref), custom_call_target="tpu_custom_call" | custom-call | flops 4294967296 | bytes 6291456 | tf_op jit(solution)/shard_map/route/pallas_call | solution.py:339
  45.5 4.4 %shard_map.93.refs_2_ = bf16[3072,256]{1,0:T(8,128)(2,1)} custom-call(s32[8,384]{1,0:T(8,128)} %get-tuple-element.26.refs_0_.refs_13_, bf16[4096,256]{1,0:T(8,128)(2,1)} %norm.1.refs_1_), custom_call_target="tpu_custom_call" | custom-call | flops 2147483648 | bytes 8388608 | tf_op jit(solution)/shard_map/pallas_call | solution.py:365
  50.1 0.5 collective-permute-start.4
  50.6 4.8 %collective-permute-done.5.refs_6_ = bf16[1024,256]{1,0:T(8,128)(2,1)S(1)} collective-permute-done((bf16[1024,256]{1,0:T(8,128)(2,1)S(1)}, bf16[1024,256]{1,0:T(8,128)(2,1)S(1)}, u32[]{:S(2)}, u32[]{:S(2)}) %collective-permute-start.5) | collective-permute-done | bytes 524320 | tf_op jit(solution)/shard_map/ppermute | solution.py:311
  55.4 8.9 %shard_map.94.refs_14_ = bf16[3072,256]{1,0:T(8,128)(2,1)} custom-call(s32[8,384]{1,0:T(8,128)} %get-tuple-element.26.refs_0_.refs_13_, bf16[4096,256]{1,0:T(8,128)(2,1)} %norm.1.refs_1_, bf16[3072,256]{1,0:T(8,128)(2,1)} %shard_map.93.refs_2_), custom_call_target="tpu_custom_call", output_to_operand_aliasing={{}: (2, {})} | custom-call | flops 6442450944 | bytes 8388608 | tf_op jit(solution)/shard_map/pallas_call | solution.py:365
  64.4 0.8 copy-done.11
  65.2 15.7 %owner.1 = (bf16[3072,256]{1,0:T(8,128)(2,1)}, f32[1,3072]{1,0:T(1,128)}, bf16[1536,256]{1,0:T(8,128)(2,1)}, f32[1,1536]{1,0:T(1,128)}, bf16[1536,384]{1,0:T(8,128)(2,1)}, /*index=5*/f32[1,256]{1,0:T(1,128)}) custom-call(bf16[1024,256]{1,0:T(8,128)(2,1)} %refs_0_.3, bf16[1024,256]{1,0:T(8,128)(2,1)} %copy-done.8, bf16[1024,256]{1,0:T(8,128)(2,1)} %copy-done.7, ...), custom_call_target="tpu_custom_call" | custom-call | flops 9663676416 | bytes 3145728 | tf_op jit(solution)/shard_map/owner/pallas_call | solution.py:380
  80.9 1.0 dynamic-slice_bitcast_fusion
  82.3 3.8 %all-to-all-start.1 = ((bf16[8,384,256]{2,1,0:T(8,128)(2,1)}), bf16[8,384,256]{2,1,0:T(8,128)(2,1)S(1)}, u32[]{:S(2)}, u32[]{:S(2)}) async-start(bf16[8,384,256]{2,1,0:T(8,128)(2,1)} %bitcast.6), calls=%async_computation.1 | async-start | bytes 3145728 | tf_op jit(solution)/shard_map/all_to_all | solution.py:403
  86.1 5.8 %shard_map.96 = (bf16[1024,256]{1,0:T(8,128)(2,1)}, bf16[1024,256]{1,0:T(8,128)(2,1)}) custom-call(bf16[3072,256]{1,0:T(8,128)(2,1)} %get-tuple-element.32.refs_0_, f32[1,3072]{1,0:T(1,128)} %get-tuple-element.33.refs_1_), custom_call_target="tpu_custom_call" | custom-call | flops 3221225472 | bytes 1048576 | tf_op jit(solution)/shard_map/pallas_call | solution.py:412
  92.0 1.5 collective-permute-start.10
  93.4 1.5 collective-permute-start.11
  95.0 1.1 fusion
  96.1 1.8 %collective-permute-start.18 = (bf16[4,2,48,256]{3,2,1,0:T(8,128)(2,1)S(1)}, bf16[4,2,48,256]{3,2,1,0:T(8,128)(2,1)S(1)}, u32[]{:S(2)}, u32[]{:S(2)}) collective-permute-start(bf16[4,2,48,256]{3,2,1,0:T(8,128)(2,1)S(1)} %dynamic-slice_bitcast_fusion.1), channel_id=1, source_target_pairs={{0,2},{1,3},{2,0},{3,1},{4,6},{5,7},{6,4},{7,5},{8,10},{9,11},{10,... | collective-permute-start | bytes 589832 | tf_op jit(solution)/shard_map/ppermute | solution.py:451
  97.9 5.8 %shard_map.95 = (bf16[1024,256]{1,0:T(8,128)(2,1)}, bf16[1024,256]{1,0:T(8,128)(2,1)}) custom-call(bf16[3072,256]{1,0:T(8,128)(2,1)} %get-tuple-element.32.refs_0_, f32[1,3072]{1,0:T(1,128)} %get-tuple-element.33.refs_1_), custom_call_target="tpu_custom_call" | custom-call | flops 3221225472 | bytes 1048576 | tf_op jit(solution)/shard_map/pallas_call | solution.py:412
  104.2 12.3 %collective-permute-done.18 = bf16[4,2,48,256]{3,2,1,0:T(8,128)(2,1)S(1)} collective-permute-done((bf16[4,2,48,256]{3,2,1,0:T(8,128)(2,1)S(1)}, bf16[4,2,48,256]{3,2,1,0:T(8,128)(2,1)S(1)}, u32[]{:S(2)}, u32[]{:S(2)}) %collective-permute-start.18) | collective-permute-done | bytes 196640 | tf_op jit(solution)/shard_map/ppermute | solution.py:451
  116.6 4.6 %collective-permute-start.19 = (bf16[4,1,48,256]{3,2,1,0:T(8,128)(2,1)S(1)}, bf16[4,1,48,256]{3,2,1,0:T(8,128)(2,1)S(1)}, u32[]{:S(2)}, u32[]{:S(2)}) collective-permute-start(bf16[4,1,48,256]{3,2,1,0:T(8,128)(2,1)S(1)} %constant_dynamic-slice_fusion), channel_id=1, source_target_pairs={{0,4},{1,5},{2,6},{3,7},{4,0},{5,1},{6,2},{7,3},{8,12},{9,13},{10,... | collective-permute-start | bytes 294920 | tf_op jit(solution)/shard_map/ppermute | solution.py:451
  121.2 0.6 stack.23.refs_0_
  121.8 6.1 %collective-permute-done.19 = bf16[4,1,48,256]{3,2,1,0:T(8,128)(2,1)S(1)} collective-permute-done((bf16[4,1,48,256]{3,2,1,0:T(8,128)(2,1)S(1)}, bf16[4,1,48,256]{3,2,1,0:T(8,128)(2,1)S(1)}, u32[]{:S(2)}, u32[]{:S(2)}) %collective-permute-start.19) | collective-permute-done | bytes 98336 | tf_op jit(solution)/shard_map/ppermute | solution.py:451
  127.9 1.6 collective-permute-start.21
  129.5 1.5 collective-permute-start.20
  131.5 1.5 add_convert_fusion.refs_3_
  132.9 1.6 collective-permute-start.15
  134.5 1.5 collective-permute-start.13
  136.0 1.5 collective-permute-done.22
  137.5 0.7 add_convert_fusion.1.refs_4_.refs_5_
  138.2 4.5 %shard_map.97 = (f32[4096,256]{1,0:T(8,128)}, f32[1,4096]{1,0:T(1,128)}) custom-call(s32[5]{0:T(128)} %stack.23.refs_0_, f32[4096,256]{1,0:T(8,128)} %refs_1_.5, f32[1,4096]{1,0:T(1,128)} %bitcast.52, bf16[1024,256]{1,0:T(8,128)(2,1)} %copy-done.2, bf16[192,256]{1,0:T(8,128)(2,1)} %add_convert_fusion.1.refs_4_.refs_5_, ...), custom_call_target="tpu_custom_call" | custom-call | flops 4294967296 | bytes 5242880 | tf_op jit(solution)/shard_map/pallas_call | solution.py:477
  142.7 4.5 %collective-permute-done.15.refs_4_ = bf16[1024,256]{1,0:T(8,128)(2,1)S(1)} collective-permute-done((bf16[1024,256]{1,0:T(8,128)(2,1)S(1)}, bf16[1024,256]{1,0:T(8,128)(2,1)S(1)}, u32[]{:S(2)}, u32[]{:S(2)}) %collective-permute-start.15) | collective-permute-done | bytes 524320 | tf_op jit(solution)/shard_map/ppermute | solution.py:434
  147.2 0.9 collective-permute-start.16
  148.2 1.6 collective-permute-start.14
  149.8 6.9 %shard_map.98 = (f32[4096,256]{1,0:T(8,128)}, f32[1,4096]{1,0:T(1,128)}) custom-call(s32[5]{0:T(128)} %stack.23.refs_0_, f32[4096,256]{1,0:T(8,128)} %refs_1_.5, f32[1,4096]{1,0:T(1,128)} %bitcast.53, bf16[1024,256]{1,0:T(8,128)(2,1)} %copy-done.5, bf16[1024,256]{1,0:T(8,128)(2,1)} %copy-done.4, ...), custom_call_target="tpu_custom_call", output_to_operand_aliasing={{0}: (7, {}), {1}: (8, {})} | custom-call | flops 4294967296 | bytes 5242880 | tf_op jit(solution)/shard_map/pallas_call | solution.py:477
  156.6 1.2 copy-done
  157.8 9.3 %home.1 = (bf16[1024,256]{1,0:T(8,128)(2,1)}, f32[1,1024]{1,0:T(1,128)}) custom-call(bf16[1024,256]{1,0:T(8,128)(2,1)} %refs_0_.3, f32[1,1024]{1,0:T(1,128)} %get-tuple-element.25.refs_1_, s32[1,1024]{1,0:T(1,128)} %bitcast.50, bf16[3072,256]{1,0:T(8,128)(2,1)} %bitcast.37, bf16[1536,384]{1,0:T(8,128)(2,1)} %get-tuple-element.28.refs_4_, ...), custom_call_target="tpu_custom_call" | custom-call | flops 8589934592 | bytes 3145728 | tf_op jit(solution)/shard_map/home/pallas_call | solution.py:509
  167.1 0.7 copy-done.13
  167.8 4.6 %shard_map.99 = (f32[4096,256]{1,0:T(8,128)}, f32[1,4096]{1,0:T(1,128)}) custom-call(s32[5]{0:T(128)} %stack.23.refs_0_, f32[4096,256]{1,0:T(8,128)} %refs_1_.5, f32[1,4096]{1,0:T(1,128)} %bitcast.54, bf16[512,256]{1,0:T(8,128)(2,1)} %copy-done.13, bf16[512,256]{1,0:T(8,128)(2,1)} %collective-permute-done.16.refs_4_, ...), custom_call_target="tpu_custom_call", output_to_operand_aliasing={{0}: (7, {}), {1}: (8, {})} | custom-call | flops 4294967296 | bytes 5242880 | tf_op jit(solution)/shard_map/pallas_call | solution.py:477
  (73 shorter events, 3.7 us)
Async XLA Ops:
  0.6 27.2 %collective-permute-start.1 = (bf16[1024,256]{1,0:T(8,128)(2,1)}, bf16[1024,256]{1,0:T(8,128)(2,1)S(1)}, u32[]{:S(2)}, u32[]{:S(2)}) collective-permute-start(bf16[1024,256]{1,0:T(8,128)(2,1)} %refs_0_.3), channel_id=1, source_target_pairs={{0,2},{1,3},{2,4},{3,5},{4,6},{5,7},{6,0},{7,1},{8,10},{9,11},{10,... | collective-permute-start | bytes 1572872 | tf_op jit(solution)/shard_map/ppermute | solution.py:311
  5.8 15.2 %copy-start.6 = (s32[1024]{0:T(1024)}, s32[1024]{0:T(1024)S(1)}, u32[]{:S(2)}) copy-start(s32[1024]{0:T(1024)S(1)} %get-tuple-element.47) | copy-start | bytes 12292
  10.1 14.3 %all-to-all-start = ((bf16[8,48,384]{2,1,0:T(8,128)(2,1)}), bf16[8,48,384]{2,1,0:T(8,128)(2,1)S(1)}, u32[]{:S(2)}, u32[]{:S(2)}) async-start(bf16[8,48,384]{2,1,0:T(8,128)(2,1)} %broadcast_in_dim.9), calls=%async_computation | async-start | bytes 589824 | tf_op jit(solution)/shard_map/all_to_all | solution.py:283
  13.9 36.0 %collective-permute-start = (bf16[1024,256]{1,0:T(8,128)(2,1)}, bf16[1024,256]{1,0:T(8,128)(2,1)S(1)}, u32[]{:S(2)}, u32[]{:S(2)}) collective-permute-start(bf16[1024,256]{1,0:T(8,128)(2,1)} %refs_0_.3), channel_id=1, source_target_pairs={{0,1},{1,0},{2,3},{3,2},{4,5},{5,4},{6,7},{7,6},{8,9},{9,8},{10,11... | collective-permute-start | bytes 1572872 | tf_op jit(solution)/shard_map/ppermute | solution.py:312
  24.3 21.2 %copy-start.3 = (bf16[8,48,384]{2,1,0:T(8,128)(2,1)}, bf16[8,48,384]{2,1,0:T(8,128)(2,1)S(1)}, u32[]{:S(2)}) copy-start(bf16[8,48,384]{2,1,0:T(8,128)(2,1)S(1)} %all-to-all-done) | copy-start | bytes 884740
  24.3 25.7 %collective-permute-start.9 = (bf16[384,384]{1,0:T(8,128)(2,1)S(1)}, bf16[384,384]{1,0:T(8,128)(2,1)S(1)}, u32[]{:S(2)}, u32[]{:S(2)}) collective-permute-start(bf16[384,384]{1,0:T(8,128)(2,1)S(1)} %bitcast.42), channel_id=1, source_target_pairs={{0,24},{8,16},{16,8},{24,0},{1,25},{9,17},{17,9},{25,1},{2,26},{10... | collective-permute-start | bytes 884744 | tf_op jit(solution)/shard_map/ppermute | solution.py:336
  26.8 37.6 %collective-permute-start.8 = (bf16[384,384]{1,0:T(8,128)(2,1)S(1)}, bf16[384,384]{1,0:T(8,128)(2,1)}, u32[]{:S(2)}, u32[]{:S(2)}) collective-permute-start(bf16[384,384]{1,0:T(8,128)(2,1)S(1)} %bitcast.43), channel_id=1, source_target_pairs={{0,16},{8,24},{16,0},{24,8},{1,17},{9,25},{17,1},{25,9},{2,18},{10... | collective-permute-start | bytes 884744 | tf_op jit(solution)/shard_map/ppermute | solution.py:336
  27.3 37.1 %collective-permute-start.7 = (bf16[384,384]{1,0:T(8,128)(2,1)S(1)}, bf16[384,384]{1,0:T(8,128)(2,1)}, u32[]{:S(2)}, u32[]{:S(2)}) collective-permute-start(bf16[384,384]{1,0:T(8,128)(2,1)S(1)} %bitcast.44), channel_id=1, source_target_pairs={{0,8},{8,0},{16,24},{24,16},{1,9},{9,1},{17,25},{25,17},{2,10},{10... | collective-permute-start | bytes 884744 | tf_op jit(solution)/shard_map/ppermute | solution.py:336
  27.8 22.1 %copy-start.7 = (bf16[1024,256]{1,0:T(8,128)(2,1)}, bf16[1024,256]{1,0:T(8,128)(2,1)S(1)}, u32[]{:S(2)}) copy-start(bf16[1024,256]{1,0:T(8,128)(2,1)S(1)} %collective-permute-done.1.refs_2_) | copy-start | bytes 1572868
  27.8 14.2 %collective-permute-start.3 = (bf16[1024,256]{1,0:T(8,128)(2,1)S(1)}, bf16[1024,256]{1,0:T(8,128)(2,1)S(1)}, u32[]{:S(2)}, u32[]{:S(2)}) collective-permute-start(bf16[1024,256]{1,0:T(8,128)(2,1)S(1)} %collective-permute-done.1.refs_2_), channel_id=1, source_target_pairs={{0,2},{1,3},{2,4},{3,5},{4,6},{5,7},{6,0},{7,1},{8,10},{9,11},{10,... | collective-permute-start | bytes 1572872 | tf_op jit(solution)/shard_map/ppermute | solution.py:311
  42.0 8.0 %copy-start.9 = (bf16[1024,256]{1,0:T(8,128)(2,1)}, bf16[1024,256]{1,0:T(8,128)(2,1)S(1)}, u32[]{:S(2)}) copy-start(bf16[1024,256]{1,0:T(8,128)(2,1)S(1)} %collective-permute-done.3.refs_4_) | copy-start | bytes 1572868
  42.1 13.4 %collective-permute-start.5 = (bf16[1024,256]{1,0:T(8,128)(2,1)S(1)}, bf16[1024,256]{1,0:T(8,128)(2,1)S(1)}, u32[]{:S(2)}, u32[]{:S(2)}) collective-permute-start(bf16[1024,256]{1,0:T(8,128)(2,1)S(1)} %collective-permute-done.3.refs_4_), channel_id=1, source_target_pairs={{0,2},{1,3},{2,4},{3,5},{4,6},{5,7},{6,0},{7,1},{8,10},{9,11},{10,... | collective-permute-start | bytes 1572872 | tf_op jit(solution)/shard_map/ppermute | solution.py:311
  50.0 14.4 %copy-start.8 = (bf16[1024,256]{1,0:T(8,128)(2,1)}, bf16[1024,256]{1,0:T(8,128)(2,1)S(1)}, u32[]{:S(2)}) copy-start(bf16[1024,256]{1,0:T(8,128)(2,1)S(1)} %collective-permute-done.refs_1_) | copy-start | bytes 1572868
  50.0 14.4 %collective-permute-start.2 = (bf16[1024,256]{1,0:T(8,128)(2,1)S(1)}, bf16[1024,256]{1,0:T(8,128)(2,1)S(1)}, u32[]{:S(2)}, u32[]{:S(2)}) collective-permute-start(bf16[1024,256]{1,0:T(8,128)(2,1)S(1)} %collective-permute-done.1.refs_2_), channel_id=1, source_target_pairs={{0,1},{1,0},{2,3},{3,2},{4,5},{5,4},{6,7},{7,6},{8,9},{9,8},{10,11... | collective-permute-start | bytes 1572872 | tf_op jit(solution)/shard_map/ppermute | solution.py:312
  50.1 14.3 %copy-start.12 = (bf16[384,384]{1,0:T(8,128)(2,1)}, bf16[384,384]{1,0:T(8,128)(2,1)S(1)}, u32[]{:S(2)}) copy-start(bf16[384,384]{1,0:T(8,128)(2,1)S(1)} %collective-permute-done.9.refs_11_) | copy-start | bytes 884740
  50.1 14.3 %collective-permute-start.4 = (bf16[1024,256]{1,0:T(8,128)(2,1)S(1)}, bf16[1024,256]{1,0:T(8,128)(2,1)}, u32[]{:S(2)}, u32[]{:S(2)}) collective-permute-start(bf16[1024,256]{1,0:T(8,128)(2,1)S(1)} %collective-permute-done.3.refs_4_), channel_id=1, source_target_pairs={{0,1},{1,0},{2,3},{3,2},{4,5},{5,4},{6,7},{7,6},{8,9},{9,8},{10,11... | collective-permute-start | bytes 1572872 | tf_op jit(solution)/shard_map/ppermute | solution.py:312
  55.4 8.9 %copy-start.10 = (bf16[1024,256]{1,0:T(8,128)(2,1)}, bf16[1024,256]{1,0:T(8,128)(2,1)S(1)}, u32[]{:S(2)}) copy-start(bf16[1024,256]{1,0:T(8,128)(2,1)S(1)} %collective-permute-done.5.refs_6_) | copy-start | bytes 1572868
  55.4 9.0 %collective-permute-start.6 = (bf16[1024,256]{1,0:T(8,128)(2,1)S(1)}, bf16[1024,256]{1,0:T(8,128)(2,1)}, u32[]{:S(2)}, u32[]{:S(2)}) collective-permute-start(bf16[1024,256]{1,0:T(8,128)(2,1)S(1)} %collective-permute-done.5.refs_6_), channel_id=1, source_target_pairs={{0,1},{1,0},{2,3},{3,2},{4,5},{5,4},{6,7},{7,6},{8,9},{9,8},{10,11... | collective-permute-start | bytes 1572872 | tf_op jit(solution)/shard_map/ppermute | solution.py:312
  64.4 0.8 copy-start.11
  82.0 13.0 %collective-permute-start.17 = (bf16[4,4,48,256]{3,2,1,0:T(8,128)(2,1)S(1)}, bf16[4,4,48,256]{3,2,1,0:T(8,128)(2,1)}, u32[]{:S(2)}, u32[]{:S(2)}) collective-permute-start(bf16[4,4,48,256]{3,2,1,0:T(8,128)(2,1)S(1)} %dynamic-slice_bitcast_fusion), channel_id=1, source_target_pairs={{0,1},{1,0},{2,3},{3,2},{4,5},{5,4},{6,7},{7,6},{8,9},{9,8},{10,11... | collective-permute-start | bytes 1179656 | tf_op jit(solution)/shard_map/ppermute | solution.py:451
  82.3 74.3 %all-to-all-start.1 = ((bf16[8,384,256]{2,1,0:T(8,128)(2,1)}), bf16[8,384,256]{2,1,0:T(8,128)(2,1)S(1)}, u32[]{:S(2)}, u32[]{:S(2)}) async-start(bf16[8,384,256]{2,1,0:T(8,128)(2,1)} %bitcast.6), calls=%async_computation.1 | async-start | bytes 3145728 | tf_op jit(solution)/shard_map/all_to_all | solution.py:403
  86.1 8.9 %copy-start.1 = (bf16[1536,256]{1,0:T(8,128)(2,1)S(1)}, bf16[1536,256]{1,0:T(8,128)(2,1)}, u32[]{:S(2)}) copy-start(bf16[1536,256]{1,0:T(8,128)(2,1)} %get-tuple-element.38) | copy-start | bytes 2359300
  92.0 39.0 %collective-permute-start.10 = (bf16[1024,256]{1,0:T(8,128)(2,1)}, bf16[1024,256]{1,0:T(8,128)(2,1)S(1)}, u32[]{:S(2)}, u32[]{:S(2)}) collective-permute-start(bf16[1024,256]{1,0:T(8,128)(2,1)} %get-tuple-element.35), channel_id=1, source_target_pairs={{0,8},{8,0},{16,24},{24,16},{1,9},{9,1},{17,25},{25,17},{2,10},{10... | collective-permute-start | bytes 1572872 | tf_op jit(solution)/shard_map/ppermute | solution.py:426
  93.4 38.0 %collective-permute-start.11 = (bf16[1024,256]{1,0:T(8,128)(2,1)}, bf16[1024,256]{1,0:T(8,128)(2,1)}, u32[]{:S(2)}, u32[]{:S(2)}) collective-permute-start(bf16[1024,256]{1,0:T(8,128)(2,1)} %get-tuple-element.36), channel_id=1, source_target_pairs={{0,16},{8,24},{16,0},{24,8},{1,17},{9,25},{17,1},{25,9},{2,18},{10... | collective-permute-start | bytes 1572872 | tf_op jit(solution)/shard_map/ppermute | solution.py:426
  96.1 20.4 %collective-permute-start.18 = (bf16[4,2,48,256]{3,2,1,0:T(8,128)(2,1)S(1)}, bf16[4,2,48,256]{3,2,1,0:T(8,128)(2,1)S(1)}, u32[]{:S(2)}, u32[]{:S(2)}) collective-permute-start(bf16[4,2,48,256]{3,2,1,0:T(8,128)(2,1)S(1)} %dynamic-slice_bitcast_fusion.1), channel_id=1, source_target_pairs={{0,2},{1,3},{2,0},{3,1},{4,6},{5,7},{6,4},{7,5},{8,10},{9,11},{10,... | collective-permute-start | bytes 589832 | tf_op jit(solution)/shard_map/ppermute | solution.py:451
  103.7 27.8 %collective-permute-start.12 = (bf16[1024,256]{1,0:T(8,128)(2,1)}, bf16[1024,256]{1,0:T(8,128)(2,1)S(1)}, u32[]{:S(2)}, u32[]{:S(2)}) collective-permute-start(bf16[1024,256]{1,0:T(8,128)(2,1)} %get-tuple-element.37), channel_id=1, source_target_pairs={{0,24},{8,16},{16,8},{24,0},{1,25},{9,17},{17,9},{25,1},{2,26},{10... | collective-permute-start | bytes 1572872 | tf_op jit(solution)/shard_map/ppermute | solution.py:428
  116.6 11.3 %collective-permute-start.19 = (bf16[4,1,48,256]{3,2,1,0:T(8,128)(2,1)S(1)}, bf16[4,1,48,256]{3,2,1,0:T(8,128)(2,1)S(1)}, u32[]{:S(2)}, u32[]{:S(2)}) collective-permute-start(bf16[4,1,48,256]{3,2,1,0:T(8,128)(2,1)S(1)} %constant_dynamic-slice_fusion), channel_id=1, source_target_pairs={{0,4},{1,5},{2,6},{3,7},{4,0},{5,1},{6,2},{7,3},{8,12},{9,13},{10,... | collective-permute-start | bytes 294920 | tf_op jit(solution)/shard_map/ppermute | solution.py:451
  127.9 8.1 %collective-permute-start.21 = (bf16[192,256]{1,0:T(8,128)(2,1)S(1)}, bf16[192,256]{1,0:T(8,128)(2,1)S(1)}, u32[]{:S(2)}, u32[]{:S(2)}) collective-permute-start(bf16[192,256]{1,0:T(8,128)(2,1)S(1)} %bitcast.46), channel_id=1, source_target_pairs={{0,16},{8,24},{16,0},{24,8},{1,17},{9,25},{17,1},{25,9},{2,18},{10... | collective-permute-start | bytes 294920 | tf_op jit(solution)/shard_map/ppermute | solution.py:455
  129.5 6.5 %collective-permute-start.20 = (bf16[192,256]{1,0:T(8,128)(2,1)S(1)}, bf16[192,256]{1,0:T(8,128)(2,1)S(1)}, u32[]{:S(2)}, u32[]{:S(2)}) collective-permute-start(bf16[192,256]{1,0:T(8,128)(2,1)S(1)} %bitcast.47), channel_id=1, source_target_pairs={{0,8},{8,0},{16,24},{24,16},{1,9},{9,1},{17,25},{25,17},{2,10},{10... | collective-permute-start | bytes 294920 | tf_op jit(solution)/shard_map/ppermute | solution.py:455
  131.0 6.5 %collective-permute-start.22 = (bf16[192,256]{1,0:T(8,128)(2,1)S(1)}, bf16[192,256]{1,0:T(8,128)(2,1)S(1)}, u32[]{:S(2)}, u32[]{:S(2)}) collective-permute-start(bf16[192,256]{1,0:T(8,128)(2,1)S(1)} %bitcast.48), channel_id=1, source_target_pairs={{0,24},{8,16},{16,8},{24,0},{1,25},{9,17},{17,9},{25,1},{2,26},{10... | collective-permute-start | bytes 294920 | tf_op jit(solution)/shard_map/ppermute | solution.py:455
  132.9 5.3 %copy-start.2 = (bf16[1024,256]{1,0:T(8,128)(2,1)}, bf16[1024,256]{1,0:T(8,128)(2,1)S(1)}, u32[]{:S(2)}) copy-start(bf16[1024,256]{1,0:T(8,128)(2,1)S(1)} %add_convert_fusion.refs_3_) | copy-start | bytes 1572868
  132.9 14.3 %collective-permute-start.15 = (bf16[1024,256]{1,0:T(8,128)(2,1)S(1)}, bf16[1024,256]{1,0:T(8,128)(2,1)S(1)}, u32[]{:S(2)}, u32[]{:S(2)}) collective-permute-start(bf16[1024,256]{1,0:T(8,128)(2,1)S(1)} %add_convert_fusion.refs_3_), channel_id=1, source_target_pairs={{0,16},{8,24},{16,0},{24,8},{1,17},{9,25},{17,1},{25,9},{2,18},{10... | collective-permute-start | bytes 1572872 | tf_op jit(solution)/shard_map/ppermute | solution.py:434
  134.5 13.7 %collective-permute-start.13 = (bf16[1024,256]{1,0:T(8,128)(2,1)S(1)}, bf16[1024,256]{1,0:T(8,128)(2,1)S(1)}, u32[]{:S(2)}, u32[]{:S(2)}) collective-permute-start(bf16[1024,256]{1,0:T(8,128)(2,1)S(1)} %add_convert_fusion.refs_3_), channel_id=1, source_target_pairs={{0,8},{8,0},{16,24},{24,16},{1,9},{9,1},{17,25},{25,17},{2,10},{10... | collective-permute-start | bytes 1572872 | tf_op jit(solution)/shard_map/ppermute | solution.py:434
  147.2 2.6 %copy-start.4 = (bf16[1024,256]{1,0:T(8,128)(2,1)}, bf16[1024,256]{1,0:T(8,128)(2,1)S(1)}, u32[]{:S(2)}) copy-start(bf16[1024,256]{1,0:T(8,128)(2,1)S(1)} %collective-permute-done.15.refs_4_) | copy-start | bytes 1572868
  147.2 19.9 %collective-permute-start.16 = (bf16[512,256]{1,0:T(8,128)(2,1)S(1)}, bf16[512,256]{1,0:T(8,128)(2,1)}, u32[]{:S(2)}, u32[]{:S(2)}) collective-permute-start(bf16[512,256]{1,0:T(8,128)(2,1)S(1)} %slice.31), channel_id=1, source_target_pairs={{0,8},{8,0},{16,24},{24,16},{1,9},{9,1},{17,25},{25,17},{2,10},{10... | collective-permute-start | bytes 786440 | tf_op jit(solution)/shard_map/ppermute | solution.py:440
  148.2 1.6 copy-start.5
  148.2 18.9 %collective-permute-start.14 = (bf16[512,256]{1,0:T(8,128)(2,1)S(1)}, bf16[512,256]{1,0:T(8,128)(2,1)S(1)}, u32[]{:S(2)}, u32[]{:S(2)}) collective-permute-start(bf16[512,256]{1,0:T(8,128)(2,1)S(1)} %slice.30), channel_id=1, source_target_pairs={{0,16},{8,24},{16,0},{24,8},{1,17},{9,25},{17,1},{25,9},{2,18},{10... | collective-permute-start | bytes 786440 | tf_op jit(solution)/shard_map/ppermute | solution.py:440
  156.6 1.2 copy-start
  167.1 0.7 copy-start.13

commit v6 on v5

--- a/solution.py
+++ b/solution.py
@@ -503,21 +503,24 @@
         )(places, item_table, adagrad_state[None, :], *pieces, neg_sum, neg_spots, *updated)
     new_table, new_state = updated
 
-    part = math.gcd(examples, 512)
-    tall = pl.BlockSpec((part, width), lambda step: (step, 0))
-    flat = pl.BlockSpec((1, part), lambda step: (0, step))
-    query_grad, example_loss = pl.pallas_call(
-        lambda *refs: home_kernel(table_rows, *refs),
-        out_shape=(
-            jax.ShapeDtypeStruct((examples, width), BF16),
-            jax.ShapeDtypeStruct((1, examples), F32),
-        ),
-        grid=(examples // part,),
-        in_specs=[tall, flat, flat, whole(), whole(), whole()],
-        out_specs=(tall, flat),
-        cost_estimate=cost(2**33, 8 * negs * width),
-        name="home",
-    )(queries, place, own_gid[None, :], back, all_negs, local_ids)
+    part = examples // 2
+    homes = ()
+    for side in range(2):
+        tall = pl.BlockSpec((part, width), lambda step, side=side: (side + step, 0))
+        flat = pl.BlockSpec((1, part), lambda step, side=side: (0, side + step))
+        homes = pl.pallas_call(
+            lambda *refs: home_kernel(table_rows, *refs),
+            out_shape=(
+                jax.ShapeDtypeStruct((examples, width), BF16),
+                jax.ShapeDtypeStruct((1, examples), F32),
+            ),
+            grid=(1,),
+            in_specs=[tall, flat, flat, whole(), whole(), whole()] + [anywhere] * len(homes),
+            out_specs=(tall, flat),
+            input_output_aliases={6: 0, 7: 1} if homes else {},
+            cost_estimate=cost(2**32, 8 * negs * width),
+        )(queries, place, own_gid[None, :], back, all_negs, local_ids, *homes)
+    query_grad, example_loss = homes
     return (query_grad, example_loss.reshape(examples), new_table, new_state.reshape(table_rows))
 
 

time: 173 us -> 176 us (1.017)
  Pallas kernels: 75.9 us -> 78.4 us
    pallas_call x1 -> x2, Pallas kernels: 9.27 us -> 11.7 us  [on_device(): pl.pallas_call(lambda *refs: home_kernel(table_rows, *refs), out_shape=(j...]
  transfers between devices with their start and end apart: 25 -> 25, of which waited for: 7 -> 7; matrix products, arithmetic and copies ran while one was open for 7% -> 6% of each run, Pallas kernels for 32% -> 33%
where the time goes in v6:
time: 176 us; the launch traced here: 175 us
  Pallas kernels  78.4 us (45%)
  waiting for transfers between devices  45.8 us (26%)
  starting transfers between devices  34.7 us (20%)
  local copies, waits for them, and re-layouts  8.57 us (5%)
  other arithmetic  6.47 us (4%)
    ppermute x3, waiting for transfers between devices, on_device(): neg_sum = add(keep, lax.ppermute(give, 'item', flip(items, bit)))  18.4 us
    ppermute x3, waiting for transfers between devices, on_device(): block = lax.ppermute(block, 'item', ring)  18 us
    pallas_call x3, Pallas kernels, on_device(): pl.pallas_call(lambda *refs, first=first, count=count: update_kernel(firs...  15.9 us
    pallas_call x1, Pallas kernels, on_device(): pl.pallas_call(lambda *refs: owner_kernel(table_rows, *refs), out_shape=(...  15.8 us
    pallas_call x2, Pallas kernels, on_device(): pl.pallas_call(lambda *refs, start=start: find_kernel(start, *refs), out_...  13.4 us
    pallas_call x2, Pallas kernels, on_device(): pl.pallas_call(lambda *refs: home_kernel(table_rows, *refs), out_shape=(j...  11.7 us
    pallas_call x2, Pallas kernels, scatter(): pl.pallas_call(lambda *refs: scatter_kernel(others, *refs), out_shape=(ja...  11.6 us
    ppermute x3, starting transfers between devices, on_device(): neg_sum = add(keep, lax.ppermute(give, 'item', flip(items, bit)))  6.74 us
  transfers between devices with their start and end apart: 25, of which 7 were waited for; matrix products, arithmetic and copies ran while one was open for 6% of the time, Pallas kernels for 33%

profile of v6, /device:TPU:0, one launch (start us, length us, event | category | flops | bytes accessed | tf_op | source)
XLA Modules:
  0.0 174.8 jit_solution(15710758135369430114)
XLA Ops:
  0.6 3.1 %collective-permute-start.1 = (bf16[1024,256]{1,0:T(8,128)(2,1)}, bf16[1024,256]{1,0:T(8,128)(2,1)S(1)}, u32[]{:S(2)}, u32[]{:S(2)}) collective-permute-start(bf16[1024,256]{1,0:T(8,128)(2,1)} %refs_0_.5), channel_id=1, source_target_pairs={{0,2},{1,3},{2,4},{3,5},{4,6},{5,7},{6,0},{7,1},{8,10},{9,11},{10,... | collective-permute-start | bytes 1572872 | tf_op jit(solution)/shard_map/ppermute | solution.py:311
  3.7 0.7 fusion.16
  4.4 0.7 broadcast_multiply_fusion
  5.1 0.7 fusion.9
  6.2 2.8 %gather_fusion = f32[48,256]{1,0:T(8,128)S(1)} fusion(f32[4096,256]{1,0:T(8,128)} %refs_1_.5, s32[1024]{0:T(1024)S(1)} %pad_clamp_fusion), kind=kCustom, calls=%fused_computation | custom fusion | bytes 98496 | tf_op jit(solution)/shard_map/gather | solution.py:322
  9.3 0.7 broadcast_in_dim.9
  10.1 3.9 %all-to-all-start = ((bf16[8,48,384]{2,1,0:T(8,128)(2,1)}), bf16[8,48,384]{2,1,0:T(8,128)(2,1)S(1)}, u32[]{:S(2)}, u32[]{:S(2)}) async-start(bf16[8,48,384]{2,1,0:T(8,128)(2,1)} %broadcast_in_dim.9), calls=%async_computation | async-start | bytes 589824 | tf_op jit(solution)/shard_map/all_to_all | solution.py:283
  14.4 6.6 %norm.1.refs_1_ = bf16[4096,256]{1,0:T(8,128)(2,1)} custom-call(f32[4096,256]{1,0:T(8,128)} %refs_1_.5), custom_call_target="tpu_custom_call" | custom-call | flops 4294967296 | bytes 6291456 | tf_op jit(solution)/shard_map/norm/pallas_call | solution.py:353
  21.0 3.3 %all-to-all-done = bf16[8,48,384]{2,1,0:T(8,128)(2,1)S(1)} async-done(((bf16[8,48,384]{2,1,0:T(8,128)(2,1)}), bf16[8,48,384]{2,1,0:T(8,128)(2,1)S(1)}, u32[]{:S(2)}, u32[]{:S(2)}) %all-to-all-start) | async-done | bytes 294944 | tf_op jit(solution)/shard_map/all_to_all | solution.py:283
  24.3 2.4 %collective-permute-start.9 = (bf16[384,384]{1,0:T(8,128)(2,1)S(1)}, bf16[384,384]{1,0:T(8,128)(2,1)S(1)}, u32[]{:S(2)}, u32[]{:S(2)}) collective-permute-start(bf16[384,384]{1,0:T(8,128)(2,1)S(1)} %bitcast.43), channel_id=1, source_target_pairs={{0,24},{8,16},{16,8},{24,0},{1,25},{9,17},{17,9},{25,1},{2,26},{10... | collective-permute-start | bytes 884744 | tf_op jit(solution)/shard_map/ppermute | solution.py:336
  27.3 0.5 collective-permute-start.7
  28.2 0.6 fusion.6.gid_ref
  28.8 13.2 %collective-permute-done.3.refs_4_ = bf16[1024,256]{1,0:T(8,128)(2,1)S(1)} collective-permute-done((bf16[1024,256]{1,0:T(8,128)(2,1)S(1)}, bf16[1024,256]{1,0:T(8,128)(2,1)S(1)}, u32[]{:S(2)}, u32[]{:S(2)}) %collective-permute-start.3) | collective-permute-done | bytes 524320 | tf_op jit(solution)/shard_map/ppermute | solution.py:311
  42.1 3.4 %route.1 = (f32[8,1024]{1,0:T(8,128)}, s32[8,384]{1,0:T(8,128)}, f32[1,1024]{1,0:T(1,128)}) custom-call(s32[8,1024]{1,0:T(8,128)} %fusion.6.gid_ref, s32[1,1024]{1,0:T(1,128)} %bitcast.50, s32[1]{0:T(128)} %constant.118.clone.1.rows_ref), custom_call_target="tpu_custom_call" | custom-call | flops 4294967296 | bytes 6291456 | tf_op jit(solution)/shard_map/route/pallas_call | solution.py:339
  45.5 4.5 %shard_map.93.refs_2_ = bf16[3072,256]{1,0:T(8,128)(2,1)} custom-call(s32[8,384]{1,0:T(8,128)} %get-tuple-element.28.refs_0_.refs_13_, bf16[4096,256]{1,0:T(8,128)(2,1)} %norm.1.refs_1_), custom_call_target="tpu_custom_call" | custom-call | flops 2147483648 | bytes 8388608 | tf_op jit(solution)/shard_map/pallas_call | solution.py:365
  50.6 4.8 %collective-permute-done.5.refs_6_ = bf16[1024,256]{1,0:T(8,128)(2,1)S(1)} collective-permute-done((bf16[1024,256]{1,0:T(8,128)(2,1)S(1)}, bf16[1024,256]{1,0:T(8,128)(2,1)S(1)}, u32[]{:S(2)}, u32[]{:S(2)}) %collective-permute-start.5) | collective-permute-done | bytes 524320 | tf_op jit(solution)/shard_map/ppermute | solution.py:311
  55.4 8.9 %shard_map.94.refs_14_ = bf16[3072,256]{1,0:T(8,128)(2,1)} custom-call(s32[8,384]{1,0:T(8,128)} %get-tuple-element.28.refs_0_.refs_13_, bf16[4096,256]{1,0:T(8,128)(2,1)} %norm.1.refs_1_, bf16[3072,256]{1,0:T(8,128)(2,1)} %shard_map.93.refs_2_), custom_call_target="tpu_custom_call", output_to_operand_aliasing={{}: (2, {})} | custom-call | flops 6442450944 | bytes 8388608 | tf_op jit(solution)/shard_map/pallas_call | solution.py:365
  64.4 0.8 copy-done.11
  65.2 15.8 %owner.1 = (bf16[3072,256]{1,0:T(8,128)(2,1)}, f32[1,3072]{1,0:T(1,128)}, bf16[1536,256]{1,0:T(8,128)(2,1)}, f32[1,1536]{1,0:T(1,128)}, bf16[1536,384]{1,0:T(8,128)(2,1)}, /*index=5*/f32[1,256]{1,0:T(1,128)}) custom-call(bf16[1024,256]{1,0:T(8,128)(2,1)} %refs_0_.5, bf16[1024,256]{1,0:T(8,128)(2,1)} %copy-done.8, bf16[1024,256]{1,0:T(8,128)(2,1)} %copy-done.7, ...), custom_call_target="tpu_custom_call" | custom-call | flops 9663676416 | bytes 3145728 | tf_op jit(solution)/shard_map/owner/pallas_call | solution.py:380
  81.0 1.0 dynamic-slice_bitcast_fusion
  82.4 3.8 %all-to-all-start.1 = ((bf16[8,384,256]{2,1,0:T(8,128)(2,1)}), bf16[8,384,256]{2,1,0:T(8,128)(2,1)S(1)}, u32[]{:S(2)}, u32[]{:S(2)}) async-start(bf16[8,384,256]{2,1,0:T(8,128)(2,1)} %bitcast.6), calls=%async_computation.1 | async-start | bytes 3145728 | tf_op jit(solution)/shard_map/all_to_all | solution.py:403
  86.1 5.9 %shard_map.98 = (bf16[1024,256]{1,0:T(8,128)(2,1)}, bf16[1024,256]{1,0:T(8,128)(2,1)}) custom-call(bf16[3072,256]{1,0:T(8,128)(2,1)} %get-tuple-element.36.refs_0_, f32[1,3072]{1,0:T(1,128)} %get-tuple-element.37.refs_1_), custom_call_target="tpu_custom_call" | custom-call | flops 3221225472 | bytes 1048576 | tf_op jit(solution)/shard_map/pallas_call | solution.py:412
  92.0 1.5 collective-permute-start.10
  93.5 1.5 collective-permute-start.11
  95.0 1.1 fusion
  96.1 1.8 %collective-permute-start.18 = (bf16[4,2,48,256]{3,2,1,0:T(8,128)(2,1)S(1)}, bf16[4,2,48,256]{3,2,1,0:T(8,128)(2,1)S(1)}, u32[]{:S(2)}, u32[]{:S(2)}) collective-permute-start(bf16[4,2,48,256]{3,2,1,0:T(8,128)(2,1)S(1)} %dynamic-slice_bitcast_fusion.1), channel_id=1, source_target_pairs={{0,2},{1,3},{2,0},{3,1},{4,6},{5,7},{6,4},{7,5},{8,10},{9,11},{10,... | collective-permute-start | bytes 589832 | tf_op jit(solution)/shard_map/ppermute | solution.py:451
  97.9 5.8 %shard_map.97 = (bf16[1024,256]{1,0:T(8,128)(2,1)}, bf16[1024,256]{1,0:T(8,128)(2,1)}) custom-call(bf16[3072,256]{1,0:T(8,128)(2,1)} %get-tuple-element.36.refs_0_, f32[1,3072]{1,0:T(1,128)} %get-tuple-element.37.refs_1_), custom_call_target="tpu_custom_call" | custom-call | flops 3221225472 | bytes 1048576 | tf_op jit(solution)/shard_map/pallas_call | solution.py:412
  104.2 12.3 %collective-permute-done.18 = bf16[4,2,48,256]{3,2,1,0:T(8,128)(2,1)S(1)} collective-permute-done((bf16[4,2,48,256]{3,2,1,0:T(8,128)(2,1)S(1)}, bf16[4,2,48,256]{3,2,1,0:T(8,128)(2,1)S(1)}, u32[]{:S(2)}, u32[]{:S(2)}) %collective-permute-start.18) | collective-permute-done | bytes 196640 | tf_op jit(solution)/shard_map/ppermute | solution.py:451
  116.6 4.6 %collective-permute-start.19 = (bf16[4,1,48,256]{3,2,1,0:T(8,128)(2,1)S(1)}, bf16[4,1,48,256]{3,2,1,0:T(8,128)(2,1)S(1)}, u32[]{:S(2)}, u32[]{:S(2)}) collective-permute-start(bf16[4,1,48,256]{3,2,1,0:T(8,128)(2,1)S(1)} %constant_dynamic-slice_fusion), channel_id=1, source_target_pairs={{0,4},{1,5},{2,6},{3,7},{4,0},{5,1},{6,2},{7,3},{8,12},{9,13},{10,... | collective-permute-start | bytes 294920 | tf_op jit(solution)/shard_map/ppermute | solution.py:451
  121.2 0.7 stack.23.refs_0_
  121.9 6.0 %collective-permute-done.19 = bf16[4,1,48,256]{3,2,1,0:T(8,128)(2,1)S(1)} collective-permute-done((bf16[4,1,48,256]{3,2,1,0:T(8,128)(2,1)S(1)}, bf16[4,1,48,256]{3,2,1,0:T(8,128)(2,1)S(1)}, u32[]{:S(2)}, u32[]{:S(2)}) %collective-permute-start.19) | collective-permute-done | bytes 98336 | tf_op jit(solution)/shard_map/ppermute | solution.py:451
  127.9 1.6 collective-permute-start.21
  129.5 1.5 collective-permute-start.20
  131.5 1.5 add_convert_fusion.refs_3_
  133.0 1.6 collective-permute-start.15
  134.5 1.5 collective-permute-start.13
  136.0 1.5 collective-permute-done.22
  137.5 0.7 add_convert_fusion.1.refs_4_.refs_5_
  138.2 4.5 %shard_map.99 = (f32[4096,256]{1,0:T(8,128)}, f32[1,4096]{1,0:T(1,128)}) custom-call(s32[5]{0:T(128)} %stack.23.refs_0_, f32[4096,256]{1,0:T(8,128)} %refs_1_.5, f32[1,4096]{1,0:T(1,128)} %bitcast.54, bf16[1024,256]{1,0:T(8,128)(2,1)} %copy-done.2, bf16[192,256]{1,0:T(8,128)(2,1)} %add_convert_fusion.1.refs_4_.refs_5_, ...), custom_call_target="tpu_custom_call" | custom-call | flops 4294967296 | bytes 5242880 | tf_op jit(solution)/shard_map/pallas_call | solution.py:477
  142.7 4.5 %collective-permute-done.15.refs_4_ = bf16[1024,256]{1,0:T(8,128)(2,1)S(1)} collective-permute-done((bf16[1024,256]{1,0:T(8,128)(2,1)S(1)}, bf16[1024,256]{1,0:T(8,128)(2,1)S(1)}, u32[]{:S(2)}, u32[]{:S(2)}) %collective-permute-start.15) | collective-permute-done | bytes 524320 | tf_op jit(solution)/shard_map/ppermute | solution.py:434
  147.3 0.9 collective-permute-start.16
  148.2 1.6 collective-permute-start.14
  149.8 6.9 %shard_map.100 = (f32[4096,256]{1,0:T(8,128)}, f32[1,4096]{1,0:T(1,128)}) custom-call(s32[5]{0:T(128)} %stack.23.refs_0_, f32[4096,256]{1,0:T(8,128)} %refs_1_.5, f32[1,4096]{1,0:T(1,128)} %bitcast.55, bf16[1024,256]{1,0:T(8,128)(2,1)} %copy-done.5, bf16[1024,256]{1,0:T(8,128)(2,1)} %copy-done.4, ...), custom_call_target="tpu_custom_call", output_to_operand_aliasing={{0}: (7, {}), {1}: (8, {})} | custom-call | flops 4294967296 | bytes 5242880 | tf_op jit(solution)/shard_map/pallas_call | solution.py:477
  156.7 1.2 copy-done
  157.9 5.9 %shard_map.95 = (bf16[1024,256]{1,0:T(8,128)(2,1)}, f32[1,1024]{1,0:T(1,128)}) custom-call(bf16[1024,256]{1,0:T(8,128)(2,1)} %refs_0_.5, f32[1,1024]{1,0:T(1,128)} %get-tuple-element.27.refs_1_, s32[1,1024]{1,0:T(1,128)} %bitcast.51, bf16[3072,256]{1,0:T(8,128)(2,1)} %bitcast.37, bf16[1536,384]{1,0:T(8,128)(2,1)} %get-tuple-element.30.refs_4_, ...), custom_call_target="tpu_custom_call" | custom-call | flops 4294967296 | bytes 3145728 | tf_op jit(solution)/shard_map/pallas_call | solution.py:511
  163.7 5.9 %shard_map.96 = (bf16[1024,256]{1,0:T(8,128)(2,1)}, f32[1,1024]{1,0:T(1,128)}) custom-call(bf16[1024,256]{1,0:T(8,128)(2,1)} %refs_0_.5, f32[1,1024]{1,0:T(1,128)} %get-tuple-element.27.refs_1_, s32[1,1024]{1,0:T(1,128)} %bitcast.52, bf16[3072,256]{1,0:T(8,128)(2,1)} %bitcast.38, ...), custom_call_target="tpu_custom_call", output_to_operand_aliasing={{0}: (6, {}), {1}: (7, {})} | custom-call | flops 4294967296 | bytes 3145728 | tf_op jit(solution)/shard_map/pallas_call | solution.py:511
  169.6 0.7 copy-done.13
  170.3 4.6 %shard_map.101 = (f32[4096,256]{1,0:T(8,128)}, f32[1,4096]{1,0:T(1,128)}) custom-call(s32[5]{0:T(128)} %stack.23.refs_0_, f32[4096,256]{1,0:T(8,128)} %refs_1_.5, f32[1,4096]{1,0:T(1,128)} %bitcast.56, bf16[512,256]{1,0:T(8,128)(2,1)} %copy-done.13, bf16[512,256]{1,0:T(8,128)(2,1)} %collective-permute-done.16.refs_4_, ...), custom_call_target="tpu_custom_call", output_to_operand_aliasing={{0}: (7, {}), {1}: (8, {})} | custom-call | flops 4294967296 | bytes 5242880 | tf_op jit(solution)/shard_map/pallas_call | solution.py:477
  (74 shorter events, 4.2 us)
Async XLA Ops:
  0.6 27.2 %collective-permute-start.1 = (bf16[1024,256]{1,0:T(8,128)(2,1)}, bf16[1024,256]{1,0:T(8,128)(2,1)S(1)}, u32[]{:S(2)}, u32[]{:S(2)}) collective-permute-start(bf16[1024,256]{1,0:T(8,128)(2,1)} %refs_0_.5), channel_id=1, source_target_pairs={{0,2},{1,3},{2,4},{3,5},{4,6},{5,7},{6,0},{7,1},{8,10},{9,11},{10,... | collective-permute-start | bytes 1572872 | tf_op jit(solution)/shard_map/ppermute | solution.py:311
  5.8 15.2 %copy-start.6 = (s32[1024]{0:T(1024)}, s32[1024]{0:T(1024)S(1)}, u32[]{:S(2)}) copy-start(s32[1024]{0:T(1024)S(1)} %get-tuple-element.51) | copy-start | bytes 12292
  10.1 14.3 %all-to-all-start = ((bf16[8,48,384]{2,1,0:T(8,128)(2,1)}), bf16[8,48,384]{2,1,0:T(8,128)(2,1)S(1)}, u32[]{:S(2)}, u32[]{:S(2)}) async-start(bf16[8,48,384]{2,1,0:T(8,128)(2,1)} %broadcast_in_dim.9), calls=%async_computation | async-start | bytes 589824 | tf_op jit(solution)/shard_map/all_to_all | solution.py:283
  13.9 36.0 %collective-permute-start = (bf16[1024,256]{1,0:T(8,128)(2,1)}, bf16[1024,256]{1,0:T(8,128)(2,1)S(1)}, u32[]{:S(2)}, u32[]{:S(2)}) collective-permute-start(bf16[1024,256]{1,0:T(8,128)(2,1)} %refs_0_.5), channel_id=1, source_target_pairs={{0,1},{1,0},{2,3},{3,2},{4,5},{5,4},{6,7},{7,6},{8,9},{9,8},{10,11... | collective-permute-start | bytes 1572872 | tf_op jit(solution)/shard_map/ppermute | solution.py:312
  24.3 21.2 %copy-start.3 = (bf16[8,48,384]{2,1,0:T(8,128)(2,1)}, bf16[8,48,384]{2,1,0:T(8,128)(2,1)S(1)}, u32[]{:S(2)}) copy-start(bf16[8,48,384]{2,1,0:T(8,128)(2,1)S(1)} %all-to-all-done) | copy-start | bytes 884740
  24.3 25.7 %collective-permute-start.9 = (bf16[384,384]{1,0:T(8,128)(2,1)S(1)}, bf16[384,384]{1,0:T(8,128)(2,1)S(1)}, u32[]{:S(2)}, u32[]{:S(2)}) collective-permute-start(bf16[384,384]{1,0:T(8,128)(2,1)S(1)} %bitcast.43), channel_id=1, source_target_pairs={{0,24},{8,16},{16,8},{24,0},{1,25},{9,17},{17,9},{25,1},{2,26},{10... | collective-permute-start | bytes 884744 | tf_op jit(solution)/shard_map/ppermute | solution.py:336
  26.8 37.6 %collective-permute-start.8 = (bf16[384,384]{1,0:T(8,128)(2,1)S(1)}, bf16[384,384]{1,0:T(8,128)(2,1)}, u32[]{:S(2)}, u32[]{:S(2)}) collective-permute-start(bf16[384,384]{1,0:T(8,128)(2,1)S(1)} %bitcast.44), channel_id=1, source_target_pairs={{0,16},{8,24},{16,0},{24,8},{1,17},{9,25},{17,1},{25,9},{2,18},{10... | collective-permute-start | bytes 884744 | tf_op jit(solution)/shard_map/ppermute | solution.py:336
  27.3 37.1 %collective-permute-start.7 = (bf16[384,384]{1,0:T(8,128)(2,1)S(1)}, bf16[384,384]{1,0:T(8,128)(2,1)}, u32[]{:S(2)}, u32[]{:S(2)}) collective-permute-start(bf16[384,384]{1,0:T(8,128)(2,1)S(1)} %bitcast.45), channel_id=1, source_target_pairs={{0,8},{8,0},{16,24},{24,16},{1,9},{9,1},{17,25},{25,17},{2,10},{10... | collective-permute-start | bytes 884744 | tf_op jit(solution)/shard_map/ppermute | solution.py:336
  27.8 22.1 %copy-start.7 = (bf16[1024,256]{1,0:T(8,128)(2,1)}, bf16[1024,256]{1,0:T(8,128)(2,1)S(1)}, u32[]{:S(2)}) copy-start(bf16[1024,256]{1,0:T(8,128)(2,1)S(1)} %collective-permute-done.1.refs_2_) | copy-start | bytes 1572868
  27.8 14.2 %collective-permute-start.3 = (bf16[1024,256]{1,0:T(8,128)(2,1)S(1)}, bf16[1024,256]{1,0:T(8,128)(2,1)S(1)}, u32[]{:S(2)}, u32[]{:S(2)}) collective-permute-start(bf16[1024,256]{1,0:T(8,128)(2,1)S(1)} %collective-permute-done.1.refs_2_), channel_id=1, source_target_pairs={{0,2},{1,3},{2,4},{3,5},{4,6},{5,7},{6,0},{7,1},{8,10},{9,11},{10,... | collective-permute-start | bytes 1572872 | tf_op jit(solution)/shard_map/ppermute | solution.py:311
  42.0 8.0 %copy-start.9 = (bf16[1024,256]{1,0:T(8,128)(2,1)}, bf16[1024,256]{1,0:T(8,128)(2,1)S(1)}, u32[]{:S(2)}) copy-start(bf16[1024,256]{1,0:T(8,128)(2,1)S(1)} %collective-permute-done.3.refs_4_) | copy-start | bytes 1572868
  42.1 13.4 %collective-permute-start.5 = (bf16[1024,256]{1,0:T(8,128)(2,1)S(1)}, bf16[1024,256]{1,0:T(8,128)(2,1)S(1)}, u32[]{:S(2)}, u32[]{:S(2)}) collective-permute-start(bf16[1024,256]{1,0:T(8,128)(2,1)S(1)} %collective-permute-done.3.refs_4_), channel_id=1, source_target_pairs={{0,2},{1,3},{2,4},{3,5},{4,6},{5,7},{6,0},{7,1},{8,10},{9,11},{10,... | collective-permute-start | bytes 1572872 | tf_op jit(solution)/shard_map/ppermute | solution.py:311
  50.0 14.4 %copy-start.8 = (bf16[1024,256]{1,0:T(8,128)(2,1)}, bf16[1024,256]{1,0:T(8,128)(2,1)S(1)}, u32[]{:S(2)}) copy-start(bf16[1024,256]{1,0:T(8,128)(2,1)S(1)} %collective-permute-done.refs_1_) | copy-start | bytes 1572868
  50.0 14.4 %collective-permute-start.2 = (bf16[1024,256]{1,0:T(8,128)(2,1)S(1)}, bf16[1024,256]{1,0:T(8,128)(2,1)S(1)}, u32[]{:S(2)}, u32[]{:S(2)}) collective-permute-start(bf16[1024,256]{1,0:T(8,128)(2,1)S(1)} %collective-permute-done.1.refs_2_), channel_id=1, source_target_pairs={{0,1},{1,0},{2,3},{3,2},{4,5},{5,4},{6,7},{7,6},{8,9},{9,8},{10,11... | collective-permute-start | bytes 1572872 | tf_op jit(solution)/shard_map/ppermute | solution.py:312
  50.1 14.3 %copy-start.12 = (bf16[384,384]{1,0:T(8,128)(2,1)}, bf16[384,384]{1,0:T(8,128)(2,1)S(1)}, u32[]{:S(2)}) copy-start(bf16[384,384]{1,0:T(8,128)(2,1)S(1)} %collective-permute-done.9.refs_11_) | copy-start | bytes 884740
  50.1 14.3 %collective-permute-start.4 = (bf16[1024,256]{1,0:T(8,128)(2,1)S(1)}, bf16[1024,256]{1,0:T(8,128)(2,1)}, u32[]{:S(2)}, u32[]{:S(2)}) collective-permute-start(bf16[1024,256]{1,0:T(8,128)(2,1)S(1)} %collective-permute-done.3.refs_4_), channel_id=1, source_target_pairs={{0,1},{1,0},{2,3},{3,2},{4,5},{5,4},{6,7},{7,6},{8,9},{9,8},{10,11... | collective-permute-start | bytes 1572872 | tf_op jit(solution)/shard_map/ppermute | solution.py:312
  55.4 8.9 %copy-start.10 = (bf16[1024,256]{1,0:T(8,128)(2,1)}, bf16[1024,256]{1,0:T(8,128)(2,1)S(1)}, u32[]{:S(2)}) copy-start(bf16[1024,256]{1,0:T(8,128)(2,1)S(1)} %collective-permute-done.5.refs_6_) | copy-start | bytes 1572868
  55.4 9.0 %collective-permute-start.6 = (bf16[1024,256]{1,0:T(8,128)(2,1)S(1)}, bf16[1024,256]{1,0:T(8,128)(2,1)}, u32[]{:S(2)}, u32[]{:S(2)}) collective-permute-start(bf16[1024,256]{1,0:T(8,128)(2,1)S(1)} %collective-permute-done.5.refs_6_), channel_id=1, source_target_pairs={{0,1},{1,0},{2,3},{3,2},{4,5},{5,4},{6,7},{7,6},{8,9},{9,8},{10,11... | collective-permute-start | bytes 1572872 | tf_op jit(solution)/shard_map/ppermute | solution.py:312
  64.4 0.8 copy-start.11
  82.0 13.0 %collective-permute-start.17 = (bf16[4,4,48,256]{3,2,1,0:T(8,128)(2,1)S(1)}, bf16[4,4,48,256]{3,2,1,0:T(8,128)(2,1)}, u32[]{:S(2)}, u32[]{:S(2)}) collective-permute-start(bf16[4,4,48,256]{3,2,1,0:T(8,128)(2,1)S(1)} %dynamic-slice_bitcast_fusion), channel_id=1, source_target_pairs={{0,1},{1,0},{2,3},{3,2},{4,5},{5,4},{6,7},{7,6},{8,9},{9,8},{10,11... | collective-permute-start | bytes 1179656 | tf_op jit(solution)/shard_map/ppermute | solution.py:451
  82.4 74.3 %all-to-all-start.1 = ((bf16[8,384,256]{2,1,0:T(8,128)(2,1)}), bf16[8,384,256]{2,1,0:T(8,128)(2,1)S(1)}, u32[]{:S(2)}, u32[]{:S(2)}) async-start(bf16[8,384,256]{2,1,0:T(8,128)(2,1)} %bitcast.6), calls=%async_computation.1 | async-start | bytes 3145728 | tf_op jit(solution)/shard_map/all_to_all | solution.py:403
  86.1 8.9 %copy-start.1 = (bf16[1536,256]{1,0:T(8,128)(2,1)S(1)}, bf16[1536,256]{1,0:T(8,128)(2,1)}, u32[]{:S(2)}) copy-start(bf16[1536,256]{1,0:T(8,128)(2,1)} %get-tuple-element.42) | copy-start | bytes 2359300
  92.0 39.0 %collective-permute-start.10 = (bf16[1024,256]{1,0:T(8,128)(2,1)}, bf16[1024,256]{1,0:T(8,128)(2,1)S(1)}, u32[]{:S(2)}, u32[]{:S(2)}) collective-permute-start(bf16[1024,256]{1,0:T(8,128)(2,1)} %get-tuple-element.39), channel_id=1, source_target_pairs={{0,8},{8,0},{16,24},{24,16},{1,9},{9,1},{17,25},{25,17},{2,10},{10... | collective-permute-start | bytes 1572872 | tf_op jit(solution)/shard_map/ppermute | solution.py:426
  93.5 38.0 %collective-permute-start.11 = (bf16[1024,256]{1,0:T(8,128)(2,1)}, bf16[1024,256]{1,0:T(8,128)(2,1)}, u32[]{:S(2)}, u32[]{:S(2)}) collective-permute-start(bf16[1024,256]{1,0:T(8,128)(2,1)} %get-tuple-element.40), channel_id=1, source_target_pairs={{0,16},{8,24},{16,0},{24,8},{1,17},{9,25},{17,1},{25,9},{2,18},{10... | collective-permute-start | bytes 1572872 | tf_op jit(solution)/shard_map/ppermute | solution.py:426
  96.1 20.4 %collective-permute-start.18 = (bf16[4,2,48,256]{3,2,1,0:T(8,128)(2,1)S(1)}, bf16[4,2,48,256]{3,2,1,0:T(8,128)(2,1)S(1)}, u32[]{:S(2)}, u32[]{:S(2)}) collective-permute-start(bf16[4,2,48,256]{3,2,1,0:T(8,128)(2,1)S(1)} %dynamic-slice_bitcast_fusion.1), channel_id=1, source_target_pairs={{0,2},{1,3},{2,0},{3,1},{4,6},{5,7},{6,4},{7,5},{8,10},{9,11},{10,... | collective-permute-start | bytes 589832 | tf_op jit(solution)/shard_map/ppermute | solution.py:451
  103.7 27.8 %collective-permute-start.12 = (bf16[1024,256]{1,0:T(8,128)(2,1)}, bf16[1024,256]{1,0:T(8,128)(2,1)S(1)}, u32[]{:S(2)}, u32[]{:S(2)}) collective-permute-start(bf16[1024,256]{1,0:T(8,128)(2,1)} %get-tuple-element.41), channel_id=1, source_target_pairs={{0,24},{8,16},{16,8},{24,0},{1,25},{9,17},{17,9},{25,1},{2,26},{10... | collective-permute-start | bytes 1572872 | tf_op jit(solution)/shard_map/ppermute | solution.py:428
  116.6 11.3 %collective-permute-start.19 = (bf16[4,1,48,256]{3,2,1,0:T(8,128)(2,1)S(1)}, bf16[4,1,48,256]{3,2,1,0:T(8,128)(2,1)S(1)}, u32[]{:S(2)}, u32[]{:S(2)}) collective-permute-start(bf16[4,1,48,256]{3,2,1,0:T(8,128)(2,1)S(1)} %constant_dynamic-slice_fusion), channel_id=1, source_target_pairs={{0,4},{1,5},{2,6},{3,7},{4,0},{5,1},{6,2},{7,3},{8,12},{9,13},{10,... | collective-permute-start | bytes 294920 | tf_op jit(solution)/shard_map/ppermute | solution.py:451
  127.9 8.1 %collective-permute-start.21 = (bf16[192,256]{1,0:T(8,128)(2,1)S(1)}, bf16[192,256]{1,0:T(8,128)(2,1)S(1)}, u32[]{:S(2)}, u32[]{:S(2)}) collective-permute-start(bf16[192,256]{1,0:T(8,128)(2,1)S(1)} %bitcast.47), channel_id=1, source_target_pairs={{0,16},{8,24},{16,0},{24,8},{1,17},{9,25},{17,1},{25,9},{2,18},{10... | collective-permute-start | bytes 294920 | tf_op jit(solution)/shard_map/ppermute | solution.py:455
  129.5 6.5 %collective-permute-start.20 = (bf16[192,256]{1,0:T(8,128)(2,1)S(1)}, bf16[192,256]{1,0:T(8,128)(2,1)S(1)}, u32[]{:S(2)}, u32[]{:S(2)}) collective-permute-start(bf16[192,256]{1,0:T(8,128)(2,1)S(1)} %bitcast.48), channel_id=1, source_target_pairs={{0,8},{8,0},{16,24},{24,16},{1,9},{9,1},{17,25},{25,17},{2,10},{10... | collective-permute-start | bytes 294920 | tf_op jit(solution)/shard_map/ppermute | solution.py:455
  131.0 6.5 %collective-permute-start.22 = (bf16[192,256]{1,0:T(8,128)(2,1)S(1)}, bf16[192,256]{1,0:T(8,128)(2,1)S(1)}, u32[]{:S(2)}, u32[]{:S(2)}) collective-permute-start(bf16[192,256]{1,0:T(8,128)(2,1)S(1)} %bitcast.49), channel_id=1, source_target_pairs={{0,24},{8,16},{16,8},{24,0},{1,25},{9,17},{17,9},{25,1},{2,26},{10... | collective-permute-start | bytes 294920 | tf_op jit(solution)/shard_map/ppermute | solution.py:455
  132.9 5.3 %copy-start.2 = (bf16[1024,256]{1,0:T(8,128)(2,1)}, bf16[1024,256]{1,0:T(8,128)(2,1)S(1)}, u32[]{:S(2)}) copy-start(bf16[1024,256]{1,0:T(8,128)(2,1)S(1)} %add_convert_fusion.refs_3_) | copy-start | bytes 1572868
  133.0 14.3 %collective-permute-start.15 = (bf16[1024,256]{1,0:T(8,128)(2,1)S(1)}, bf16[1024,256]{1,0:T(8,128)(2,1)S(1)}, u32[]{:S(2)}, u32[]{:S(2)}) collective-permute-start(bf16[1024,256]{1,0:T(8,128)(2,1)S(1)} %add_convert_fusion.refs_3_), channel_id=1, source_target_pairs={{0,16},{8,24},{16,0},{24,8},{1,17},{9,25},{17,1},{25,9},{2,18},{10... | collective-permute-start | bytes 1572872 | tf_op jit(solution)/shard_map/ppermute | solution.py:434
  134.5 13.7 %collective-permute-start.13 = (bf16[1024,256]{1,0:T(8,128)(2,1)S(1)}, bf16[1024,256]{1,0:T(8,128)(2,1)S(1)}, u32[]{:S(2)}, u32[]{:S(2)}) collective-permute-start(bf16[1024,256]{1,0:T(8,128)(2,1)S(1)} %add_convert_fusion.refs_3_), channel_id=1, source_target_pairs={{0,8},{8,0},{16,24},{24,16},{1,9},{9,1},{17,25},{25,17},{2,10},{10... | collective-permute-start | bytes 1572872 | tf_op jit(solution)/shard_map/ppermute | solution.py:434
  147.2 2.6 %copy-start.4 = (bf16[1024,256]{1,0:T(8,128)(2,1)}, bf16[1024,256]{1,0:T(8,128)(2,1)S(1)}, u32[]{:S(2)}) copy-start(bf16[1024,256]{1,0:T(8,128)(2,1)S(1)} %collective-permute-done.15.refs_4_) | copy-start | bytes 1572868
  147.3 22.3 %collective-permute-start.16 = (bf16[512,256]{1,0:T(8,128)(2,1)S(1)}, bf16[512,256]{1,0:T(8,128)(2,1)}, u32[]{:S(2)}, u32[]{:S(2)}) collective-permute-start(bf16[512,256]{1,0:T(8,128)(2,1)S(1)} %slice.31), channel_id=1, source_target_pairs={{0,8},{8,0},{16,24},{24,16},{1,9},{9,1},{17,25},{25,17},{2,10},{10... | collective-permute-start | bytes 786440 | tf_op jit(solution)/shard_map/ppermute | solution.py:440
  148.2 1.6 copy-start.5
  148.2 21.4 %collective-permute-start.14 = (bf16[512,256]{1,0:T(8,128)(2,1)S(1)}, bf16[512,256]{1,0:T(8,128)(2,1)S(1)}, u32[]{:S(2)}, u32[]{:S(2)}) collective-permute-start(bf16[512,256]{1,0:T(8,128)(2,1)S(1)} %slice.30), channel_id=1, source_target_pairs={{0,16},{8,24},{16,0},{24,8},{1,17},{9,25},{17,1},{25,9},{2,18},{10... | collective-permute-start | bytes 786440 | tf_op jit(solution)/shard_map/ppermute | solution.py:440
  156.7 1.2 copy-start
  169.6 0.7 copy-start.13
